TPU v7x, 512 devices: a whole 4x4x16 slice. The times are simulated.
512 devices in a mesh: seq: 64 (over z, x), head: 8 (over y, core).
Axes of the slice: x: 4, y: 4, z: 16, core: 2. Of those that a mesh axis runs over, the one named last changes fastest.
Arguments:
- head_inputs: bfloat16 [8192, 8192], P(('seq', 'head')), may hold values from -1.5 to 1.5
- state_proj: bfloat16 [8192, 2048], P(('seq', 'head')), may hold values from -6 to 6
- gate_inputs: bfloat16 [8192, 8192], P(('seq', 'head')), may hold values from -6 to 6
- step_raw: bfloat16 [8192, 128], P(('seq', 'head')), may hold values from -4 to 4
- step_bias: float32 [128], P('head'), may hold values from -2 to 2
- decay_log: float32 [128], P('head'), may hold values from -13 to -2
- skip_gain: float32 [128], P('head'), may hold values from 0.5 to 1.5
- filter_inner: float32 [4, 8192], P(None, 'head'), may hold values from -3 to 3
- filter_state: float32 [4, 2048], P(None, 'head'), may hold values from -3 to 3
- norm_gain: float32 [8192], P('head'), may hold values from 0.5 to 1.5
- prompt_lengths: int32 [7], replicated, may hold values from 1 to 4096, 8192 in all
- request_prompt: int32 [64, 1], P('seq'), may hold values from 0 to 6
Outputs:
- hidden: bfloat16 [8192, 8192], P('seq', 'head')
- final_state: float32 [64, 128, 64, 128], P('seq', 'head')
- edge_inner: bfloat16 [64, 3, 8192], P('seq', None, 'head')
- edge_state: bfloat16 [64, 3, 2048], P('seq', None, 'head')
Inputs may be any that keep to these rules, and one draw needn't show every extreme that they name: `request_prompt`: every prompt is shared by at least one request; request r is served by index r of seq.
All inputs are finite; a program needn't handle non-finite values.
Results may differ from a plain program's by a relative error of at most 0.0065.
Values may be sent and summed in bfloat16 or wider, within the bound.
No kernel may reach another device: no remote copies, remote signals or barrier semaphores. Data moves between devices by JAX's collectives and lax.ppermute only.
A program may use at most 128 MiB of HBM per device.

v0:
```python
import jax
import jax.numpy as jnp
from jax import lax
from jax.sharding import PartitionSpec as P

STATE = 128
SPAN = 256


EPSILON = 1e-05


def from_behind(value, axis, steps):
    count = lax.axis_size(axis)
    first, last = (max(0, -steps), min(count, count - steps))
    return lax.ppermute(value, axis, [(source, source + steps) for source in range(first, last)])


def carried_in(array, axis, combine, identity):
    length, place = (lax.axis_size(axis), lax.axis_index(axis))
    everything = jax.tree.map(lambda part: lax.all_gather(part, axis), array)
    start = jax.tree.map(
        lambda part, zero: jnp.broadcast_to(jnp.asarray(zero, part.dtype), part.shape),
        array,
        identity,
    )

    def step(k, before):
        reached = k < place
        new = combine(before, jax.tree.map(lambda part: part[k], everything))
        return jax.tree.map(lambda a, b: jnp.where(reached, a, b), new, before)

    return lax.fori_loop(0, length, step, start)


def segment_of(position, prompt_starts):
    return jnp.sum((position[:, None] >= prompt_starts[None, :]).astype(jnp.int32), axis=1) - 1


def start_of(position, prompt_starts):
    return jnp.max(
        jnp.where(position[:, None] >= prompt_starts[None, :], prompt_starts[None, :], 0), axis=1
    )


def causal_filter(source_rows, prior_rows, kernel, position, row_start):
    padded = jnp.concatenate([prior_rows, source_rows], axis=0)
    row_count = source_rows.shape[0]
    taps = kernel.shape[0]
    summed = jnp.zeros(source_rows.shape, jnp.float32)
    for offset in range(taps):
        source = position - (taps - 1) + offset
        inside = (source >= row_start).astype(jnp.float32)[:, None]
        summed = (
            summed
            + inside
            * padded[offset : offset + row_count].astype(jnp.float32)
            * kernel[offset][None, :]
        )
    return jax.nn.silu(summed).astype(jnp.bfloat16)


def combine(earlier, later):
    return (earlier[0] * later[0], later[0][..., None, None] * earlier[1] + later[1])


def per_device(
    head_inputs,
    state_proj,
    gate_inputs,
    step_raw,
    step_bias,
    decay_log,
    skip_gain,
    filter_inner,
    filter_state,
    norm_gain,
    prompt_lengths,
    request_prompt,
):
    inner_rows, proj_rows, gate_rows, step_rows = (
        lax.all_to_all(head_inputs, "head", split_axis=1, concat_axis=0, tiled=True),
        lax.all_to_all(state_proj, "head", split_axis=1, concat_axis=0, tiled=True),
        lax.all_to_all(gate_inputs, "head", split_axis=1, concat_axis=0, tiled=True),
        lax.all_to_all(step_raw, "head", split_axis=1, concat_axis=0, tiled=True),
    )
    row_count = inner_rows.shape[0]
    head_count = step_rows.shape[1]
    group_count = proj_rows.shape[1] // (2 * STATE)
    per_group = head_count // group_count
    head_width = inner_rows.shape[1] // head_count
    prompt_count = prompt_lengths.shape[0]
    edge_rows = filter_inner.shape[0] - 1
    block_rows = min(row_count, SPAN)
    block_count = row_count // block_rows
    first_row = lax.axis_index("seq") * row_count
    position = first_row + jnp.arange(row_count, dtype=jnp.int32)
    prompt_ends = jnp.cumsum(prompt_lengths) - 1
    prompt_starts = prompt_ends + 1 - prompt_lengths
    prompt_ids = jnp.arange(prompt_count, dtype=jnp.int32)
    segment = segment_of(position, prompt_starts)
    row_start = start_of(position, prompt_starts)
    prior_segment = segment_of(jnp.reshape(first_row - 1, (1,)), prompt_starts)[0]
    left_inner, left_state = from_behind(
        (inner_rows[row_count - edge_rows :], proj_rows[row_count - edge_rows :]), "seq", 1
    )
    inner_act = causal_filter(inner_rows, left_inner, filter_inner, position, row_start)
    state_act = causal_filter(proj_rows, left_state, filter_state, position, row_start)
    proj_pairs = state_act.reshape(row_count, group_count, 2, STATE)
    write_proj = proj_pairs[:, :, 0]
    read_proj = proj_pairs[:, :, 1]
    step_size = jax.nn.softplus(step_rows.astype(jnp.float32) + step_bias[None, :])
    rates = (step_size * (-jnp.exp(decay_log))[None, :]).reshape(
        block_count, block_rows, head_count
    )
    decay_blocks = jnp.cumsum(rates, axis=1)
    log_decay = decay_blocks.reshape(row_count, head_count)
    head_act = inner_act.reshape(row_count, head_count, head_width)
    segment_blocks = segment.reshape(block_count, block_rows)
    position_blocks = position.reshape(block_count, block_rows)
    step_blocks = step_size.reshape(block_count, block_rows, head_count)
    read_blocks = read_proj.reshape(block_count, block_rows, group_count, STATE)
    write_blocks = write_proj.reshape(block_count, block_rows, group_count, STATE)
    input_blocks = head_act.reshape(block_count, block_rows, head_count, head_width)
    causal_mask = (segment_blocks[:, :, None] == segment_blocks[:, None, :]) & (
        position_blocks[:, :, None] >= position_blocks[:, None, :]
    )
    decay_heads = jnp.swapaxes(decay_blocks, 1, 2)
    log_gap = jnp.where(
        causal_mask[:, None], decay_heads[:, :, :, None] - decay_heads[:, :, None, :], -jnp.inf
    )
    scores = jnp.einsum(
        "ntgs,njgs->ngtj", read_blocks, write_blocks, preferred_element_type=jnp.float32
    )
    scores = jnp.repeat(scores, per_group, axis=1)
    mixing = (scores * jnp.exp(log_gap) * jnp.swapaxes(step_blocks, 1, 2)[:, :, None, :]).astype(
        jnp.bfloat16
    )
    within = jnp.einsum("nhtj,njhp->nthp", mixing, input_blocks, preferred_element_type=jnp.float32)
    segment_before = jnp.concatenate(
        [jnp.reshape(prior_segment, (1,)), segment_blocks[:-1, -1]], axis=0
    )
    segment_last = segment_blocks[:, -1]
    tail_mask = segment_blocks == segment_last[:, None]
    tail_gap = jnp.where(tail_mask[:, :, None], decay_blocks[:, -1:, :] - decay_blocks, -jnp.inf)
    tail_weighted = ((jnp.exp(tail_gap) * step_blocks)[..., None] * input_blocks).astype(
        jnp.bfloat16
    )
    block_state = jnp.einsum(
        "njgkd,njgs->ngkds",
        tail_weighted.reshape(block_count, block_rows, group_count, per_group, head_width),
        write_blocks,
        preferred_element_type=jnp.float32,
    )
    block_decay = (
        jnp.exp(decay_blocks[:, -1]) * (segment_last == segment_before).astype(jnp.float32)[:, None]
    ).reshape(block_count, group_count, per_group)
    running = jnp.zeros((group_count, per_group, head_width, STATE), jnp.float32)
    factor = jnp.ones((group_count, per_group), jnp.float32)
    entering = []
    entering.append(running)
    factors = [factor]
    running = block_decay[0][..., None, None] * running + block_state[0]
    factor = block_decay[0] * factor
    entering = jnp.stack(entering)
    from_start = jnp.stack(factors)
    identity = (jnp.ones_like(factor), jnp.zeros_like(running))
    scanned = carried_in((factor, running), "seq", combine, identity)
    incoming = scanned[1]
    entering = entering + from_start[..., None, None] * incoming[None]
    inflow = (
        jnp.exp(decay_blocks)
        * (segment_blocks == segment_before[:, None]).astype(jnp.float32)[:, :, None]
    )
    across = jnp.einsum(
        "ntgs,ngkds->ntgkd",
        read_blocks.astype(jnp.float32),
        entering,
        precision=lax.Precision.HIGHEST,
    )
    across = across.reshape(block_count, block_rows, head_count, head_width)
    output_sum = (
        within
        + inflow[..., None] * across
        + skip_gain[None, None, :, None] * input_blocks.astype(jnp.float32)
    )
    gated = output_sum.reshape(row_count, head_count * head_width) * jax.nn.silu(
        gate_rows.astype(jnp.float32)
    )
    grouped = gated.reshape(row_count, group_count, per_group * head_width)
    inverse_rms = lax.rsqrt(jnp.mean(grouped * grouped, axis=2, keepdims=True) + EPSILON)
    hidden = (
        (grouped * inverse_rms).reshape(row_count, head_count * head_width) * norm_gain[None, :]
    ).astype(jnp.bfloat16)
    ends_here = (prompt_ends >= first_row) & (prompt_ends < first_row + row_count)
    end_block = jnp.clip((prompt_ends - first_row) // block_rows, 0, block_count - 1)
    block_ids = jnp.arange(block_count, dtype=jnp.int32)
    block_onehot = ((block_ids[None, :] == end_block[:, None]) & ends_here[:, None]).astype(
        jnp.float32
    )
    state_at_end = jnp.einsum(
        "pn,ngkds->pgkds", block_onehot, entering, precision=lax.Precision.HIGHEST
    )
    segment_before_end = jnp.sum(block_onehot.astype(jnp.int32) * segment_before[None, :], axis=1)
    end_onehot = (position[None, :] == prompt_ends[:, None]).astype(jnp.float32)
    end_decay = jnp.dot(end_onehot, log_decay, precision=lax.Precision.HIGHEST)
    same_block = position[None, :] // block_rows == prompt_ends[:, None] // block_rows
    member = (
        (segment[None, :] == prompt_ids[:, None])
        & (position[None, :] <= prompt_ends[:, None])
        & same_block
        & ends_here[:, None]
    )
    decay_gap = jnp.where(member[:, :, None], end_decay[:, None, :] - log_decay[None], -jnp.inf)
    weighted = ((jnp.exp(decay_gap) * step_size[None])[..., None] * head_act[None]).astype(
        jnp.bfloat16
    )
    own_part = jnp.einsum(
        "ptgkd,tgs->pgkds",
        weighted.reshape(prompt_count, row_count, group_count, per_group, head_width),
        write_proj,
        preferred_element_type=jnp.float32,
    )
    carried = (
        jnp.exp(end_decay)
        * (ends_here & (prompt_ids == segment_before_end)).astype(jnp.float32)[:, None]
    )
    finals = (
        own_part
        + carried.reshape(prompt_count, group_count, per_group)[..., None, None] * state_at_end
    )
    offsets = (
        prompt_ends[:, None] - (edge_rows - 1) + jnp.arange(edge_rows, dtype=jnp.int32)[None, :]
    )
    index_rows = jnp.clip(offsets - (first_row - edge_rows), 0, row_count + edge_rows - 1)
    inside = ((offsets >= prompt_starts[:, None]) & ends_here[:, None])[..., None]
    padded_inner = jnp.concatenate([left_inner, inner_rows], axis=0)
    padded_state = jnp.concatenate([left_state, proj_rows], axis=0)
    edge_inner = jnp.where(inside, padded_inner[index_rows], 0).astype(jnp.float32)
    edge_state = jnp.where(inside, padded_state[index_rows], 0).astype(jnp.float32)
    finals, edge_inner, edge_state = lax.psum((finals, edge_inner, edge_state), "seq")
    choose = (request_prompt == prompt_ids[None, :]).astype(jnp.float32)
    final_state = jnp.dot(choose, finals.reshape(prompt_count, -1), precision=lax.Precision.HIGHEST)
    final_state = final_state.reshape(-1, head_count, head_width, STATE)
    chosen_inner = jnp.dot(
        choose, edge_inner.reshape(prompt_count, -1), precision=lax.Precision.HIGHEST
    )
    chosen_inner = chosen_inner.reshape(-1, edge_rows, inner_rows.shape[1]).astype(jnp.bfloat16)
    chosen_state = jnp.dot(
        choose, edge_state.reshape(prompt_count, -1), precision=lax.Precision.HIGHEST
    )
    chosen_state = chosen_state.reshape(-1, edge_rows, proj_rows.shape[1]).astype(jnp.bfloat16)
    return (hidden, final_state, chosen_inner, chosen_state)


def solution(mesh):
    return jax.shard_map(
        per_device,
        mesh=mesh,
        in_specs=(
            P(("seq", "head"), None),
            P(("seq", "head"), None),
            P(("seq", "head"), None),
            P(("seq", "head"), None),
            P("head"),
            P("head"),
            P("head"),
            P(None, "head"),
            P(None, "head"),
            P("head"),
            P(),
            P("seq", None),
        ),
        out_specs=(
            P("seq", "head"),
            P("seq", "head", None, None),
            P("seq", None, "head"),
            P("seq", None, "head"),
        ),
        check_vma=False,
    )
```

profile of v0, /device:TPU:8, one launch (start us, length us, event | category | flops | bytes accessed | tf_op | source)
XLA Modules:
  0.0 744.1 jit_solution(5373502963145911985)
XLA Ops:
  8.7 9.0 %all-to-all-start.2 = ((bf16[8,2,128]{2,1,0:T(2,128)(2,1)}), bf16[8,2,128]{2,1,0:T(2,128)(2,1)S(1)}, u32[]{:S(2)}, u32[]{:S(2)}) async-start(bf16[8,2,128]{2,1,0:T(2,128)(2,1)} %reshape.1105), calls=%async_computation.2 | async-start | bytes 8192 | tf_op jit(solution)/shard_map/all_to_all | solution.py:85
  18.5 1.3 bitcast_add_fusion.2
  24.9 1.7 copy.187
  26.5 1.5 copy.188
  28.0 4.8 all-to-all-start.1
  34.2 2.8 all-to-all-done.1
  37.0 4.8 all-to-all-start
  42.5 1.3 collective-permute-start.1
  44.1 3.8 all-to-all-done
  47.9 1.3 collective-permute-start
  52.7 80.2 %all_gather.10 = f32[64,1,16]{2,1,0:T(1,128)S(1)} all-gather(f32[1,1,16]{2,1,0:T(1,128)S(1)} %get-tuple-element.173), channel_id=1, replica_groups=mesh['seq'=64,'head'=8] {'seq'}, dimensions={0}, use_global_device_ids=true | all-gather | bytes 4160 | tf_op jit(solution)/shard_map/all_gather | solution.py:21
  135.6 2.5 fusion.29
  138.1 210.4 %all-gather.3.cloned.1.call-done = f32[1024,64,128]{2,1,0:T(8,128)} async-done(((f32[16,64,128]{2,1,0:T(8,128)}), f32[1024,64,128]{2,1,0:T(8,128)}) %all-gather.3.cloned.1.call-update) | async-done | bytes 33554448 | tf_op jit(solution)/shard_map/all_gather | solution.py:21
  348.5 77.8 %while.14 = (s32[]{:T(128)}, f32[1,16,64,128]{3,2,1,0:T(8,128)S(1)}, s32[]{:T(128)}, f32[64,1,16]{2,1,0:T(1,128)S(1)}, f32[64,1,16,64,128]{4,3,2,1,0:T(8,128)}, /*index=5*/s32[]{:T(128)}, s32[]{:T(128)}) while((s32[]{:T(128)}, f32[1,16,64,128]{3,2,1,0:T(8,128)S(1)}, s32[]{:T(128)}, f32[64,1,16]{2,1,0:T(1,128)S(1)}, ...), condition=%wide.region_6.7_spmd.clone, body=%wide.region_5.6_spmd.clone.sunk | while | flops 524292 | bytes 1573169 | solution.py:33
  349.8 1.2 fusion.74
  352.2 1.2 fusion.74
  353.4 1.2 fusion.74
  354.6 1.2 fusion.74
  426.3 4.3 bitcast_add_fusion.1
  430.6 5.1 reshape.1061
  435.7 4.7 copy.170
  442.1 4.8 all-to-all-start.3
  448.5 276.3 %psum.23 = f32[3,256,7]{1,2,0:T(8,128)S(1)} all-reduce(f32[3,256,7]{1,2,0:T(8,128)S(1)} %bitcast.268), channel_id=1, replica_groups=mesh['seq'=64,'head'=8] {'seq'}, use_global_device_ids=true, to_apply=%region_10.11 | all-reduce | flops 5376 | bytes 43008 | tf_op jit(solution)/shard_map/psum | solution.py:241
  730.4 6.8 fusion.1
  (212 shorter events, 93.4 us)
Async XLA Ops:
  8.7 19.3 %all-to-all-start.2 = ((bf16[8,2,128]{2,1,0:T(2,128)(2,1)}), bf16[8,2,128]{2,1,0:T(2,128)(2,1)S(1)}, u32[]{:S(2)}, u32[]{:S(2)}) async-start(bf16[8,2,128]{2,1,0:T(2,128)(2,1)} %reshape.1105), calls=%async_computation.2 | async-start | bytes 8192 | tf_op jit(solution)/shard_map/all_to_all | solution.py:85
  28.0 9.0 %all-to-all-start.1 = ((bf16[16,8,256]{2,0,1:T(8,128)(2,1)}), bf16[16,8,256]{2,0,1:T(8,128)(2,1)S(1)}, u32[]{:S(2)}, u32[]{:S(2)}) async-start(bf16[16,8,256]{2,0,1:T(8,128)(2,1)} %bitcast.227), calls=%async_computation.1 | async-start | bytes 131072 | tf_op jit(solution)/shard_map/all_to_all | solution.py:83
  37.0 10.9 %all-to-all-start = ((bf16[16,8,1024]{2,0,1:T(8,128)(2,1)}), bf16[16,8,1024]{2,0,1:T(8,128)(2,1)S(1)}, u32[]{:S(2)}, u32[]{:S(2)}) async-start(bf16[16,8,1024]{2,0,1:T(8,128)(2,1)} %bitcast.226), calls=%async_computation | async-start | bytes 524288 | tf_op jit(solution)/shard_map/all_to_all | solution.py:82
  41.8 306.8 %all-gather.3.cloned.1.call-start = ((), (), s32[]{:S(2)}) async-start(), calls=%async_computation.4 | async-start | bytes 34078720 | tf_op jit(solution)/shard_map/all_gather | solution.py:21
  42.5 6.6 collective-permute-start.1
  47.9 2.6 collective-permute-start
  52.3 676.5 %all-reduce.3.cloned.1.call-start = ((), (), s32[]{:S(2)}) async-start(), calls=%async_computation.5 | async-start | bytes 7536640 | tf_op jit(solution)/shard_map/psum | solution.py:241
  440.4 0.9 copy-start
  441.3 285.7 %copy-start.2 = (f32[16]{0:T(128)S(1)}, f32[16]{0:T(128)}, u32[]{:S(2)}) copy-start(f32[16]{0:T(128)} %param.20) | copy-start | bytes 196
  442.1 283.7 %all-to-all-start.3 = ((bf16[16,8,1024]{2,0,1:T(8,128)(2,1)}), bf16[16,8,1024]{2,0,1:T(8,128)(2,1)S(1)}, u32[]{:S(2)}, u32[]{:S(2)}) async-start(bf16[16,8,1024]{2,0,1:T(8,128)(2,1)} %bitcast.225), calls=%async_computation.3 | async-start | bytes 524288 | tf_op jit(solution)/shard_map/all_to_all | solution.py:84
  726.6 1.2 copy-start.1
Sparse Core Ops, SparseCore 0:
  52.4 296.0 all-gather.2
  440.5 284.6 all-reduce.2
where the time goes:
time: 748 us; the launch traced here: 744 us
  blocking collectives  357 us (48%)
  waiting for transfers between devices  218 us (29%)
  other arithmetic  87.7 us (12%)
  starting transfers between devices  26.1 us (3%)
  local copies, waits for them, and re-layouts  24.2 us (3%)
  between operations  16.3 us (2%)
  matrix products  12.9 us (2%)
    psum x1, blocking collectives, per_device(): lax.psum((finals, edge_inner, edge_state), 'seq')  276 us
    all_gather x1, waiting for transfers between devices, carried_in(): everything = jax.tree.map(lambda part: lax.all_gather(part, axis), array)  210 us
    all_gather x1, blocking collectives, carried_in(): everything = jax.tree.map(lambda part: lax.all_gather(part, axis), array)  80.2 us
    select_n x64, other arithmetic, step(): return jax.tree.map(lambda a, b: jnp.where(reached, a, b), new, before)  75.1 us
  transfers between devices with their start and end apart: 8, of which 4 were waited for; matrix products, arithmetic and copies ran while one was open for 3% of the time, Pallas kernels for 0%

commit v1 on v0

v1 whole, which is shorter than its diff:
```python
import functools

import jax
import jax.numpy as jnp
from jax import lax
from jax.experimental import pallas as pl
from jax.experimental.pallas import tpu as pltpu
from jax.sharding import PartitionSpec as P

STATE = 128
EPSILON = 1e-05
PROMPTS = 7
ROWS = 128
WIDTH = 1024
WIDE = 1280
HEAD = 64
BIG = 1 << 30
F32 = jnp.float32
BF16 = jnp.bfloat16

MESSAGE = 40


def dot(a, b, dims, precision=None):
    return lax.dot_general(a, b, (dims, ((), ())), precision=precision, preferred_element_type=F32)


def bounds(length_ref):
    starts, ends = [], []
    total = jnp.int32(0)
    for p in range(PROMPTS):
        starts.append(total)
        total = total + length_ref[p]
        ends.append(total - 1)
    return starts, ends


def segment_at(position, starts):
    found = jnp.zeros_like(position) - 1
    for start in starts:
        found = found + (position >= start).astype(jnp.int32)
    return found


def spread(weights, tile, lane):
    left = jnp.broadcast_to(weights[:, 2 * tile : 2 * tile + 1], lane.shape)
    right = jnp.broadcast_to(weights[:, 2 * tile + 1 : 2 * tile + 2], lane.shape)
    return jnp.where(lane < HEAD, left, right)


def parts(value):
    first = value.astype(BF16).astype(F32)
    rest = value - first
    second = rest.astype(BF16).astype(F32)
    return first, second, rest - second


def pack_kernel(inner_ref, proj_ref, step_ref, out_ref):
    for k in range(out_ref.shape[0]):
        out_ref[k, :, 0:WIDTH] = inner_ref[:, k * WIDTH : (k + 1) * WIDTH]
        out_ref[k, :, WIDTH:WIDE] = proj_ref[:, k * 256 : (k + 1) * 256]
        out_ref[k, :, WIDE : WIDE + 128] = step_ref[...]


def front_kernel(
    place_ref, length_ref, request_ref, rows_ref, halo_ref, taps_ref, head_ref,
    message_ref, act_ref, decay_ref, step_ref, padded,
):
    first = place_ref[0] * ROWS
    starts, ends = bounds(length_ref)
    lane = lax.broadcasted_iota(jnp.int32, (ROWS, 128), 1)
    position = lax.broadcasted_iota(jnp.int32, (ROWS, 128), 0) + first
    segment = segment_at(position, starts)
    row_start = jnp.zeros_like(position)
    for start in starts:
        row_start = jnp.where(position >= start, start, row_start)
    before = segment_at(first - 1, starts)
    last = segment_at(first + ROWS - 1, starts)
    end, end_prompt, end_start = jnp.int32(BIG), jnp.int32(-2), jnp.int32(0)
    for p in reversed(range(PROMPTS)):
        here = (ends[p] >= first) & (ends[p] < first + ROWS)
        end = jnp.where(here, ends[p], end)
        end_prompt = jnp.where(here, p, end_prompt)
        end_start = jnp.where(here, starts[p], end_start)
    some_end = end < BIG

    padded[0:8, :] = halo_ref[...].astype(F32)
    padded[8:, :] = rows_ref[:, 0:WIDE].astype(F32)
    inside = [(position - 3 + k) >= row_start for k in range(4)]
    for tile in range(WIDE // 128):
        cols = slice(tile * 128, (tile + 1) * 128)
        total = jnp.zeros((ROWS, 128), F32)
        for k in range(4):
            total = total + jnp.where(inside[k], padded[5 + k : 5 + k + ROWS, cols], 0.0) * taps_ref[k : k + 1, cols]
        act_ref[:, cols] = (total * jax.nn.sigmoid(total)).astype(BF16)

    raw = rows_ref[:, WIDE : WIDE + 128].astype(F32)
    raw = pltpu.roll(raw, place_ref[2], 1)
    step = jax.nn.softplus(raw + head_ref[0:1, :])
    rate = step * -jnp.exp(head_ref[1:2, :])
    lower = (
        lax.broadcasted_iota(jnp.int32, (ROWS, ROWS), 0) >= lax.broadcasted_iota(jnp.int32, (ROWS, ROWS), 1)
    ).astype(F32)
    decay = dot(lower, rate, ((1,), (0,)), lax.Precision.HIGHEST)
    decay_ref[...] = decay
    step_ref[...] = step

    last_decay = decay[ROWS - 1 : ROWS, :]
    tail = jnp.where(segment == last, jnp.exp(jnp.minimum(last_decay - decay, 0.0)), 0.0) * step
    end_decay = jnp.sum(jnp.where(position == end, decay, 0.0), axis=0, keepdims=True)
    member = (segment == end_prompt) & (position <= end)
    own = jnp.where(member, jnp.exp(jnp.minimum(end_decay - decay, 0.0)), 0.0) * step
    write = act_ref[:, WIDTH : WIDTH + STATE]
    for tile in range(WIDTH // 128):
        x = act_ref[:, tile * 128 : (tile + 1) * 128].astype(F32)
        for at, weights in ((0, tail), (16, own)):
            weighted = (spread(weights, tile, lane) * x).astype(BF16)
            block = dot(weighted, write, ((0,), (0,)))
            message_ref[tile * 8 : (tile + 1) * 8, at : at + 16, :] = block.astype(BF16).reshape(8, 16, 128)

    keep = jnp.where(last == before, jnp.exp(last_decay), 0.0)
    carried = jnp.where(some_end & (end_prompt == before), jnp.exp(end_decay), 0.0)
    index = lax.broadcasted_iota(jnp.int32, (8, 128), 0)
    small = jnp.where(index == 7, request_ref[0, 0].astype(F32), jnp.zeros((8, 128), F32))
    for at, piece in enumerate(parts(keep) + parts(carried)):
        small = jnp.where(index == at + 1, piece, small)
    for k in range(3):
        local = jnp.where(some_end, end - first, 0) - 2 + k
        valid = some_end & (end - 2 + k >= end_start)
        row = jnp.where(valid, padded[pl.ds(8 + local, 1), :], 0.0)
        for c in range(WIDE // 128):
            piece = row[:, c * 128 : (c + 1) * 128]
            message_ref[k * 10 + c, 32:40, :] = jnp.where(index == 0, piece, small).astype(BF16)
    rest = small.astype(BF16)
    for k in range(30, 64):
        message_ref[k, 32:40, :] = rest


def scan_kernel(place_ref, length_ref, got_ref, extra_ref, out_ref, states, finals):
    starts, ends = bounds(length_ref)
    head = place_ref[0] // 4
    pick = (lax.broadcasted_iota(jnp.int32, (128, 128), 0) == head).astype(BF16)
    small = dot(got_ref[:, 32:40, :].reshape(64 * 8, 128), pick, ((1,), (0,)))
    state = jnp.zeros((16, 128), F32)
    for j in range(64):
        states[j, 0:16, :] = state
        keep = small[8 * j + 1 : 8 * j + 2] + small[8 * j + 2 : 8 * j + 3] + small[8 * j + 3 : 8 * j + 4]
        states[j, 16:17, :] = small[8 * j + 4 : 8 * j + 5] + small[8 * j + 5 : 8 * j + 6] + small[8 * j + 6 : 8 * j + 7]
        out_ref[j, 0:16, :] = state.astype(BF16)
        state = keep * state + got_ref[j, 0:16, :].astype(F32)
    for p in range(PROMPTS):
        block = ends[p] // ROWS
        one = got_ref[block, 16:40, :].astype(F32)
        value = one[0:16] + states[block, 16:17, :] * states[block, 0:16, :]
        value = jnp.concatenate([value, one[16:24]], axis=0)
        if p:
            value = jnp.where(ends[p - 1] // ROWS == block, extra_ref[p], value)
        finals[p] = value
    for r in range(64):
        request = got_ref[r, 39:40, :].astype(F32)
        value = finals[0]
        for p in range(1, PROMPTS):
            value = jnp.where(request == float(p), finals[p], value)
        out_ref[r, 16:40, :] = value.astype(BF16)


def within_kernel(place_ref, length_ref, act_ref, decay_ref, step_ref, gate_ref, head_ref, own_ref, in_ref):
    first = place_ref[0] * ROWS
    starts, _ = bounds(length_ref)
    before = segment_at(first - 1, starts)
    lane = lax.broadcasted_iota(jnp.int32, (ROWS, 128), 1)
    sub = lax.broadcasted_iota(jnp.int32, (ROWS, 128), 0)
    segment = segment_at(sub + first, starts)
    segment_j = segment_at(lane + first, starts)
    causal = (segment == segment_j) & (sub >= lane)
    write = act_ref[:, WIDTH : WIDTH + STATE]
    read = act_ref[:, WIDTH + STATE : WIDE]
    scores = dot(read, write, ((1,), (1,)))
    decay = decay_ref[...]
    decay_t = decay.T
    step_t = step_ref[...].T
    inflow = jnp.where(segment == before, jnp.exp(decay), 0.0)
    for tile in range(WIDTH // 128):
        cols = slice(tile * 128, (tile + 1) * 128)
        x = act_ref[:, cols]
        mixing = []
        for head in (2 * tile, 2 * tile + 1):
            gap = decay[:, head : head + 1] - decay_t[head : head + 1, :]
            weight = jnp.exp(jnp.where(causal, gap, -jnp.inf))
            mixing.append((scores * weight * step_t[head : head + 1, :]).astype(BF16))
        none = jnp.zeros_like(x)
        both = jnp.concatenate([jnp.where(lane < HEAD, x, none), jnp.where(lane < HEAD, none, x)], axis=0)
        within = dot(jnp.concatenate(mixing, axis=1), both, ((1,), (0,)))
        within = within + head_ref[2 + tile : 3 + tile, :] * x.astype(F32)
        gate = gate_ref[:, cols].astype(F32)
        gate = gate * jax.nn.sigmoid(gate)
        own_ref[:, cols] = within * gate
        in_ref[:, cols] = spread(inflow, tile, lane) * gate


def back_kernel(act_ref, own_ref, in_ref, got_ref, gain_ref, hidden_ref, final_ref, inner_ref, proj_ref, gated):
    read = act_ref[:, WIDTH + STATE : WIDE]
    total = jnp.zeros((ROWS, 128), F32)
    for tile in range(WIDTH // 128):
        cols = slice(tile * 128, (tile + 1) * 128)
        state = got_ref[tile * 8 : (tile + 1) * 8, 0:16, :].reshape(128, 128)
        across = dot(read, state, ((1,), (1,)))
        value = own_ref[:, cols] + in_ref[:, cols] * across
        gated[:, cols] = value
        total = total + value * value
    mean = jnp.sum(total, axis=1, keepdims=True) * (1.0 / WIDTH)
    inverse = lax.rsqrt(mean + EPSILON)
    for tile in range(WIDTH // 128):
        cols = slice(tile * 128, (tile + 1) * 128)
        hidden_ref[:, cols] = ((gated[:, cols] * inverse) * gain_ref[:, cols]).astype(BF16)
        final_ref[tile * 128 : (tile + 1) * 128, :] = (
            got_ref[tile * 8 : (tile + 1) * 8, 16:32, :].reshape(128, 128).astype(F32)
        )
    for k in range(3):
        for c in range(8):
            inner_ref[0, k : k + 1, c * 128 : (c + 1) * 128] = got_ref[k * 10 + c, 32:33, :]
        for c in range(2):
            proj_ref[0, k : k + 1, c * 128 : (c + 1) * 128] = got_ref[k * 10 + 8 + c, 32:33, :]


def call(kernel, ins, outs, scratch=(), scalars=0):
    smem = pl.BlockSpec(memory_space=pltpu.SMEM)
    vmem = pl.BlockSpec(memory_space=pltpu.VMEM)
    return pl.pallas_call(
        kernel,
        out_shape=outs,
        in_specs=[smem] * scalars + [vmem] * (len(ins) - scalars),
        out_specs=jax.tree.map(lambda _: vmem, outs),
        scratch_shapes=list(scratch),
    )(*ins)


def later_ends(place, prompt_lengths, rows, halo, act, decay, step):
    ends = jnp.cumsum(prompt_lengths) - 1
    starts = ends + 1 - prompt_lengths
    ids = jnp.arange(PROMPTS, dtype=jnp.int32)
    block = ends // ROWS
    rank = jnp.sum((block[None, :] == block[:, None]) & (ids[None, :] < ids[:, None]), axis=1)
    position = place * ROWS + jnp.arange(ROWS, dtype=jnp.int32)

    def step_of(carry):
        k, extra = carry
        mine = (block == place) & (rank == k)
        some = jnp.any(mine)
        end = jnp.sum(jnp.where(mine, ends, 0))
        start = jnp.sum(jnp.where(mine, starts, 0))
        member = some & (position >= start) & (position <= end)
        end_decay = jnp.sum(jnp.where((position == end)[:, None], decay, 0.0), axis=0, keepdims=True)
        weights = jnp.where(member[:, None], jnp.exp(jnp.minimum(end_decay - decay, 0.0)), 0.0) * step
        weights = weights[:, : WIDTH // HEAD]
        x = act[:, :WIDTH].reshape(ROWS, -1, HEAD).astype(F32)
        weighted = (weights[:, :, None] * x).reshape(ROWS, WIDTH).astype(BF16)
        own = dot(weighted, act[:, WIDTH : WIDTH + STATE], ((0,), (0,))).astype(BF16)
        padded = jnp.concatenate([halo, rows[:, :WIDE]], axis=0)
        wanted = end - 2 + jnp.arange(3, dtype=jnp.int32)
        onehot = (jnp.arange(ROWS + 8)[None, :] + (place * ROWS - 8) == wanted[:, None]) & some
        onehot = onehot & (wanted >= start)[:, None]
        edge = dot(onehot.astype(BF16), padded, ((1,), (0,))).astype(BF16)
        edge = jnp.pad(edge.reshape(30, 1, 128), ((0, 34), (0, 7), (0, 0)))
        sent = jnp.concatenate([own.reshape(64, 16, 128), edge], axis=1)
        got = lax.all_to_all(sent, "seq", 0, 0)
        taken = got[block].astype(F32)
        return k + 1, jnp.where((rank == k)[:, None, None], taken, extra)

    most = jnp.max(rank)
    return lax.while_loop(
        lambda carry: carry[0] <= most,
        step_of,
        (jnp.ones_like(most), jnp.zeros((PROMPTS, 24, 128), F32)),
    )[1]


def per_device(
    head_inputs,
    state_proj,
    gate_inputs,
    step_raw,
    step_bias,
    decay_log,
    skip_gain,
    filter_inner,
    filter_state,
    norm_gain,
    prompt_lengths,
    request_prompt,
):
    shape = jax.ShapeDtypeStruct
    seq = lax.axis_size("seq")
    place = lax.axis_index("seq").astype(jnp.int32)
    column = lax.axis_index("head").astype(jnp.int32)
    heads = step_bias.shape[0]
    places = jnp.stack([place, column, (128 - heads * column) % 128])
    heads_in = jnp.concatenate(
        [
            jnp.pad(step_bias, (0, 128 - heads))[None],
            jnp.pad(decay_log, (0, 128 - heads))[None],
            jnp.repeat(skip_gain, HEAD).reshape(8, 128),
            jnp.zeros((6, 128), F32),
        ],
        axis=0,
    )
    taps = jnp.concatenate([filter_inner, filter_state], axis=1)
    packed = call(
        pack_kernel,
        (head_inputs, state_proj, step_raw),
        shape((8, 16, WIDE + 128), BF16),
    )
    rows = lax.all_to_all(packed, "head", 0, 0).reshape(ROWS, WIDE + 128)
    halo = lax.ppermute(
        rows[ROWS - 8 :, :WIDE], "seq", [(source, source + 1) for source in range(seq - 1)]
    )
    message, act, decay, step = call(
        front_kernel,
        (places, prompt_lengths, request_prompt, rows, halo, taps, heads_in),
        (
            shape((64, MESSAGE, 128), BF16),
            shape((ROWS, WIDE), BF16),
            shape((ROWS, 128), F32),
            shape((ROWS, 128), F32),
        ),
        (pltpu.VMEM((ROWS + 8, WIDE), F32),),
        scalars=3,
    )
    got = lax.all_to_all(message, "seq", 0, 0)
    gate = lax.all_to_all(gate_inputs, "head", split_axis=1, concat_axis=0, tiled=True)
    own, inflow = call(
        within_kernel,
        (places, prompt_lengths, act, decay, step, gate, heads_in),
        (shape((ROWS, WIDTH), F32), shape((ROWS, WIDTH), F32)),
        scalars=2,
    )
    extra = later_ends(place, prompt_lengths, rows, halo, act, decay, step)
    answer = call(
        scan_kernel,
        (places, prompt_lengths, got, extra),
        shape((64, MESSAGE, 128), BF16),
        (pltpu.VMEM((64, 24, 128), F32), pltpu.VMEM((PROMPTS, 24, 128), F32)),
        scalars=2,
    )
    back = lax.all_to_all(answer, "seq", 0, 0)
    hidden, final, edge_inner, edge_state = call(
        back_kernel,
        (act, own, inflow, back, norm_gain[None]),
        (
            shape((ROWS, WIDTH), BF16),
            shape((WIDTH, STATE), F32),
            shape((1, 3, WIDTH), BF16),
            shape((1, 3, 256), BF16),
        ),
        (pltpu.VMEM((ROWS, WIDTH), F32),),
    )
    return hidden, final.reshape(1, heads, HEAD, STATE), edge_inner, edge_state


def solution(mesh):
    return jax.shard_map(
        per_device,
        mesh=mesh,
        in_specs=(
            P(("seq", "head"), None),
            P(("seq", "head"), None),
            P(("seq", "head"), None),
            P(("seq", "head"), None),
            P("head"),
            P("head"),
            P("head"),
            P(None, "head"),
            P(None, "head"),
            P("head"),
            P(),
            P("seq", None),
        ),
        out_specs=(
            P("seq", "head"),
            P("seq", "head", None, None),
            P("seq", None, "head"),
            P("seq", None, "head"),
        ),
        check_vma=False,
    )
```

time: 748 us -> 148 us (0.20)
  the two profiles are of different devices: /device:TPU:8 before, /device:TPU:2 now
where the time goes in v1:
time: 148 us
  waiting for transfers between devices  86.1 us (58%)
  starting transfers between devices  34.9 us (24%)
  Pallas kernels  13.6 us (9%)
  local copies, waits for them, and re-layouts  7.98 us (5%)
  other arithmetic  2.95 us (2%)
    all_to_all x1, waiting for transfers between devices, per_device(): got = lax.all_to_all(message, 'seq', 0, 0)  35.9 us
    all_to_all x1, waiting for transfers between devices, per_device(): back = lax.all_to_all(answer, 'seq', 0, 0)  35.1 us
    all_to_all x1, starting transfers between devices, per_device(): got = lax.all_to_all(message, 'seq', 0, 0)  17.5 us
    pallas_call x5, Pallas kernels, call(): pl.pallas_call(kernel, out_shape=outs, in_specs=[smem] * scalars + [vmem]...  13.6 us
    all_to_all x1, waiting for transfers between devices, per_device(): rows = lax.all_to_all(packed, 'head', 0, 0).reshape(ROWS, WIDE + 128)  7.76 us
    unnamed x33, local copies, waits for them, and re-layouts  6.92 us
    all_to_all x1, starting transfers between devices, per_device(): back = lax.all_to_all(answer, 'seq', 0, 0)  5.95 us
    all_to_all x1, waiting for transfers between devices, per_device(): lax.all_to_all(gate_inputs, 'head', split_axis=1, concat_axis=0, tiled=True)  4.78 us
  transfers between devices with their start and end apart: 5, of which 5 were waited for; matrix products, arithmetic and copies ran while one was open for 2% of the time, Pallas kernels for 4%

profile of v1, /device:TPU:2, one launch (start us, length us, event | category | flops | bytes accessed | tf_op | source)
XLA Modules:
  0.0 147.6 jit_solution(5340959385642637446)
XLA Ops:
  0.7 0.6 copy-done.12
  1.5 0.7 copy-done.10
  3.2 1.8 %shard_map.147 = bf16[8,16,1408]{2,1,0:T(8,128)(2,1)} custom-call(bf16[16,8192]{1,0:T(8,128)(2,1)} %inner_ref.1, bf16[16,2048]{1,0:T(8,128)(2,1)} %proj_ref.1, bf16[16,128]{1,0:T(8,128)(2,1)} %step_ref.1), custom_call_target="tpu_custom_call" | custom-call | tf_op jit(solution)/shard_map/pallas_call | solution.py:229
  4.9 0.7 maximum_maximum_fusion.head_ref
  5.6 4.6 %all-to-all-start.1 = ((bf16[8,16,1408]{2,1,0:T(8,128)(2,1)}), bf16[8,16,1408]{2,1,0:T(8,128)(2,1)S(1)}, u32[]{:S(2)}, u32[]{:S(2)}) async-start(bf16[8,16,1408]{2,1,0:T(8,128)(2,1)} %shard_map.147), calls=%async_computation.1 | async-start | bytes 720896 | tf_op jit(solution)/shard_map/all_to_all | solution.py:313
  11.0 7.8 %all-to-all-done.1 = bf16[8,16,1408]{2,1,0:T(8,128)(2,1)S(1)} async-done(((bf16[8,16,1408]{2,1,0:T(8,128)(2,1)}), bf16[8,16,1408]{2,1,0:T(8,128)(2,1)S(1)}, u32[]{:S(2)}, u32[]{:S(2)}) %all-to-all-start.1) | async-done | bytes 360480 | tf_op jit(solution)/shard_map/all_to_all | solution.py:313
  18.7 3.4 %collective-permute-start = (bf16[8,1280]{1,0:T(8,128)(2,1)S(1)}, bf16[8,1280]{1,0:T(8,128)(2,1)S(1)}, u32[]{:S(2)}, u32[]{:S(2)}) collective-permute-start(bf16[8,1280]{1,0:T(8,128)(2,1)S(1)} %slice.36), channel_id=1, source_target_pairs={{0,8},{8,16},{16,24},{24,32},{32,40},{40,48},{48,56},{56,64},{64,7... | collective-permute-start | bytes 61448 | tf_op jit(solution)/shard_map/ppermute | solution.py:314
  23.4 0.7 reduce_max.9
  24.1 2.5 %collective-permute-done.halo_ref = bf16[8,1280]{1,0:T(8,128)(2,1)S(1)} collective-permute-done((bf16[8,1280]{1,0:T(8,128)(2,1)S(1)}, bf16[8,1280]{1,0:T(8,128)(2,1)S(1)}, u32[]{:S(2)}, u32[]{:S(2)}) %collective-permute-start) | collective-permute-done | bytes 20512 | tf_op jit(solution)/shard_map/ppermute | solution.py:314
  27.2 3.6 %shard_map.148 = (bf16[64,40,128]{2,1,0:T(8,128)(2,1)}, bf16[128,1280]{1,0:T(8,128)(2,1)}, f32[128,128]{1,0:T(8,128)}, f32[128,128]{1,0:T(8,128)}) custom-call(s32[3]{0:T(128)} %pad_add_fusion.place_ref, s32[7]{0:T(128)} %length_ref.5, s32[1,1]{1,0:T(1,128)S(6)} %copy.37.request_ref, bf16[128,1408]{1,0:T(8,128)(2,1)} %bitcast.52, bf16[8,1280]{1,0:T(8,128)(2,1)} %copy-done.7, ...), custom_call_target="tpu_custom_call" | custom-call | tf_op jit(solution)/shard_map/pallas_call | solution.py:229
  30.8 1.2 copy.27
  32.1 0.7 copy-done.5
  34.3 17.5 %all-to-all-start.3 = ((bf16[64,40,128]{2,1,0:T(8,128)(2,1)}), bf16[64,40,128]{2,1,0:T(8,128)(2,1)S(1)}, u32[]{:S(2)}, u32[]{:S(2)}) async-start(bf16[64,40,128]{2,1,0:T(8,128)(2,1)} %get-tuple-element.203), calls=%async_computation.3 | async-start | bytes 1310720 | tf_op jit(solution)/shard_map/all_to_all | solution.py:329
  51.8 0.7 copy.30
  52.5 35.9 %all-to-all-done.3.got_ref = bf16[64,40,128]{2,1,0:T(8,128)(2,1)S(1)} async-done(((bf16[64,40,128]{2,1,0:T(8,128)(2,1)}), bf16[64,40,128]{2,1,0:T(8,128)(2,1)S(1)}, u32[]{:S(2)}, u32[]{:S(2)}) %all-to-all-start.3) | async-done | bytes 655392 | tf_op jit(solution)/shard_map/all_to_all | solution.py:329
  88.4 3.4 %all-to-all-start.2 = ((bf16[16,8,1024]{2,0,1:T(8,128)(2,1)}), bf16[16,8,1024]{2,0,1:T(8,128)(2,1)S(1)}, u32[]{:S(2)}, u32[]{:S(2)}) async-start(bf16[16,8,1024]{2,0,1:T(8,128)(2,1)} %bitcast.33), calls=%async_computation.2 | async-start | bytes 524288 | tf_op jit(solution)/shard_map/all_to_all | solution.py:330
  91.9 2.6 %shard_map.150 = bf16[64,40,128]{2,1,0:T(8,128)(2,1)} custom-call(s32[3]{0:T(128)} %pad_add_fusion.place_ref, s32[7]{0:T(128)} %length_ref.5, bf16[64,40,128]{2,1,0:T(8,128)(2,1)} %copy-done.2, f32[7,24,128]{2,1,0:T(8,128)S(1)} %get-tuple-element.204.extra_ref), custom_call_target="tpu_custom_call" | custom-call | tf_op jit(solution)/shard_map/pallas_call | solution.py:229
  94.5 4.8 %all-to-all-done.2 = bf16[16,8,1024]{2,0,1:T(8,128)(2,1)S(1)} async-done(((bf16[16,8,1024]{2,0,1:T(8,128)(2,1)}), bf16[16,8,1024]{2,0,1:T(8,128)(2,1)S(1)}, u32[]{:S(2)}, u32[]{:S(2)}) %all-to-all-start.2) | async-done | bytes 262176 | tf_op jit(solution)/shard_map/all_to_all | solution.py:330
  99.3 0.7 copy-done.3
  100.0 6.0 %all-to-all-start.4 = ((bf16[64,40,128]{2,1,0:T(8,128)(2,1)}), bf16[64,40,128]{2,1,0:T(8,128)(2,1)S(1)}, u32[]{:S(2)}, u32[]{:S(2)}) async-start(bf16[64,40,128]{2,1,0:T(8,128)(2,1)} %shard_map.150), calls=%async_computation.4 | async-start | bytes 1310720 | tf_op jit(solution)/shard_map/all_to_all | solution.py:345
  106.0 2.8 %shard_map.149 = (f32[128,1024]{1,0:T(8,128)}, f32[128,1024]{1,0:T(8,128)}) custom-call(s32[3]{0:T(128)} %pad_add_fusion.place_ref, s32[7]{0:T(128)} %length_ref.5, bf16[128,1280]{1,0:T(8,128)(2,1)} %get-tuple-element.265.act_ref, f32[128,128]{1,0:T(8,128)} %get-tuple-element.263.decay_ref, f32[128,128]{1,0:T(8,128)} %get-tuple-element.264.step_ref, ...), custom_call_target="tpu_custom_call" | custom-call | tf_op jit(solution)/shard_map/pallas_call | solution.py:229
  108.8 35.1 %all-to-all-done.4.got_ref = bf16[64,40,128]{2,1,0:T(8,128)(2,1)S(1)} async-done(((bf16[64,40,128]{2,1,0:T(8,128)(2,1)}), bf16[64,40,128]{2,1,0:T(8,128)(2,1)S(1)}, u32[]{:S(2)}, u32[]{:S(2)}) %all-to-all-start.4) | async-done | bytes 655392 | tf_op jit(solution)/shard_map/all_to_all | solution.py:345
  143.9 0.8 copy-done.1
  144.8 2.8 %shard_map.151 = (bf16[128,1024]{1,0:T(8,128)(2,1)}, f32[1024,128]{1,0:T(8,128)}, bf16[1,3,1024]{2,1,0:T(4,128)(2,1)}, bf16[1,3,256]{2,1,0:T(4,128)(2,1)}) custom-call(bf16[128,1280]{1,0:T(8,128)(2,1)} %get-tuple-element.265.act_ref, f32[128,1024]{1,0:T(8,128)} %get-tuple-element.201.own_ref, f32[128,1024]{1,0:T(8,128)} %get-tuple-element.202.in_ref, ...), custom_call_target="tpu_custom_call" | custom-call | tf_op jit(solution)/shard_map/pallas_call | solution.py:229
  (43 shorter events, 4.7 us)
Async XLA Ops:
  0.6 0.7 copy-start.12
  1.5 0.7 copy-start.10
  2.4 0.7 copy-start.13
  2.4 0.7 copy-start.14
  5.6 4.8 %copy-start.9 = (f32[4,1024]{1,0:T(4,128)S(1)}, f32[4,1024]{1,0:T(4,128)}, u32[]{:S(2)}) copy-start(f32[4,1024]{1,0:T(4,128)} %param.21) | copy-start | bytes 49156
  5.6 4.8 %copy-start.11 = (f32[4,256]{1,0:T(4,128)S(1)}, f32[4,256]{1,0:T(4,128)}, u32[]{:S(2)}) copy-start(f32[4,256]{1,0:T(4,128)} %param.22) | copy-start | bytes 12292
  5.6 13.2 %all-to-all-start.1 = ((bf16[8,16,1408]{2,1,0:T(8,128)(2,1)}), bf16[8,16,1408]{2,1,0:T(8,128)(2,1)S(1)}, u32[]{:S(2)}, u32[]{:S(2)}) async-start(bf16[8,16,1408]{2,1,0:T(8,128)(2,1)} %shard_map.147), calls=%async_computation.1 | async-start | bytes 720896 | tf_op jit(solution)/shard_map/all_to_all | solution.py:313
  18.7 7.8 %copy-start = (bf16[8,16,1408]{2,1,0:T(8,128)(2,1)}, bf16[8,16,1408]{2,1,0:T(8,128)(2,1)S(1)}, u32[]{:S(2)}) copy-start(bf16[8,16,1408]{2,1,0:T(8,128)(2,1)S(1)} %all-to-all-done.1) | copy-start | bytes 1081348
  18.7 7.8 %collective-permute-start = (bf16[8,1280]{1,0:T(8,128)(2,1)S(1)}, bf16[8,1280]{1,0:T(8,128)(2,1)S(1)}, u32[]{:S(2)}, u32[]{:S(2)}) collective-permute-start(bf16[8,1280]{1,0:T(8,128)(2,1)S(1)} %slice.36), channel_id=1, source_target_pairs={{0,8},{8,16},{16,24},{24,32},{32,40},{40,48},{48,56},{56,64},{64,7... | collective-permute-start | bytes 61448 | tf_op jit(solution)/shard_map/ppermute | solution.py:314
  26.6 0.6 copy-start.7
  30.8 1.2 copy-start.4
  32.0 0.8 copy-start.5
  32.8 0.7 copy-start.8
  34.2 17.5 %copy-start.6 = (bf16[16,8192]{1,0:T(8,128)(2,1)S(1)}, bf16[16,8192]{1,0:T(8,128)(2,1)}, u32[]{:S(2)}) copy-start(bf16[16,8192]{1,0:T(8,128)(2,1)} %param.16) | copy-start | bytes 786436
  34.3 54.2 %all-to-all-start.3 = ((bf16[64,40,128]{2,1,0:T(8,128)(2,1)}), bf16[64,40,128]{2,1,0:T(8,128)(2,1)S(1)}, u32[]{:S(2)}, u32[]{:S(2)}) async-start(bf16[64,40,128]{2,1,0:T(8,128)(2,1)} %get-tuple-element.203), calls=%async_computation.3 | async-start | bytes 1310720 | tf_op jit(solution)/shard_map/all_to_all | solution.py:329
  88.4 3.4 %copy-start.2 = (bf16[64,40,128]{2,1,0:T(8,128)(2,1)}, bf16[64,40,128]{2,1,0:T(8,128)(2,1)S(1)}, u32[]{:S(2)}) copy-start(bf16[64,40,128]{2,1,0:T(8,128)(2,1)S(1)} %all-to-all-done.3.got_ref) | copy-start | bytes 1966084
  88.4 10.9 %all-to-all-start.2 = ((bf16[16,8,1024]{2,0,1:T(8,128)(2,1)}), bf16[16,8,1024]{2,0,1:T(8,128)(2,1)S(1)}, u32[]{:S(2)}, u32[]{:S(2)}) async-start(bf16[16,8,1024]{2,0,1:T(8,128)(2,1)} %bitcast.33), calls=%async_computation.2 | async-start | bytes 524288 | tf_op jit(solution)/shard_map/all_to_all | solution.py:330
  99.3 0.7 copy-start.3
  100.0 43.9 %all-to-all-start.4 = ((bf16[64,40,128]{2,1,0:T(8,128)(2,1)}), bf16[64,40,128]{2,1,0:T(8,128)(2,1)S(1)}, u32[]{:S(2)}, u32[]{:S(2)}) async-start(bf16[64,40,128]{2,1,0:T(8,128)(2,1)} %shard_map.150), calls=%async_computation.4 | async-start | bytes 1310720 | tf_op jit(solution)/shard_map/all_to_all | solution.py:345
  143.9 0.8 copy-start.1

commit v2 on v1

v2 whole, which is shorter than its diff:
```python
import jax
import jax.numpy as jnp
from jax import lax
from jax.experimental import pallas as pl
from jax.experimental.pallas import tpu as pltpu
from jax.sharding import Mesh
from jax.sharding import PartitionSpec as P

STATE = 128
EPSILON = 1e-05
PROMPTS = 7
HEAD = 64
BLOCK = 128
ZS, XS, HS = 16, 4, 8
ROW = 512
BLOCKS = ROW // BLOCK
WIDTH = 256
WIDE = 512
GATE = WIDE + 128
SENT = GATE + WIDTH
SLOTS = 3
TAIL = 16 * (SLOTS + 1)
BIG = 1 << 30
F32 = jnp.float32
BF16 = jnp.bfloat16


def dot(a, b, dims, precision=None):
    return lax.dot_general(a, b, (dims, ((), ())), precision=precision, preferred_element_type=F32)


def bounds(length_ref):
    starts, ends = [], []
    total = jnp.int32(0)
    for p in range(PROMPTS):
        starts.append(total)
        total = total + length_ref[p]
        ends.append(total - 1)
    return starts, ends


def segment_at(position, starts):
    found = jnp.zeros_like(position) - 1
    for start in starts:
        found = found + (position >= start).astype(jnp.int32)
    return found


def iota(shape, axis):
    return lax.broadcasted_iota(jnp.int32, shape, axis)


def spread(weights, tile, lane):
    left = jnp.broadcast_to(weights[:, 2 * tile : 2 * tile + 1], lane.shape)
    right = jnp.broadcast_to(weights[:, 2 * tile + 1 : 2 * tile + 2], lane.shape)
    return jnp.where(lane < HEAD, left, right)


def laid_out(value, at, lane):
    value = jnp.where(lane < 4, value, 0.0)
    first = value.astype(BF16).astype(F32)
    second = (value - first).astype(BF16).astype(F32)
    third = value - first - second
    out = jnp.zeros_like(value)
    for k, part in enumerate((first, second, third)):
        shift = at + 4 * k
        out = out + (pltpu.roll(part, shift, 1) if shift else part)
    return out


def picks(head, at):
    lane = iota((128, 128), 0)
    return ((lane == at + head) | (lane == at + 4 + head) | (lane == at + 8 + head)).astype(BF16)


def pack_kernel(request_ref, inner_ref, proj_ref, step_ref, gate_ref, out_ref):
    step = step_ref[...].astype(F32)
    lane = iota(step.shape, 1)
    request = request_ref[0, 0].astype(F32)
    for q in range(XS):
        for h in range(HS):
            at = q * HS + h
            col = h * 1024 + q * WIDTH
            out_ref[at, :, 0:WIDTH] = inner_ref[:, col : col + WIDTH]
            out_ref[at, :, WIDTH:WIDE] = proj_ref[:, h * 256 : (h + 1) * 256]
            shift = (128 - (16 * h + 4 * q)) % 128
            own = pltpu.roll(step, shift, 1) if shift else step
            out_ref[at, :, WIDE:GATE] = jnp.where(lane == 4, request, own).astype(BF16)
            out_ref[at, :, GATE:] = gate_ref[:, col : col + WIDTH]


def front_kernel(
    place_ref, length_ref, rows_ref, halo_ref, inner_taps_ref, state_taps_ref, head_ref,
    message_ref, act_ref, decay_ref, step_ref, padded, weighted,
):
    first = place_ref[0] * ROW
    quarter = place_ref[1]
    starts, ends = bounds(length_ref)
    lane = iota((BLOCK, 128), 1)
    sub = iota((BLOCK, 128), 0)
    before = segment_at(first - 1, starts)
    last = segment_at(first + ROW - 1, starts)
    found = [[jnp.int32(BIG), jnp.int32(-2), jnp.int32(0)] for _ in range(SLOTS)]
    count = jnp.int32(0)
    for p in range(PROMPTS):
        here = (ends[p] >= first) & (ends[p] < first + ROW)
        for m in range(SLOTS):
            mine = here & (count == m)
            for at, value in enumerate((ends[p], jnp.int32(p), starts[p])):
                found[m][at] = jnp.where(mine, value, found[m][at])
        count = count + here.astype(jnp.int32)
    heads = pltpu.roll(head_ref[...], place_ref[2], 1)
    bias = heads[0:1, :]
    scale = -jnp.exp(heads[1:2, :])
    lower = (sub >= lane).astype(F32)

    padded[0:8, :] = halo_ref[...].astype(F32)
    padded[8:, :] = rows_ref[:, 0:WIDE].astype(F32)
    carry = jnp.zeros((1, 128), F32)
    for b in range(BLOCKS):
        rows = slice(b * BLOCK, (b + 1) * BLOCK)
        position = sub + (first + b * BLOCK)
        row_start = jnp.zeros_like(position)
        for start in starts:
            row_start = jnp.where(position >= start, start, row_start)
        inside = [(position - 3 + k) >= row_start for k in range(4)]
        for tile in range(WIDE // 128):
            cols = slice(tile * 128, (tile + 1) * 128)
            total = jnp.zeros((BLOCK, 128), F32)
            for k in range(4):
                if tile < 2:
                    at = pl.multiple_of(quarter * WIDTH + tile * 128, 128)
                    taps = inner_taps_ref[k : k + 1, pl.ds(at, 128)]
                else:
                    taps = state_taps_ref[k : k + 1, (tile - 2) * 128 : (tile - 1) * 128]
                at = b * BLOCK + 5 + k
                total = total + jnp.where(inside[k], padded[at : at + BLOCK, cols], 0.0) * taps
            act_ref[rows, cols] = (total * jax.nn.sigmoid(total)).astype(BF16)
        step = jax.nn.softplus(rows_ref[rows, WIDE:GATE].astype(F32) + bias)
        decay = dot(lower, step * scale, ((1,), (0,)), lax.Precision.HIGHEST) + carry
        carry = decay[BLOCK - 1 : BLOCK, :]
        step_ref[rows, :] = step
        decay_ref[rows, :] = decay
    row = iota((1, 128), 1)
    index = iota((8, 128), 0)
    small = laid_out(jnp.where(last == before, jnp.exp(carry), 0.0), 0, row)
    edges = []
    for m in range(-1, SLOTS):
        if m < 0:
            end_decay = carry
        else:
            end, prompt, start = found[m]
            some = end < BIG
            local = jnp.where(some, end - first, 0)
            end_decay = decay_ref[pl.ds(local, 1), :]
        for b in range(BLOCKS):
            rows = slice(b * BLOCK, (b + 1) * BLOCK)
            position = sub + (first + b * BLOCK)
            if m < 0:
                member = segment_at(position, starts) == last
            else:
                member = some & (position >= start) & (position <= end)
            gap = jnp.minimum(end_decay - decay_ref[rows, :], 0.0)
            weights = jnp.where(member, jnp.exp(gap), 0.0) * step_ref[rows, :]
            for tile in range(2):
                cols = slice(tile * 128, (tile + 1) * 128)
                weighted[rows, cols] = (spread(weights, tile, lane) * act_ref[rows, cols].astype(F32)).astype(BF16)
        at = 16 * (m + 1)
        for tile in range(2):
            state = dot(weighted[:, tile * 128 : (tile + 1) * 128], act_ref[:, WIDTH : WIDTH + STATE], ((0,), (0,)))
            message_ref[tile * 8 : (tile + 1) * 8, at : at + 16, :] = state.astype(BF16).reshape(8, 16, 128)
        if m < 0:
            continue
        carried = jnp.where(some & (prompt == before), jnp.exp(end_decay), 0.0)
        small = small + laid_out(carried, 12 * (m + 1), row)
        edge = []
        for k in range(3):
            valid = some & (end - 2 + k >= start)
            edge.append(jnp.where(valid, padded[pl.ds(8 + local - 2 + k, 1), :], 0.0))
        edges.append(edge)
    for k in range(XS):
        request = rows_ref[k * BLOCK : k * BLOCK + 8, WIDE:GATE].astype(F32)[0:1, :]
        small = small + jnp.where(row == 64 + k, pltpu.roll(request, 60 + k, 1), 0.0)
    block = jnp.where(index == SLOTS, small, jnp.zeros((8, 128), F32))
    for k in range(ZS):
        value = block
        if k < 12:
            for m in range(SLOTS):
                piece = edges[m][k // 4][:, (k % 4) * 128 : (k % 4 + 1) * 128]
                value = jnp.where(index == m, piece, value)
        message_ref[k, TAIL : TAIL + 8, :] = value.astype(BF16)


def scan_kernel(place_ref, length_ref, got_ref, extra_ref, out_ref, small, states, finals):
    _, ends = bounds(length_ref)
    head = place_ref[0] // 4
    one = [picks(head, 12 * m) for m in range(SLOTS + 1)]
    one = one + [(iota((128, 128), 0) == 64 + k).astype(BF16) for k in range(XS)]
    small[...] = dot(got_ref[:, TAIL : TAIL + 8, :].reshape(ZS * 8, 128), jnp.concatenate(one, axis=1), ((1,), (0,)))
    state = jnp.zeros((16, 128), F32)
    for j in range(ZS):
        states[j] = state
        out_ref[j, 0:16, :] = state.astype(BF16)
        at = 8 * j + SLOTS
        state = small[at : at + 1, 0:128] * state + got_ref[j, 0:16, :].astype(F32)
    for p in range(PROMPTS):
        z = ends[p] // ROW
        rank = jnp.int32(0)
        for other in range(p):
            rank = rank + (ends[other] // ROW == z).astype(jnp.int32)
        value = extra_ref[p]
        state = states[z]
        tail = got_ref[z, TAIL : TAIL + 8, :].astype(F32)
        factor = small[pl.ds(8 * z + SLOTS, 1), 128 : 128 * (SLOTS + 1)]
        for m in range(SLOTS):
            own = got_ref[z, 16 * m + 16 : 16 * m + 32, :].astype(F32) + factor[:, 128 * m : 128 * (m + 1)] * state
            edge = jnp.broadcast_to(tail[m : m + 1, :], (8, 128))
            value = jnp.where(rank == m, jnp.concatenate([own, edge], axis=0), value)
        finals[p] = value
    index = iota((8, 128), 0)
    for z in range(ZS):
        edges = jnp.zeros((8, 128), F32)
        for k in range(XS):
            at = 128 * (SLOTS + 1 + k)
            request = small[8 * z + SLOTS : 8 * z + SLOTS + 1, at : at + 128]
            value = finals[0]
            for p in range(1, PROMPTS):
                value = jnp.where(request == float(p), finals[p], value)
            out_ref[z, 16 * k + 16 : 16 * k + 32, :] = value[0:16].astype(BF16)
            edges = jnp.where(index == k, value[16:24], edges)
        out_ref[z, 80:88, :] = edges.astype(BF16)


def within_kernel(
    place_ref, length_ref, act_ref, decay_ref, step_ref, rows_ref, skip_ref, own_ref, in_ref, carried,
):
    first = place_ref[0] * ROW
    quarter = place_ref[1]
    starts, _ = bounds(length_ref)
    before_row = segment_at(first - 1, starts)
    lane = iota((BLOCK, 128), 1)
    sub = iota((BLOCK, 128), 0)
    carry = jnp.zeros((1, 128), F32)
    for b in range(BLOCKS):
        rows = slice(b * BLOCK, (b + 1) * BLOCK)
        at = first + b * BLOCK
        before = segment_at(at - 1, starts)
        last = segment_at(at + BLOCK - 1, starts)
        segment = segment_at(sub + at, starts)
        causal = (segment == segment_at(lane + at, starts)) & (sub >= lane)
        write = act_ref[rows, WIDTH : WIDTH + STATE]
        read = act_ref[rows, WIDTH + STATE : WIDE]
        scores = dot(read, write, ((1,), (1,)))
        decay = decay_ref[rows, :]
        step = step_ref[rows, :]
        decay_t = decay.T
        step_t = step.T
        inflow = jnp.where(segment == before, jnp.exp(jnp.minimum(decay - carry, 0.0)), 0.0)
        inflow_row = jnp.where(segment == before_row, jnp.exp(decay), 0.0)
        end = decay[BLOCK - 1 : BLOCK, :]
        tail = jnp.where(segment == last, jnp.exp(jnp.minimum(end - decay, 0.0)), 0.0) * step
        keep = jnp.where(last == before, jnp.exp(end - carry), 0.0)
        for tile in range(2):
            cols = slice(tile * 128, (tile + 1) * 128)
            x = act_ref[rows, cols]
            mixing = []
            for head in (2 * tile, 2 * tile + 1):
                gap = decay[:, head : head + 1] - decay_t[head : head + 1, :]
                weight = jnp.exp(jnp.where(causal, gap, -jnp.inf))
                mixing.append((scores * weight * step_t[head : head + 1, :]).astype(BF16))
            none = jnp.zeros_like(x)
            both = jnp.concatenate([jnp.where(lane < HEAD, x, none), jnp.where(lane < HEAD, none, x)], axis=0)
            value = dot(jnp.concatenate(mixing, axis=1), both, ((1,), (0,)))
            skip = skip_ref[0:1, pl.ds(pl.multiple_of(quarter * WIDTH + tile * 128, 128), 128)]
            value = value + skip * x.astype(F32)
            if b:
                across = dot(read.astype(F32), carried[tile], ((1,), (1,)), lax.Precision.HIGHEST)
                value = value + spread(inflow, tile, lane) * across
            gate = rows_ref[rows, GATE + tile * 128 : GATE + (tile + 1) * 128].astype(F32)
            gate = gate * jax.nn.sigmoid(gate)
            own_ref[rows, cols] = value * gate
            in_ref[rows, cols] = spread(inflow_row, tile, lane) * gate
            if b < BLOCKS - 1:
                weighted = (spread(tail, tile, lane) * x.astype(F32)).astype(BF16)
                state = dot(weighted, write, ((0,), (0,)))
                if b:
                    factor = jnp.where(sub < HEAD, keep[:, 2 * tile : 2 * tile + 1], keep[:, 2 * tile + 1 : 2 * tile + 2])
                    state = factor * carried[tile] + state
                carried[tile] = state
        carry = end


def across_kernel(act_ref, own_ref, in_ref, got_ref, out_ref):
    for tile in range(2):
        cols = slice(tile * 128, (tile + 1) * 128)
        state = got_ref[tile * 8 : (tile + 1) * 8, 0:16, :].reshape(128, 128)
        for b in range(BLOCKS):
            rows = slice(b * BLOCK, (b + 1) * BLOCK)
            across = dot(act_ref[rows, WIDTH + STATE : WIDE], state, ((1,), (1,)))
            value = own_ref[rows, cols] + in_ref[rows, cols] * across
            out_ref[b, tile * BLOCK : (tile + 1) * BLOCK, :] = value.astype(BF16)
    index = iota((16, 128), 0)
    edges = [jnp.zeros((16, 128), F32) for _ in range(XS)]
    for i in range(ZS):
        tail = got_ref[i, 80:88, :].astype(F32)
        for k in range(XS):
            at = 2 * BLOCK + 16 * i
            out_ref[k, at : at + 16, :] = got_ref[i, 16 * k + 16 : 16 * k + 32, :]
            if i < 12:
                edges[k] = jnp.where(index == i, tail[k : k + 1, :], edges[k])
    for k in range(XS):
        out_ref[k, 512:528, :] = edges[k].astype(BF16)


def last_kernel(got_ref, gain_ref, hidden_ref, final_ref, inner_ref, proj_ref):
    total = jnp.zeros((BLOCK, 128), F32)
    for q in range(XS):
        for tile in range(2):
            value = got_ref[q, tile * BLOCK : (tile + 1) * BLOCK, :].astype(F32)
            total = total + value * value
    mean = jnp.sum(total, axis=1, keepdims=True) * (1.0 / (XS * WIDTH))
    inverse = lax.rsqrt(mean + EPSILON)
    for q in range(XS):
        for tile in range(2):
            cols = slice(q * WIDTH + tile * 128, q * WIDTH + (tile + 1) * 128)
            value = got_ref[q, tile * BLOCK : (tile + 1) * BLOCK, :].astype(F32)
            hidden_ref[:, cols] = ((value * inverse) * gain_ref[:, cols]).astype(BF16)
        final_ref[q * WIDTH : (q + 1) * WIDTH, :] = got_ref[q, 256:512, :].astype(F32)
        edges = got_ref[q, 512:528, :].astype(F32)
        for k in range(3):
            for c in range(2):
                at = q * WIDTH + c * 128
                inner_ref[0, k : k + 1, at : at + 128] = edges[4 * k + c : 4 * k + c + 1, :].astype(BF16)
                if q == 0:
                    proj_ref[0, k : k + 1, c * 128 : (c + 1) * 128] = edges[4 * k + 2 + c : 4 * k + 3 + c, :].astype(BF16)


def call(kernel, ins, outs, scratch=(), scalars=0, limit=24 << 20):
    smem = pl.BlockSpec(memory_space=pltpu.SMEM)
    vmem = pl.BlockSpec(memory_space=pltpu.VMEM)
    return pl.pallas_call(
        kernel,
        out_shape=outs,
        in_specs=[smem] * scalars + [vmem] * (len(ins) - scalars),
        out_specs=jax.tree.map(lambda _: vmem, outs),
        scratch_shapes=list(scratch),
        compiler_params=pltpu.CompilerParams(vmem_limit_bytes=limit),
    )(*ins)


def exchange(sent, place):
    k = jnp.arange(ZS, dtype=jnp.int32)
    held = sent[(k + place) % ZS]
    for shift in (1, 2, 4, 8):
        moved = lax.ppermute(held, "z", [(source, (source + shift) % ZS) for source in range(ZS)])
        held = jnp.where(((k & shift) != 0)[:, None, None], moved, held)
    return held[(place - k) % ZS]


def later_ends(place, prompt_lengths, rows, halo, act, decay, step):
    ends = jnp.cumsum(prompt_lengths) - 1
    starts = ends + 1 - prompt_lengths
    ids = jnp.arange(PROMPTS, dtype=jnp.int32)
    z = ends // ROW
    rank = jnp.sum((z[None, :] == z[:, None]) & (ids[None, :] < ids[:, None]), axis=1)
    position = place * ROW + jnp.arange(ROW, dtype=jnp.int32)

    def step_of(carry):
        k, extra = carry
        mine = (z == place) & (rank == k)
        some = jnp.any(mine)
        end = jnp.sum(jnp.where(mine, ends, 0))
        start = jnp.sum(jnp.where(mine, starts, 0))
        member = some & (position >= start) & (position <= end)
        end_decay = jnp.sum(jnp.where((position == end)[:, None], decay, 0.0), axis=0, keepdims=True)
        weights = jnp.where(member[:, None], jnp.exp(jnp.minimum(end_decay - decay, 0.0)), 0.0) * step
        weights = weights[:, : WIDTH // HEAD]
        x = act[:, :WIDTH].reshape(ROW, -1, HEAD).astype(F32)
        weighted = (weights[:, :, None] * x).reshape(ROW, WIDTH).astype(BF16)
        own = dot(weighted, act[:, WIDTH : WIDTH + STATE], ((0,), (0,))).astype(BF16)
        padded = jnp.concatenate([halo, rows[:, :WIDE]], axis=0)
        wanted = end - 2 + jnp.arange(3, dtype=jnp.int32)
        onehot = (jnp.arange(ROW + 8)[None, :] + (place * ROW - 8) == wanted[:, None]) & some
        onehot = onehot & (wanted >= start)[:, None]
        edge = dot(onehot.astype(BF16), padded, ((1,), (0,))).astype(BF16)
        edge = jnp.pad(edge.reshape(12, 1, 128), ((0, 4), (0, 7), (0, 0)))
        sent = jnp.concatenate([own.reshape(ZS, 16, 128), edge], axis=1)
        taken = exchange(sent, place)[z].astype(F32)
        taken = jnp.concatenate([taken[:, :16], jnp.broadcast_to(taken[:, 16:17], (PROMPTS, 8, 128))], axis=1)
        return k + 1, jnp.where((rank == k)[:, None, None], taken, extra)

    most = jnp.max(rank)
    none = jnp.zeros((PROMPTS, 24, 128), F32)
    return lax.cond(
        most >= SLOTS,
        lambda: lax.while_loop(lambda carry: carry[0] <= most, step_of, (jnp.full_like(most, SLOTS), none))[1],
        lambda: none,
    )


def per_device(
    head_inputs,
    state_proj,
    gate_inputs,
    step_raw,
    step_bias,
    decay_log,
    skip_gain,
    filter_inner,
    filter_state,
    norm_gain,
    prompt_lengths,
    request_prompt,
):
    shape = jax.ShapeDtypeStruct
    place = lax.axis_index("z").astype(jnp.int32)
    quarter = lax.axis_index("x").astype(jnp.int32)
    heads = step_bias.shape[0]
    places = jnp.stack([place, quarter, (128 - 4 * quarter) % 128])
    heads_in = jnp.pad(jnp.stack([step_bias, decay_log]), ((0, 6), (0, 128 - heads)))
    skip = jnp.repeat(skip_gain, HEAD)[None]
    packed = call(
        pack_kernel,
        (request_prompt, head_inputs, state_proj, step_raw, gate_inputs),
        shape((XS * HS, 16, SENT), BF16),
        scalars=1,
        limit=None,
    )
    rows = lax.all_to_all(packed, ("x", "head"), 0, 0).reshape(ROW, SENT)
    halo = lax.ppermute(rows[ROW - 8 :, :WIDE], "z", [(source, source + 1) for source in range(ZS - 1)])
    message, act, decay, step = call(
        front_kernel,
        (places, prompt_lengths, rows, halo, filter_inner, filter_state, heads_in),
        (
            shape((ZS, TAIL + 8, 128), BF16),
            shape((ROW, WIDE), BF16),
            shape((ROW, 128), F32),
            shape((ROW, 128), F32),
        ),
        (pltpu.VMEM((ROW + 8, WIDE), F32), pltpu.VMEM((ROW, WIDTH), BF16)),
        scalars=2,
    )
    got = lax.all_to_all(message, "z", 0, 0)
    own, inflow = call(
        within_kernel,
        (places, prompt_lengths, act, decay, step, rows, skip),
        (shape((ROW, WIDTH), F32), shape((ROW, WIDTH), F32)),
        (pltpu.VMEM((2, 128, 128), F32),),
        scalars=2,
    )
    own, rows, halo, act, decay, step = lax.optimization_barrier((own, rows, halo, act, decay, step))
    extra = later_ends(place, prompt_lengths, rows, halo, act, decay, step)
    answer = call(
        scan_kernel,
        (places, prompt_lengths, got, extra),
        shape((ZS, 88, 128), BF16),
        (
            pltpu.VMEM((ZS * 8, 128 * (SLOTS + 1 + XS)), F32),
            pltpu.VMEM((ZS, 16, 128), F32),
            pltpu.VMEM((PROMPTS, 24, 128), F32),
        ),
        scalars=2,
    )
    back = lax.all_to_all(answer, "z", 0, 0)
    shared = call(across_kernel, (act, own, inflow, back), shape((XS, 528, 128), BF16))
    shared = lax.all_to_all(shared, "x", 0, 0)
    hidden, final, edge_inner, edge_state = call(
        last_kernel,
        (shared, norm_gain[None]),
        (
            shape((BLOCK, XS * WIDTH), BF16),
            shape((XS * WIDTH, STATE), F32),
            shape((1, 3, XS * WIDTH), BF16),
            shape((1, 3, 256), BF16),
        ),
    )
    return hidden, final.reshape(1, heads, HEAD, STATE), edge_inner, edge_state


def solution(mesh):
    seq = ("z", "x")
    mesh = Mesh(mesh.devices.reshape(ZS, XS, HS), ("z", "x", "head"))
    tokens = P(("z", "x", "head"), None)
    return jax.shard_map(
        per_device,
        mesh=mesh,
        in_specs=(
            tokens,
            tokens,
            tokens,
            tokens,
            P("head"),
            P("head"),
            P("head"),
            P(None, "head"),
            P(None, "head"),
            P("head"),
            P(),
            P(seq, None),
        ),
        out_specs=(
            P(seq, "head"),
            P(seq, "head", None, None),
            P(seq, None, "head"),
            P(seq, None, "head"),
        ),
        check_vma=False,
    )
```

time: 148 us -> 114 us (0.77)
  waiting for transfers between devices: 86.1 us -> 28.7 us
  blocking collectives: 0 us -> 39.8 us
  local copies, waits for them, and re-layouts: 7.98 us -> 0.84 us
  starting transfers between devices: 34.9 us -> 28.3 us
  other arithmetic: 2.95 us -> 1.12 us
    all_to_all x4 -> x2, waiting for transfers between devices: 83.6 us -> 27.5 us  [the longest x1 14.2 us: per_device(): got = lax.all_to_all(message, 'z', 0, 0)]
    all_to_all x0 -> x2, blocking collectives: none -> 39.8 us  [the longest x1 27.9 us: per_device(): back = lax.all_to_all(answer, 'z', 0, 0)]
    unnamed x33 -> x14, local copies, waits for them, and re-layouts: 6.92 us -> 0.03 us
    all_to_all x4 -> x2, starting transfers between devices: 31.5 us -> 26.4 us  [the longest x1 16.8 us: per_device(): got = lax.all_to_all(message, 'z', 0, 0)]
    ppermute x1, starting transfers between devices: 3.39 us -> 1.83 us  [per_device(): lax.ppermute(rows[ROW - 8:, :WIDE], 'z', [(source, source + 1) for source...]
    pallas_call x5 -> x6, Pallas kernels: 13.6 us -> 12.2 us  [call(): pl.pallas_call(kernel, out_shape=outs, in_specs=[smem] * scalars + [vmem]...]
  transfers between devices with their start and end apart: 5 -> 3, of which waited for: 5 -> 3; matrix products, arithmetic and copies ran while one was open for 2% -> 2% of each run, Pallas kernels for 4% -> 2%
where the time goes in v2:
time: 114 us; the launch traced here: 113 us
  blocking collectives  39.8 us (35%)
  waiting for transfers between devices  28.7 us (25%)
  starting transfers between devices  28.3 us (25%)
  Pallas kernels  12.2 us (11%)
  between operations  2.11 us (2%)
    all_to_all x1, blocking collectives, per_device(): back = lax.all_to_all(answer, 'z', 0, 0)  27.9 us
    all_to_all x1, starting transfers between devices, per_device(): got = lax.all_to_all(message, 'z', 0, 0)  16.8 us
    all_to_all x1, waiting for transfers between devices, per_device(): got = lax.all_to_all(message, 'z', 0, 0)  14.2 us
    all_to_all x1, waiting for transfers between devices, per_device(): rows = lax.all_to_all(packed, ('x', 'head'), 0, 0).reshape(ROW, SENT)  13.3 us
    pallas_call x6, Pallas kernels, call(): pl.pallas_call(kernel, out_shape=outs, in_specs=[smem] * scalars + [vmem]...  12.2 us
    all_to_all x1, blocking collectives, per_device(): shared = lax.all_to_all(shared, 'x', 0, 0)  11.9 us
    all_to_all x1, starting transfers between devices, per_device(): rows = lax.all_to_all(packed, ('x', 'head'), 0, 0).reshape(ROW, SENT)  9.64 us
  transfers between devices with their start and end apart: 3, of which 3 were waited for; matrix products, arithmetic and copies ran while one was open for 2% of the time, Pallas kernels for 2%

profile of v2, /device:TPU:2, one launch (start us, length us, event | category | flops | bytes accessed | tf_op | source)
XLA Modules:
  0.0 113.1 jit_solution(9972392002479974875)
XLA Ops:
  1.3 2.1 %shard_map.147 = bf16[32,16,896]{2,1,0:T(8,128)(2,1)} custom-call(s32[1,1]{1,0:T(1,128)S(6)} %copy.39.request_ref, bf16[16,8192]{1,0:T(8,128)(2,1)} %inner_ref.1, bf16[16,2048]{1,0:T(8,128)(2,1)} %proj_ref.1, bf16[16,128]{1,0:T(8,128)(2,1)} %step_ref.1, bf16[16,8192]{1,0:T(8,128)(2,1)} %gate_ref.1), custom_call_target="tpu_custom_call" | custom-call | tf_op jit(solution)/shard_map/pallas_call | solution.py:341
  3.4 0.0 copy-start.4
  3.4 9.6 %all-to-all-start = ((bf16[32,16,896]{2,1,0:T(8,128)(2,1)}), bf16[32,16,896]{2,1,0:T(8,128)(2,1)S(1)}, u32[]{:S(2)}, u32[]{:S(2)}) async-start(bf16[32,16,896]{2,1,0:T(8,128)(2,1)} %shard_map.147), calls=%async_computation | async-start | bytes 1835008 | tf_op jit(solution)/shard_map/all_to_all | solution.py:429
  13.1 0.0 copy-start.7
  13.2 13.3 %all-to-all-done = bf16[32,16,896]{2,1,0:T(8,128)(2,1)S(1)} async-done(((bf16[32,16,896]{2,1,0:T(8,128)(2,1)}), bf16[32,16,896]{2,1,0:T(8,128)(2,1)S(1)}, u32[]{:S(2)}, u32[]{:S(2)}) %all-to-all-start) | async-done | bytes 917536 | tf_op jit(solution)/shard_map/all_to_all | solution.py:429
  26.5 1.8 %collective-permute-start.4 = (bf16[8,512]{1,0:T(8,128)(2,1)S(1)}, bf16[8,512]{1,0:T(8,128)(2,1)S(1)}, u32[]{:S(2)}, u32[]{:S(2)}) collective-permute-start(bf16[8,512]{1,0:T(8,128)(2,1)S(1)} %slice.50), channel_id=1, source_target_pairs={{0,32},{32,64},{64,96},{96,128},{128,160},{160,192},{192,224},{224... | collective-permute-start | bytes 24584 | tf_op jit(solution)/shard_map/ppermute | solution.py:430
  28.3 0.1 pad_add_fusion.place_ref
  28.4 1.3 %collective-permute-done.4.halo_ref = bf16[8,512]{1,0:T(8,128)(2,1)S(1)} collective-permute-done((bf16[8,512]{1,0:T(8,128)(2,1)S(1)}, bf16[8,512]{1,0:T(8,128)(2,1)S(1)}, u32[]{:S(2)}, u32[]{:S(2)}) %collective-permute-start.4) | collective-permute-done | bytes 8224 | tf_op jit(solution)/shard_map/ppermute | solution.py:430
  29.7 4.6 %shard_map.148 = (bf16[16,72,128]{2,1,0:T(8,128)(2,1)}, bf16[512,512]{1,0:T(8,128)(2,1)S(1)}, f32[512,128]{1,0:T(8,128)S(1)}, f32[512,128]{1,0:T(8,128)S(1)}) custom-call(s32[3]{0:T(128)S(1)} %pad_add_fusion.place_ref, s32[7]{0:T(128)S(1)} %copy-done.4, bf16[512,896]{1,0:T(8,128)(2,1)S(1)} %bitcast.60, bf16[8,512]{1,0:T(8,128)(2,1)S(1)} %collective-permute-done.4.halo_ref, ...), custom_call_target="tpu_custom_call" | custom-call | tf_op jit(solution)/shard_map/pallas_call | solution.py:341
  34.3 16.8 %all-to-all-start.1 = ((bf16[16,72,128]{2,1,0:T(8,128)(2,1)}), bf16[16,72,128]{2,1,0:T(8,128)(2,1)S(1)}, u32[]{:S(2)}, u32[]{:S(2)}) async-start(bf16[16,72,128]{2,1,0:T(8,128)(2,1)} %get-tuple-element.287), calls=%async_computation.1 | async-start | bytes 589824 | tf_op jit(solution)/shard_map/all_to_all | solution.py:443
  51.1 0.1 broadcast_in_dim.134
  51.1 0.1 broadcast_in_dim_reshape.3.skip_ref
  51.2 0.2 reduce-window.7
  51.4 0.2 convert_reduce_fusion
  51.6 0.6 reduce_max.9
  52.9 2.6 %shard_map.149 = (f32[512,256]{1,0:T(8,128)S(1)}, f32[512,256]{1,0:T(8,128)S(1)}) custom-call(s32[3]{0:T(128)S(1)} %pad_add_fusion.place_ref, s32[7]{0:T(128)S(1)} %copy-done.4, bf16[512,512]{1,0:T(8,128)(2,1)S(1)} %get-tuple-element.284.act_ref, f32[512,128]{1,0:T(8,128)S(1)} %get-tuple-element.290.decay_ref, f32[512,128]{1,0:T(8,128)S(1)} %get-tuple-element.291.step_ref, ...), custom_call_target="tpu_custom_call" | custom-call | tf_op jit(solution)/shard_map/pallas_call | solution.py:341
  55.6 0.7 conditional.1
  55.6 0.6 broadcast_in_dim.118
  56.2 14.2 %all-to-all-done.1.got_ref = bf16[16,72,128]{2,1,0:T(8,128)(2,1)S(1)} async-done(((bf16[16,72,128]{2,1,0:T(8,128)(2,1)}), bf16[16,72,128]{2,1,0:T(8,128)(2,1)S(1)}, u32[]{:S(2)}, u32[]{:S(2)}) %all-to-all-start.1) | async-done | bytes 294944 | tf_op jit(solution)/shard_map/all_to_all | solution.py:443
  70.4 1.4 %shard_map.150 = bf16[16,88,128]{2,1,0:T(8,128)(2,1)S(1)} custom-call(s32[3]{0:T(128)S(1)} %pad_add_fusion.place_ref, s32[7]{0:T(128)S(1)} %copy-done.4, bf16[16,72,128]{2,1,0:T(8,128)(2,1)S(1)} %all-to-all-done.1.got_ref, f32[7,24,128]{2,1,0:T(8,128)} %get-tuple-element.518.extra_ref), custom_call_target="tpu_custom_call" | custom-call | tf_op jit(solution)/shard_map/pallas_call | solution.py:341
  71.8 27.9 %all_to_all.20.got_ref = bf16[16,88,128]{2,1,0:T(8,128)(2,1)S(1)} all-to-all(bf16[16,88,128]{2,1,0:T(8,128)(2,1)S(1)} %shard_map.150), channel_id=1, replica_groups=mesh['z'=16,'x'=4,'head'=8] {'z'}, dimensions={0} | all-to-all | bytes 720896 | tf_op jit(solution)/shard_map/all_to_all | solution.py:464
  99.8 0.3 shard_map.151
  100.1 11.9 %all_to_all.21.got_ref = bf16[4,528,128]{2,1,0:T(8,128)(2,1)S(1)} all-to-all(bf16[4,528,128]{2,1,0:T(8,128)(2,1)S(1)} %shard_map.151), channel_id=1, replica_groups=mesh['z'=16,'x'=4,'head'=8] {'x'}, dimensions={0} | all-to-all | bytes 1081344 | tf_op jit(solution)/shard_map/all_to_all | solution.py:466
  112.0 1.1 shard_map.152
  (21 shorter events, 0.1 us)
Async XLA Ops:
  3.4 9.7 %copy-start.5 = (f32[16]{0:T(128)S(1)}, f32[16]{0:T(128)}, u32[]{:S(2)}) copy-start(f32[16]{0:T(128)} %param.21) | copy-start | bytes 196
  3.4 9.7 %copy-start.6 = (f32[16]{0:T(128)S(1)}, f32[16]{0:T(128)}, u32[]{:S(2)}) copy-start(f32[16]{0:T(128)} %param.20) | copy-start | bytes 196
  3.4 26.2 %copy-start = (f32[4,1024]{1,0:T(4,128)S(1)}, f32[4,1024]{1,0:T(4,128)}, u32[]{:S(2)}) copy-start(f32[4,1024]{1,0:T(4,128)} %inner_taps_ref.1) | copy-start | bytes 49156
  3.4 26.2 %copy-start.1 = (f32[4,256]{1,0:T(4,128)S(1)}, f32[4,256]{1,0:T(4,128)}, u32[]{:S(2)}) copy-start(f32[4,256]{1,0:T(4,128)} %state_taps_ref.1) | copy-start | bytes 12292
  3.4 26.2 %copy-start.4 = (s32[7]{0:T(128)S(1)}, s32[7]{0:T(128)}, u32[]{:S(2)}) copy-start(s32[7]{0:T(128)} %length_ref.5) | copy-start | bytes 88
  3.4 23.0 %all-to-all-start = ((bf16[32,16,896]{2,1,0:T(8,128)(2,1)}), bf16[32,16,896]{2,1,0:T(8,128)(2,1)S(1)}, u32[]{:S(2)}, u32[]{:S(2)}) async-start(bf16[32,16,896]{2,1,0:T(8,128)(2,1)} %shard_map.147), calls=%async_computation | async-start | bytes 1835008 | tf_op jit(solution)/shard_map/all_to_all | solution.py:429
  13.1 38.0 %copy-start.7 = (f32[16]{0:T(128)S(1)}, f32[16]{0:T(128)}, u32[]{:S(2)}) copy-start(f32[16]{0:T(128)} %param.22) | copy-start | bytes 196
  26.5 3.2 %collective-permute-start.4 = (bf16[8,512]{1,0:T(8,128)(2,1)S(1)}, bf16[8,512]{1,0:T(8,128)(2,1)S(1)}, u32[]{:S(2)}, u32[]{:S(2)}) collective-permute-start(bf16[8,512]{1,0:T(8,128)(2,1)S(1)} %slice.50), channel_id=1, source_target_pairs={{0,32},{32,64},{64,96},{96,128},{128,160},{160,192},{192,224},{224... | collective-permute-start | bytes 24584 | tf_op jit(solution)/shard_map/ppermute | solution.py:430
  34.3 36.1 %all-to-all-start.1 = ((bf16[16,72,128]{2,1,0:T(8,128)(2,1)}), bf16[16,72,128]{2,1,0:T(8,128)(2,1)S(1)}, u32[]{:S(2)}, u32[]{:S(2)}) async-start(bf16[16,72,128]{2,1,0:T(8,128)(2,1)} %get-tuple-element.287), calls=%async_computation.1 | async-start | bytes 589824 | tf_op jit(solution)/shard_map/all_to_all | solution.py:443
  100.1 11.9 %copy-start.2 = (f32[1024]{0:T(1024)S(1)}, f32[1024]{0:T(1024)}, u32[]{:S(2)}) copy-start(f32[1024]{0:T(1024)} %param.25) | copy-start | bytes 12292

commit v3 on v2

--- a/solution.py
+++ b/solution.py
@@ -1,3 +1,5 @@
+import functools
+
 import jax
 import jax.numpy as jnp
 from jax import lax
@@ -16,10 +18,9 @@
 BLOCKS = ROW // BLOCK
 WIDTH = 256
 WIDE = 512
-GATE = WIDE + 128
-SENT = GATE + WIDTH
-SLOTS = 3
-TAIL = 16 * (SLOTS + 1)
+STEPS, GATE, SENT = 64, 72, 104
+FEW = 2
+REQUEST = 96
 BIG = 1 << 30
 F32 = jnp.float32
 BF16 = jnp.bfloat16
@@ -75,18 +76,119 @@
 
 def pack_kernel(request_ref, inner_ref, proj_ref, step_ref, gate_ref, out_ref):
     step = step_ref[...].astype(F32)
-    lane = iota(step.shape, 1)
+    lane = iota((8, 128), 1)
     request = request_ref[0, 0].astype(F32)
     for q in range(XS):
         for h in range(HS):
             at = q * HS + h
-            col = h * 1024 + q * WIDTH
-            out_ref[at, :, 0:WIDTH] = inner_ref[:, col : col + WIDTH]
-            out_ref[at, :, WIDTH:WIDE] = proj_ref[:, h * 256 : (h + 1) * 256]
+            for c in range(2):
+                col = h * 1024 + q * WIDTH + c * 128
+                out_ref[at, c * 16 : c * 16 + 16, :] = inner_ref[:, col : col + 128]
+                out_ref[at, GATE + c * 16 : GATE + c * 16 + 16, :] = gate_ref[:, col : col + 128]
+                col = h * 256 + c * 128
+                out_ref[at, 32 + c * 16 : 48 + c * 16, :] = proj_ref[:, col : col + 128]
             shift = (128 - (16 * h + 4 * q)) % 128
-            own = pltpu.roll(step, shift, 1) if shift else step
-            out_ref[at, :, WIDE:GATE] = jnp.where(lane == 4, request, own).astype(BF16)
-            out_ref[at, :, GATE:] = gate_ref[:, col : col + WIDTH]
+            early = pltpu.roll(step[0:8], shift, 1) if shift else step[0:8]
+            shift = (shift + 64) % 128
+            late = pltpu.roll(step[8:16], shift, 1) if shift else step[8:16]
+            own = jnp.where(lane < 64, early, late)
+            out_ref[at, STEPS:GATE, :] = jnp.where(lane == 4, request, own).astype(BF16)
+
+
+def block_of(rows_ref, b, row):
+    return rows_ref[8 * b : 8 * b + 8, row : row + 16, :].reshape(BLOCK, 128)
+
+
+def steps_of(rows_ref, b):
+    early = rows_ref[8 * b : 8 * b + 8, STEPS:GATE, :].astype(F32)
+    late = pltpu.roll(early.reshape(64, 128), 64, 1).reshape(8, 8, 128)
+    return jnp.concatenate([early, late], axis=1).reshape(BLOCK, 128)
+
+
+def padded_rows(rows_ref, halo_ref, padded):
+    for tile in range(WIDE // 128):
+        cols = slice(tile * 128, (tile + 1) * 128)
+        padded[0:8, cols] = halo_ref[tile].astype(F32)
+        for b in range(BLOCKS):
+            at = 8 + b * BLOCK
+            padded[at : at + BLOCK, cols] = block_of(rows_ref, b, tile * 16).astype(F32)
+
+
+def weigh(weighted, act_ref, decay_ref, step_ref, end_decay, member_of):
+    lane = iota((BLOCK, 128), 1)
+    for b in range(BLOCKS):
+        rows = slice(b * BLOCK, (b + 1) * BLOCK)
+        gap = jnp.minimum(end_decay - decay_ref[rows, :], 0.0)
+        weights = jnp.where(member_of(b), jnp.exp(gap), 0.0) * step_ref[rows, :]
+        for tile in range(2):
+            cols = slice(tile * 128, (tile + 1) * 128)
+            weighted[rows, cols] = (spread(weights, tile, lane) * act_ref[rows, cols].astype(F32)).astype(BF16)
+
+
+def send_state(message_ref, at, weighted, act_ref):
+    for tile in range(2):
+        state = dot(weighted[:, tile * 128 : (tile + 1) * 128], act_ref[:, WIDTH : WIDTH + STATE], ((0,), (0,)))
+        message_ref[tile * 8 : (tile + 1) * 8, at : at + 16, :] = state.astype(BF16).reshape(8, 16, 128)
+
+
+def send_ends(slots, first, length_ref, rows_ref, act_ref, decay_ref, step_ref, message_ref, padded, weighted):
+    starts, ends = bounds(length_ref)
+    before = segment_at(first - 1, starts)
+    last = segment_at(first + ROW - 1, starts)
+    sub = iota((BLOCK, 128), 0)
+    row = iota((1, 128), 1)
+    index = iota((8, 128), 0)
+    found = [[jnp.int32(BIG), jnp.int32(-2), jnp.int32(0)] for _ in range(slots)]
+    count = jnp.int32(0)
+    for p in range(PROMPTS):
+        here = (ends[p] >= first) & (ends[p] < first + ROW)
+        for m in range(slots):
+            mine = here & (count == m)
+            for at, value in enumerate((ends[p], jnp.int32(p), starts[p])):
+                found[m][at] = jnp.where(mine, value, found[m][at])
+        count = count + here.astype(jnp.int32)
+    carry = decay_ref[ROW - 1 : ROW, :]
+    small = laid_out(jnp.where(last == before, jnp.exp(carry), 0.0), 0, row)
+    edges = []
+    for m in range(slots):
+        end, prompt, start = found[m]
+        some = end < BIG
+        local = jnp.where(some, end - first, 0)
+        end_decay = decay_ref[pl.ds(local, 1), :]
+        at = 16 * (m + 1)
+
+        @pl.when(some)
+        def _(end=end, start=start, end_decay=end_decay, at=at):
+            def member_of(b):
+                position = sub + (first + b * BLOCK)
+                return (position >= start) & (position <= end)
+
+            weigh(weighted, act_ref, decay_ref, step_ref, end_decay, member_of)
+            send_state(message_ref, at, weighted, act_ref)
+
+        @pl.when(jnp.logical_not(some))
+        def _(at=at):
+            message_ref[:, at : at + 16, :] = jnp.zeros((ZS, 16, 128), BF16)
+
+        carried = jnp.where(some & (prompt == before), jnp.exp(end_decay), 0.0)
+        small = small + laid_out(carried, 12 * (m + 1), row)
+        edge = []
+        for k in range(3):
+            valid = some & (end - 2 + k >= start)
+            edge.append(jnp.where(valid, padded[pl.ds(8 + local - 2 + k, 1), :], 0.0))
+        edges.append(edge)
+    for k in range(XS):
+        request = rows_ref[k * 8, STEPS:GATE, :].astype(F32)[0:1, :]
+        small = small + jnp.where(row == REQUEST + k, pltpu.roll(request, REQUEST - 4 + k, 1), 0.0)
+    block = jnp.where(index == slots, small, jnp.zeros((8, 128), F32))
+    tail = 16 * (slots + 1)
+    for k in range(ZS):
+        value = block
+        if k < 12:
+            for m in range(slots):
+                piece = edges[m][k // 4][:, (k % 4) * 128 : (k % 4 + 1) * 128]
+                value = jnp.where(index == m, piece, value)
+        message_ref[k, tail : tail + 8, :] = value.astype(BF16)
 
 
 def front_kernel(
@@ -95,27 +197,15 @@
 ):
     first = place_ref[0] * ROW
     quarter = place_ref[1]
-    starts, ends = bounds(length_ref)
-    lane = iota((BLOCK, 128), 1)
+    starts, _ = bounds(length_ref)
     sub = iota((BLOCK, 128), 0)
-    before = segment_at(first - 1, starts)
     last = segment_at(first + ROW - 1, starts)
-    found = [[jnp.int32(BIG), jnp.int32(-2), jnp.int32(0)] for _ in range(SLOTS)]
-    count = jnp.int32(0)
-    for p in range(PROMPTS):
-        here = (ends[p] >= first) & (ends[p] < first + ROW)
-        for m in range(SLOTS):
-            mine = here & (count == m)
-            for at, value in enumerate((ends[p], jnp.int32(p), starts[p])):
-                found[m][at] = jnp.where(mine, value, found[m][at])
-        count = count + here.astype(jnp.int32)
     heads = pltpu.roll(head_ref[...], place_ref[2], 1)
     bias = heads[0:1, :]
     scale = -jnp.exp(heads[1:2, :])
-    lower = (sub >= lane).astype(F32)
-
-    padded[0:8, :] = halo_ref[...].astype(F32)
-    padded[8:, :] = rows_ref[:, 0:WIDE].astype(F32)
+    lower = (sub >= iota((BLOCK, 128), 1)).astype(F32)
+
+    padded_rows(rows_ref, halo_ref, padded)
     carry = jnp.zeros((1, 128), F32)
     for b in range(BLOCKS):
         rows = slice(b * BLOCK, (b + 1) * BLOCK)
@@ -136,83 +226,53 @@
                 at = b * BLOCK + 5 + k
                 total = total + jnp.where(inside[k], padded[at : at + BLOCK, cols], 0.0) * taps
             act_ref[rows, cols] = (total * jax.nn.sigmoid(total)).astype(BF16)
-        step = jax.nn.softplus(rows_ref[rows, WIDE:GATE].astype(F32) + bias)
+        step = jax.nn.softplus(steps_of(rows_ref, b) + bias)
         decay = dot(lower, step * scale, ((1,), (0,)), lax.Precision.HIGHEST) + carry
         carry = decay[BLOCK - 1 : BLOCK, :]
         step_ref[rows, :] = step
         decay_ref[rows, :] = decay
-    row = iota((1, 128), 1)
-    index = iota((8, 128), 0)
-    small = laid_out(jnp.where(last == before, jnp.exp(carry), 0.0), 0, row)
-    edges = []
-    for m in range(-1, SLOTS):
-        if m < 0:
-            end_decay = carry
-        else:
-            end, prompt, start = found[m]
-            some = end < BIG
-            local = jnp.where(some, end - first, 0)
-            end_decay = decay_ref[pl.ds(local, 1), :]
-        for b in range(BLOCKS):
-            rows = slice(b * BLOCK, (b + 1) * BLOCK)
-            position = sub + (first + b * BLOCK)
-            if m < 0:
-                member = segment_at(position, starts) == last
-            else:
-                member = some & (position >= start) & (position <= end)
-            gap = jnp.minimum(end_decay - decay_ref[rows, :], 0.0)
-            weights = jnp.where(member, jnp.exp(gap), 0.0) * step_ref[rows, :]
-            for tile in range(2):
-                cols = slice(tile * 128, (tile + 1) * 128)
-                weighted[rows, cols] = (spread(weights, tile, lane) * act_ref[rows, cols].astype(F32)).astype(BF16)
-        at = 16 * (m + 1)
-        for tile in range(2):
-            state = dot(weighted[:, tile * 128 : (tile + 1) * 128], act_ref[:, WIDTH : WIDTH + STATE], ((0,), (0,)))
-            message_ref[tile * 8 : (tile + 1) * 8, at : at + 16, :] = state.astype(BF16).reshape(8, 16, 128)
-        if m < 0:
-            continue
-        carried = jnp.where(some & (prompt == before), jnp.exp(end_decay), 0.0)
-        small = small + laid_out(carried, 12 * (m + 1), row)
-        edge = []
-        for k in range(3):
-            valid = some & (end - 2 + k >= start)
-            edge.append(jnp.where(valid, padded[pl.ds(8 + local - 2 + k, 1), :], 0.0))
-        edges.append(edge)
-    for k in range(XS):
-        request = rows_ref[k * BLOCK : k * BLOCK + 8, WIDE:GATE].astype(F32)[0:1, :]
-        small = small + jnp.where(row == 64 + k, pltpu.roll(request, 60 + k, 1), 0.0)
-    block = jnp.where(index == SLOTS, small, jnp.zeros((8, 128), F32))
-    for k in range(ZS):
-        value = block
-        if k < 12:
-            for m in range(SLOTS):
-                piece = edges[m][k // 4][:, (k % 4) * 128 : (k % 4 + 1) * 128]
-                value = jnp.where(index == m, piece, value)
-        message_ref[k, TAIL : TAIL + 8, :] = value.astype(BF16)
-
-
-def scan_kernel(place_ref, length_ref, got_ref, extra_ref, out_ref, small, states, finals):
+
+    def member_of(b):
+        return segment_at(sub + (first + b * BLOCK), starts) == last
+
+    weigh(weighted, act_ref, decay_ref, step_ref, carry, member_of)
+    send_state(message_ref, 0, weighted, act_ref)
+    send_ends(FEW, first, length_ref, rows_ref, act_ref, decay_ref, step_ref, message_ref, padded, weighted)
+
+
+def many_kernel(
+    place_ref, length_ref, rows_ref, halo_ref, act_ref, decay_ref, step_ref, few_ref, message_ref, padded, weighted,
+):
+    padded_rows(rows_ref, halo_ref, padded)
+    message_ref[:, 0:16, :] = few_ref[:, 0:16, :]
+    send_ends(
+        PROMPTS, place_ref[0] * ROW, length_ref, rows_ref, act_ref, decay_ref, step_ref, message_ref, padded, weighted
+    )
+
+
+def scan_kernel(slots, place_ref, length_ref, got_ref, out_ref, small, states, finals):
     _, ends = bounds(length_ref)
     head = place_ref[0] // 4
-    one = [picks(head, 12 * m) for m in range(SLOTS + 1)]
-    one = one + [(iota((128, 128), 0) == 64 + k).astype(BF16) for k in range(XS)]
-    small[...] = dot(got_ref[:, TAIL : TAIL + 8, :].reshape(ZS * 8, 128), jnp.concatenate(one, axis=1), ((1,), (0,)))
+    tail_at = 16 * (slots + 1)
+    one = [picks(head, 12 * m) for m in range(slots + 1)]
+    one = one + [(iota((128, 128), 0) == REQUEST + k).astype(BF16) for k in range(XS)]
+    small[...] = dot(got_ref[:, tail_at : tail_at + 8, :].reshape(ZS * 8, 128), jnp.concatenate(one, axis=1), ((1,), (0,)))
     state = jnp.zeros((16, 128), F32)
     for j in range(ZS):
         states[j] = state
         out_ref[j, 0:16, :] = state.astype(BF16)
-        at = 8 * j + SLOTS
+        at = 8 * j + slots
         state = small[at : at + 1, 0:128] * state + got_ref[j, 0:16, :].astype(F32)
     for p in range(PROMPTS):
         z = ends[p] // ROW
         rank = jnp.int32(0)
         for other in range(p):
             rank = rank + (ends[other] // ROW == z).astype(jnp.int32)
-        value = extra_ref[p]
+        value = jnp.zeros((24, 128), F32)
         state = states[z]
-        tail = got_ref[z, TAIL : TAIL + 8, :].astype(F32)
-        factor = small[pl.ds(8 * z + SLOTS, 1), 128 : 128 * (SLOTS + 1)]
-        for m in range(SLOTS):
+        tail = got_ref[z, tail_at : tail_at + 8, :].astype(F32)
+        factor = small[pl.ds(8 * z + slots, 1), 128 : 128 * (slots + 1)]
+        for m in range(slots):
             own = got_ref[z, 16 * m + 16 : 16 * m + 32, :].astype(F32) + factor[:, 128 * m : 128 * (m + 1)] * state
             edge = jnp.broadcast_to(tail[m : m + 1, :], (8, 128))
             value = jnp.where(rank == m, jnp.concatenate([own, edge], axis=0), value)
@@ -221,8 +281,8 @@
     for z in range(ZS):
         edges = jnp.zeros((8, 128), F32)
         for k in range(XS):
-            at = 128 * (SLOTS + 1 + k)
-            request = small[8 * z + SLOTS : 8 * z + SLOTS + 1, at : at + 128]
+            at = 128 * (slots + 1 + k)
+            request = small[8 * z + slots : 8 * z + slots + 1, at : at + 128]
             value = finals[0]
             for p in range(1, PROMPTS):
                 value = jnp.where(request == float(p), finals[p], value)
@@ -276,7 +336,7 @@
             if b:
                 across = dot(read.astype(F32), carried[tile], ((1,), (1,)), lax.Precision.HIGHEST)
                 value = value + spread(inflow, tile, lane) * across
-            gate = rows_ref[rows, GATE + tile * 128 : GATE + (tile + 1) * 128].astype(F32)
+            gate = block_of(rows_ref, b, GATE + tile * 16).astype(F32)
             gate = gate * jax.nn.sigmoid(gate)
             own_ref[rows, cols] = value * gate
             in_ref[rows, cols] = spread(inflow_row, tile, lane) * gate
@@ -346,56 +406,6 @@
         scratch_shapes=list(scratch),
         compiler_params=pltpu.CompilerParams(vmem_limit_bytes=limit),
     )(*ins)
-
-
-def exchange(sent, place):
-    k = jnp.arange(ZS, dtype=jnp.int32)
-    held = sent[(k + place) % ZS]
-    for shift in (1, 2, 4, 8):
-        moved = lax.ppermute(held, "z", [(source, (source + shift) % ZS) for source in range(ZS)])
-        held = jnp.where(((k & shift) != 0)[:, None, None], moved, held)
-    return held[(place - k) % ZS]
-
-
-def later_ends(place, prompt_lengths, rows, halo, act, decay, step):
-    ends = jnp.cumsum(prompt_lengths) - 1
-    starts = ends + 1 - prompt_lengths
-    ids = jnp.arange(PROMPTS, dtype=jnp.int32)
-    z = ends // ROW
-    rank = jnp.sum((z[None, :] == z[:, None]) & (ids[None, :] < ids[:, None]), axis=1)
-    position = place * ROW + jnp.arange(ROW, dtype=jnp.int32)
-
-    def step_of(carry):
-        k, extra = carry
-        mine = (z == place) & (rank == k)
-        some = jnp.any(mine)
-        end = jnp.sum(jnp.where(mine, ends, 0))
-        start = jnp.sum(jnp.where(mine, starts, 0))
-        member = some & (position >= start) & (position <= end)
-        end_decay = jnp.sum(jnp.where((position == end)[:, None], decay, 0.0), axis=0, keepdims=True)
-        weights = jnp.where(member[:, None], jnp.exp(jnp.minimum(end_decay - decay, 0.0)), 0.0) * step
-        weights = weights[:, : WIDTH // HEAD]
-        x = act[:, :WIDTH].reshape(ROW, -1, HEAD).astype(F32)
-        weighted = (weights[:, :, None] * x).reshape(ROW, WIDTH).astype(BF16)
-        own = dot(weighted, act[:, WIDTH : WIDTH + STATE], ((0,), (0,))).astype(BF16)
-        padded = jnp.concatenate([halo, rows[:, :WIDE]], axis=0)
-        wanted = end - 2 + jnp.arange(3, dtype=jnp.int32)
-        onehot = (jnp.arange(ROW + 8)[None, :] + (place * ROW - 8) == wanted[:, None]) & some
-        onehot = onehot & (wanted >= start)[:, None]
-        edge = dot(onehot.astype(BF16), padded, ((1,), (0,))).astype(BF16)
-        edge = jnp.pad(edge.reshape(12, 1, 128), ((0, 4), (0, 7), (0, 0)))
-        sent = jnp.concatenate([own.reshape(ZS, 16, 128), edge], axis=1)
-        taken = exchange(sent, place)[z].astype(F32)
-        taken = jnp.concatenate([taken[:, :16], jnp.broadcast_to(taken[:, 16:17], (PROMPTS, 8, 128))], axis=1)
-        return k + 1, jnp.where((rank == k)[:, None, None], taken, extra)
-
-    most = jnp.max(rank)
-    none = jnp.zeros((PROMPTS, 24, 128), F32)
-    return lax.cond(
-        most >= SLOTS,
-        lambda: lax.while_loop(lambda carry: carry[0] <= most, step_of, (jnp.full_like(most, SLOTS), none))[1],
-        lambda: none,
-    )
 
 
 def per_device(
@@ -422,17 +432,17 @@
     packed = call(
         pack_kernel,
         (request_prompt, head_inputs, state_proj, step_raw, gate_inputs),
-        shape((XS * HS, 16, SENT), BF16),
+        shape((XS * HS, SENT, 128), BF16),
         scalars=1,
         limit=None,
     )
-    rows = lax.all_to_all(packed, ("x", "head"), 0, 0).reshape(ROW, SENT)
-    halo = lax.ppermute(rows[ROW - 8 :, :WIDE], "z", [(source, source + 1) for source in range(ZS - 1)])
+    rows = lax.all_to_all(packed, ("x", "head"), 0, 0)
+    halo = lax.ppermute(rows[-1, :STEPS].reshape(WIDE // 128, 16, 128)[:, 8:], "z", [(source, source + 1) for source in range(ZS - 1)])
     message, act, decay, step = call(
         front_kernel,
         (places, prompt_lengths, rows, halo, filter_inner, filter_state, heads_in),
         (
-            shape((ZS, TAIL + 8, 128), BF16),
+            shape((ZS, 16 * (FEW + 1) + 8, 128), BF16),
             shape((ROW, WIDE), BF16),
             shape((ROW, 128), F32),
             shape((ROW, 128), F32),
@@ -440,27 +450,43 @@
         (pltpu.VMEM((ROW + 8, WIDE), F32), pltpu.VMEM((ROW, WIDTH), BF16)),
         scalars=2,
     )
-    got = lax.all_to_all(message, "z", 0, 0)
-    own, inflow = call(
-        within_kernel,
-        (places, prompt_lengths, act, decay, step, rows, skip),
-        (shape((ROW, WIDTH), F32), shape((ROW, WIDTH), F32)),
-        (pltpu.VMEM((2, 128, 128), F32),),
-        scalars=2,
-    )
-    own, rows, halo, act, decay, step = lax.optimization_barrier((own, rows, halo, act, decay, step))
-    extra = later_ends(place, prompt_lengths, rows, halo, act, decay, step)
-    answer = call(
-        scan_kernel,
-        (places, prompt_lengths, got, extra),
-        shape((ZS, 88, 128), BF16),
-        (
-            pltpu.VMEM((ZS * 8, 128 * (SLOTS + 1 + XS)), F32),
-            pltpu.VMEM((ZS, 16, 128), F32),
-            pltpu.VMEM((PROMPTS, 24, 128), F32),
-        ),
-        scalars=2,
-    )
+    scratch = (pltpu.VMEM((ROW + 8, WIDE), F32), pltpu.VMEM((ROW, WIDTH), BF16))
+
+    def onward(slots, message):
+        got = lax.all_to_all(message, "z", 0, 0)
+        own, inflow = call(
+            within_kernel,
+            (places, prompt_lengths, act, decay, step, rows, skip),
+            (shape((ROW, WIDTH), F32), shape((ROW, WIDTH), F32)),
+            (pltpu.VMEM((2, 128, 128), F32),),
+            scalars=2,
+        )
+        answer = call(
+            functools.partial(scan_kernel, slots),
+            (places, prompt_lengths, got),
+            shape((ZS, 88, 128), BF16),
+            (
+                pltpu.VMEM((ZS * 8, 128 * (slots + 1 + XS)), F32),
+                pltpu.VMEM((ZS, 16, 128), F32),
+                pltpu.VMEM((PROMPTS, 24, 128), F32),
+            ),
+            scalars=2,
+        )
+        return answer, own, inflow
+
+    def many():
+        full = call(
+            many_kernel,
+            (places, prompt_lengths, rows, halo, act, decay, step, message),
+            shape((ZS, 16 * (PROMPTS + 1) + 8, 128), BF16),
+            scratch,
+            scalars=2,
+        )
+        return onward(PROMPTS, full)
+
+    z = (jnp.cumsum(prompt_lengths) - 1) // ROW
+    most = jnp.max(jnp.sum((z[None, :] == z[:, None]).astype(jnp.int32), axis=1))
+    answer, own, inflow = lax.cond(most > FEW, many, lambda: onward(FEW, message))
     back = lax.all_to_all(answer, "z", 0, 0)
     shared = call(across_kernel, (act, own, inflow, back), shape((XS, 528, 128), BF16))
     shared = lax.all_to_all(shared, "x", 0, 0)

time: 114 us -> 109 us (0.956)
  waiting for transfers between devices: 28.7 us -> 25 us
  local copies, waits for them, and re-layouts: 0.84 us -> 2.1 us
    all_to_all x2, waiting for transfers between devices: 27.5 us -> 25 us  [the longest x1 14 us: onward(): got = lax.all_to_all(message, 'z', 0, 0)]
    unnamed x14 -> x16, local copies, waits for them, and re-layouts: 0.03 us -> 1.95 us
    ppermute x1, waiting for transfers between devices: 1.27 us -> 0.01 us  [per_device(): lax.ppermute(rows[-1, :STEPS].reshape(WIDE // 128, 16, 128)[:, 8:], 'z',...]
  transfers between devices with their start and end apart: 3 -> 3, of which waited for: 3 -> 2; matrix products, arithmetic and copies ran while one was open for 2% -> 1% of each run, Pallas kernels for 2% -> 3%
where the time goes in v3:
time: 109 us; the launch traced here: 108 us
  blocking collectives  38.7 us (36%)
  starting transfers between devices  27.5 us (25%)
  waiting for transfers between devices  25 us (23%)
  Pallas kernels  11.5 us (11%)
  local copies, waits for them, and re-layouts  2.1 us (2%)
  between operations  2.04 us (2%)
  other arithmetic  1.09 us (1%)
    all_to_all x1, blocking collectives, per_device(): back = lax.all_to_all(answer, 'z', 0, 0)  27.4 us
    all_to_all x1, starting transfers between devices, onward(): got = lax.all_to_all(message, 'z', 0, 0)  16 us
    all_to_all x1, waiting for transfers between devices, onward(): got = lax.all_to_all(message, 'z', 0, 0)  14 us
    pallas_call x6, Pallas kernels, call(): pl.pallas_call(kernel, out_shape=outs, in_specs=[smem] * scalars + [vmem]...  11.5 us
    all_to_all x1, blocking collectives, per_device(): shared = lax.all_to_all(shared, 'x', 0, 0)  11.3 us
    all_to_all x1, waiting for transfers between devices, per_device(): rows = lax.all_to_all(packed, ('x', 'head'), 0, 0)  11 us
    all_to_all x1, starting transfers between devices, per_device(): rows = lax.all_to_all(packed, ('x', 'head'), 0, 0)  9.49 us
  transfers between devices with their start and end apart: 3, of which 2 were waited for; matrix products, arithmetic and copies ran while one was open for 1% of the time, Pallas kernels for 3%

profile of v3, /device:TPU:2, one launch (start us, length us, event | category | flops | bytes accessed | tf_op | source)
XLA Modules:
  0.0 108.2 jit_solution(841281102215077033)
XLA Ops:
  1.3 2.1 %shard_map.147 = bf16[32,104,128]{2,1,0:T(8,128)(2,1)} custom-call(s32[1,1]{1,0:T(1,128)S(6)} %copy.22.request_ref, bf16[16,8192]{1,0:T(8,128)(2,1)} %inner_ref.1, bf16[16,2048]{1,0:T(8,128)(2,1)} %proj_ref.1, bf16[16,128]{1,0:T(8,128)(2,1)} %step_ref.1, bf16[16,8192]{1,0:T(8,128)(2,1)} %gate_ref.1), custom_call_target="tpu_custom_call" | custom-call | tf_op jit(solution)/shard_map/pallas_call | solution.py:401
  3.4 9.5 %all-to-all-start.2 = ((bf16[32,104,128]{2,1,0:T(8,128)(2,1)}), bf16[32,104,128]{2,1,0:T(8,128)(2,1)S(1)}, u32[]{:S(2)}, u32[]{:S(2)}) async-start(bf16[32,104,128]{2,1,0:T(8,128)(2,1)} %shard_map.147), calls=%async_computation.2 | async-start | bytes 1703936 | tf_op jit(solution)/shard_map/all_to_all | solution.py:439
  12.9 0.6 copy-done.4
  13.6 0.2 reduce-window.7
  13.8 0.7 copy-done.5
  14.4 0.0 copy-done.6
  14.5 0.2 convert_reduce_fusion
  14.6 11.0 %all-to-all-done.2.rows_ref = bf16[32,104,128]{2,1,0:T(8,128)(2,1)S(1)} async-done(((bf16[32,104,128]{2,1,0:T(8,128)(2,1)}), bf16[32,104,128]{2,1,0:T(8,128)(2,1)S(1)}, u32[]{:S(2)}, u32[]{:S(2)}) %all-to-all-start.2) | async-done | bytes 852000 | tf_op jit(solution)/shard_map/all_to_all | solution.py:439
  25.7 2.0 %collective-permute-start = (bf16[4,8,128]{2,1,0:T(8,128)(2,1)S(1)}, bf16[4,8,128]{2,1,0:T(8,128)(2,1)S(1)}, u32[]{:S(2)}, u32[]{:S(2)}) collective-permute-start(bf16[4,8,128]{2,1,0:T(8,128)(2,1)S(1)} %slice.9), channel_id=1, source_target_pairs={{0,32},{32,64},{64,96},{96,128},{128,160},{160,192},{192,224},{224... | collective-permute-start | bytes 24584 | tf_op jit(solution)/shard_map/ppermute | solution.py:440
  27.7 0.1 pad_add_fusion.place_ref
  27.8 0.6 reduce_max.9
  29.1 0.1 broadcast_in_dim.8
  29.2 0.1 broadcast_in_dim_reshape.3
  29.2 0.6 copy-done.1
  29.8 3.7 %shard_map.148 = (bf16[16,56,128]{2,1,0:T(8,128)(2,1)}, bf16[512,512]{1,0:T(8,128)(2,1)S(1)}, f32[512,128]{1,0:T(8,128)S(1)}, f32[512,128]{1,0:T(8,128)S(1)}) custom-call(s32[3]{0:T(128)S(1)} %pad_add_fusion.place_ref, s32[7]{0:T(128)S(1)} %copy-done.4, bf16[32,104,128]{2,1,0:T(8,128)(2,1)S(1)} %all-to-all-done.2.rows_ref, ...), custom_call_target="tpu_custom_call" | custom-call | tf_op jit(solution)/shard_map/pallas_call | solution.py:401
  33.5 34.5 %conditional.1 = (bf16[16,88,128]{2,1,0:T(8,128)(2,1)S(1)}, f32[512,256]{1,0:T(8,128)S(1)}, f32[512,256]{1,0:T(8,128)}) conditional(s32[]{:T(128)} %convert_element_type.9, (bf16[16,56,128]{2,1,0:T(8,128)(2,1)}, s32[3]{0:T(128)S(1)}, s32[7]{0:T(128)S(1)}, bf16[512,512]{1,0:T(8,128)(2,1)S(1)}, f32[512,128]{1,0:T(8,128)S(1)}, ...), branch_computations={%region_3.4_spmd, %region_4.5_spmd} | conditional | bytes 1671224 | solution.py:489
  33.5 16.0 %all-to-all-start = ((bf16[16,56,128]{2,1,0:T(8,128)(2,1)}), bf16[16,56,128]{2,1,0:T(8,128)(2,1)S(1)}, u32[]{:S(2)}, u32[]{:S(2)}) async-start(bf16[16,56,128]{2,1,0:T(8,128)(2,1)} %get-tuple-element.36), calls=%async_computation | async-start | bytes 458752 | tf_op jit(solution)/shard_map/cond/branch_0_fun/all_to_all | solution.py:456
  49.5 3.2 %branch_0_fun.3 = (f32[512,256]{1,0:T(8,128)S(1)}, f32[512,256]{1,0:T(8,128)}) custom-call(s32[3]{0:T(128)S(1)} %get-tuple-element.34.place_ref, s32[7]{0:T(128)S(1)} %get-tuple-element.35.length_ref, bf16[512,512]{1,0:T(8,128)(2,1)S(1)} %get-tuple-element.37.act_ref, f32[512,128]{1,0:T(8,128)S(1)} %get-tuple-element.38.decay_ref, ...), custom_call_target="tpu_custom_call" | custom-call | tf_op jit(solution)/shard_map/cond/branch_0_fun/pallas_call | solution.py:401
  52.7 14.0 %all-to-all-done.got_ref = bf16[16,56,128]{2,1,0:T(8,128)(2,1)S(1)} async-done(((bf16[16,56,128]{2,1,0:T(8,128)(2,1)}), bf16[16,56,128]{2,1,0:T(8,128)(2,1)S(1)}, u32[]{:S(2)}, u32[]{:S(2)}) %all-to-all-start) | async-done | bytes 229408 | tf_op jit(solution)/shard_map/cond/branch_0_fun/all_to_all | solution.py:456
  66.7 1.1 branch_0_fun.2
  68.0 27.4 %all_to_all.23.got_ref = bf16[16,88,128]{2,1,0:T(8,128)(2,1)S(1)} all-to-all(bf16[16,88,128]{2,1,0:T(8,128)(2,1)S(1)} %get-tuple-element.76), channel_id=1, replica_groups=mesh['z'=16,'x'=4,'head'=8] {'z'}, dimensions={0} | all-to-all | bytes 720896 | tf_op jit(solution)/shard_map/all_to_all | solution.py:490
  95.5 0.3 shard_map.149
  95.8 11.3 %all_to_all.24.got_ref = bf16[4,528,128]{2,1,0:T(8,128)(2,1)S(1)} all-to-all(bf16[4,528,128]{2,1,0:T(8,128)(2,1)S(1)} %shard_map.149), channel_id=1, replica_groups=mesh['z'=16,'x'=4,'head'=8] {'x'}, dimensions={0} | all-to-all | bytes 1081344 | tf_op jit(solution)/shard_map/all_to_all | solution.py:492
  107.1 1.1 shard_map.150
  (17 shorter events, 0.1 us)
Async XLA Ops:
  3.4 22.2 %all-to-all-start.2 = ((bf16[32,104,128]{2,1,0:T(8,128)(2,1)}), bf16[32,104,128]{2,1,0:T(8,128)(2,1)S(1)}, u32[]{:S(2)}, u32[]{:S(2)}) async-start(bf16[32,104,128]{2,1,0:T(8,128)(2,1)} %shard_map.147), calls=%async_computation.2 | async-start | bytes 1703936 | tf_op jit(solution)/shard_map/all_to_all | solution.py:439
  12.9 0.7 copy-start.4
  13.8 0.7 copy-start.5
  13.8 0.7 copy-start.6
  25.7 3.4 %copy-start.7 = (f32[16]{0:T(128)S(1)}, f32[16]{0:T(128)}, u32[]{:S(2)}) copy-start(f32[16]{0:T(128)} %param.20) | copy-start | bytes 196
  25.7 3.6 %collective-permute-start = (bf16[4,8,128]{2,1,0:T(8,128)(2,1)S(1)}, bf16[4,8,128]{2,1,0:T(8,128)(2,1)S(1)}, u32[]{:S(2)}, u32[]{:S(2)}) collective-permute-start(bf16[4,8,128]{2,1,0:T(8,128)(2,1)S(1)} %slice.9), channel_id=1, source_target_pairs={{0,32},{32,64},{64,96},{96,128},{128,160},{160,192},{192,224},{224... | collective-permute-start | bytes 24584 | tf_op jit(solution)/shard_map/ppermute | solution.py:440
  27.7 1.5 %copy-start = (f32[4,1024]{1,0:T(4,128)S(1)}, f32[4,1024]{1,0:T(4,128)}, u32[]{:S(2)}) copy-start(f32[4,1024]{1,0:T(4,128)} %inner_taps_ref.1) | copy-start | bytes 49156
  29.2 0.7 copy-start.1
  33.5 33.2 %all-to-all-start = ((bf16[16,56,128]{2,1,0:T(8,128)(2,1)}), bf16[16,56,128]{2,1,0:T(8,128)(2,1)S(1)}, u32[]{:S(2)}, u32[]{:S(2)}) async-start(bf16[16,56,128]{2,1,0:T(8,128)(2,1)} %get-tuple-element.36), calls=%async_computation | async-start | bytes 458752 | tf_op jit(solution)/shard_map/cond/branch_0_fun/all_to_all | solution.py:456
  68.0 27.5 %copy-start.3 = (f32[512,256]{1,0:T(8,128)S(1)}, f32[512,256]{1,0:T(8,128)}, u32[]{:S(2)}) copy-start(f32[512,256]{1,0:T(8,128)} %get-tuple-element.75.in_ref) | copy-start | bytes 1572868
  95.8 11.3 %copy-start.2 = (f32[1024]{0:T(1024)S(1)}, f32[1024]{0:T(1024)}, u32[]{:S(2)}) copy-start(f32[1024]{0:T(1024)} %param.23) | copy-start | bytes 12292

commit v4 on v3

--- a/solution.py
+++ b/solution.py
@@ -18,7 +18,7 @@
 BLOCKS = ROW // BLOCK
 WIDTH = 256
 WIDE = 512
-STEPS, GATE, SENT = 64, 72, 104
+STEPS, SENT = 64, 72
 FEW = 2
 REQUEST = 96
 BIG = 1 << 30
@@ -74,7 +74,7 @@
     return ((lane == at + head) | (lane == at + 4 + head) | (lane == at + 8 + head)).astype(BF16)
 
 
-def pack_kernel(request_ref, inner_ref, proj_ref, step_ref, gate_ref, out_ref):
+def pack_kernel(request_ref, inner_ref, proj_ref, step_ref, out_ref):
     step = step_ref[...].astype(F32)
     lane = iota((8, 128), 1)
     request = request_ref[0, 0].astype(F32)
@@ -84,7 +84,6 @@
             for c in range(2):
                 col = h * 1024 + q * WIDTH + c * 128
                 out_ref[at, c * 16 : c * 16 + 16, :] = inner_ref[:, col : col + 128]
-                out_ref[at, GATE + c * 16 : GATE + c * 16 + 16, :] = gate_ref[:, col : col + 128]
                 col = h * 256 + c * 128
                 out_ref[at, 32 + c * 16 : 48 + c * 16, :] = proj_ref[:, col : col + 128]
             shift = (128 - (16 * h + 4 * q)) % 128
@@ -92,7 +91,12 @@
             shift = (shift + 64) % 128
             late = pltpu.roll(step[8:16], shift, 1) if shift else step[8:16]
             own = jnp.where(lane < 64, early, late)
-            out_ref[at, STEPS:GATE, :] = jnp.where(lane == 4, request, own).astype(BF16)
+            out_ref[at, STEPS:SENT, :] = jnp.where(lane == 4, request, own).astype(BF16)
+
+
+def gate_kernel(gate_ref, out_ref):
+    for h in range(HS):
+        out_ref[h] = gate_ref[:, h * 1024 : (h + 1) * 1024]
 
 
 def block_of(rows_ref, b, row):
@@ -100,7 +104,7 @@
 
 
 def steps_of(rows_ref, b):
-    early = rows_ref[8 * b : 8 * b + 8, STEPS:GATE, :].astype(F32)
+    early = rows_ref[8 * b : 8 * b + 8, STEPS:SENT, :].astype(F32)
     late = pltpu.roll(early.reshape(64, 128), 64, 1).reshape(8, 8, 128)
     return jnp.concatenate([early, late], axis=1).reshape(BLOCK, 128)
 
@@ -178,7 +182,7 @@
             edge.append(jnp.where(valid, padded[pl.ds(8 + local - 2 + k, 1), :], 0.0))
         edges.append(edge)
     for k in range(XS):
-        request = rows_ref[k * 8, STEPS:GATE, :].astype(F32)[0:1, :]
+        request = rows_ref[k * 8, STEPS:SENT, :].astype(F32)[0:1, :]
         small = small + jnp.where(row == REQUEST + k, pltpu.roll(request, REQUEST - 4 + k, 1), 0.0)
     block = jnp.where(index == slots, small, jnp.zeros((8, 128), F32))
     tail = 16 * (slots + 1)
@@ -292,7 +296,7 @@
 
 
 def within_kernel(
-    place_ref, length_ref, act_ref, decay_ref, step_ref, rows_ref, skip_ref, own_ref, in_ref, carried,
+    place_ref, length_ref, act_ref, decay_ref, step_ref, skip_ref, own_ref, in_ref, carried,
 ):
     first = place_ref[0] * ROW
     quarter = place_ref[1]
@@ -336,10 +340,8 @@
             if b:
                 across = dot(read.astype(F32), carried[tile], ((1,), (1,)), lax.Precision.HIGHEST)
                 value = value + spread(inflow, tile, lane) * across
-            gate = block_of(rows_ref, b, GATE + tile * 16).astype(F32)
-            gate = gate * jax.nn.sigmoid(gate)
-            own_ref[rows, cols] = value * gate
-            in_ref[rows, cols] = spread(inflow_row, tile, lane) * gate
+            own_ref[rows, cols] = value
+            in_ref[rows, cols] = spread(inflow_row, tile, lane)
             if b < BLOCKS - 1:
                 weighted = (spread(tail, tile, lane) * x.astype(F32)).astype(BF16)
                 state = dot(weighted, write, ((0,), (0,)))
@@ -372,19 +374,21 @@
         out_ref[k, 512:528, :] = edges[k].astype(BF16)
 
 
-def last_kernel(got_ref, gain_ref, hidden_ref, final_ref, inner_ref, proj_ref):
+def last_kernel(got_ref, gate_ref, gain_ref, hidden_ref, final_ref, inner_ref, proj_ref, gated):
     total = jnp.zeros((BLOCK, 128), F32)
     for q in range(XS):
         for tile in range(2):
-            value = got_ref[q, tile * BLOCK : (tile + 1) * BLOCK, :].astype(F32)
+            cols = slice(q * WIDTH + tile * 128, q * WIDTH + (tile + 1) * 128)
+            gate = gate_ref[:, cols].astype(F32)
+            value = got_ref[q, tile * BLOCK : (tile + 1) * BLOCK, :].astype(F32) * (gate * jax.nn.sigmoid(gate))
+            gated[:, cols] = value
             total = total + value * value
     mean = jnp.sum(total, axis=1, keepdims=True) * (1.0 / (XS * WIDTH))
     inverse = lax.rsqrt(mean + EPSILON)
     for q in range(XS):
         for tile in range(2):
             cols = slice(q * WIDTH + tile * 128, q * WIDTH + (tile + 1) * 128)
-            value = got_ref[q, tile * BLOCK : (tile + 1) * BLOCK, :].astype(F32)
-            hidden_ref[:, cols] = ((value * inverse) * gain_ref[:, cols]).astype(BF16)
+            hidden_ref[:, cols] = ((gated[:, cols] * inverse) * gain_ref[:, cols]).astype(BF16)
         final_ref[q * WIDTH : (q + 1) * WIDTH, :] = got_ref[q, 256:512, :].astype(F32)
         edges = got_ref[q, 512:528, :].astype(F32)
         for k in range(3):
@@ -406,6 +410,13 @@
         scratch_shapes=list(scratch),
         compiler_params=pltpu.CompilerParams(vmem_limit_bytes=limit),
     )(*ins)
+
+
+def swapped(blocks, bit, mask):
+    keep = lax.dynamic_index_in_dim(blocks, bit, 2, keepdims=False)
+    send = lax.dynamic_index_in_dim(blocks, 1 - bit, 2, keepdims=False)
+    got = lax.ppermute(send, "head", [(source, source ^ mask) for source in range(HS)])
+    return jnp.where(bit == 0, jnp.stack([keep, got]), jnp.stack([got, keep]))
 
 
 def per_device(
@@ -431,12 +442,18 @@
     skip = jnp.repeat(skip_gain, HEAD)[None]
     packed = call(
         pack_kernel,
-        (request_prompt, head_inputs, state_proj, step_raw, gate_inputs),
+        (request_prompt, head_inputs, state_proj, step_raw),
         shape((XS * HS, SENT, 128), BF16),
         scalars=1,
         limit=None,
     )
+    head = lax.axis_index("head").astype(jnp.int32)
     rows = lax.all_to_all(packed, ("x", "head"), 0, 0)
+    gate = call(gate_kernel, (gate_inputs,), shape((HS, 16, XS * WIDTH), BF16))
+    gate = gate.reshape(2, 2, 2, 16, XS * WIDTH)
+    gate = swapped(gate, head & 1, 1)
+    gate = swapped(gate, (head >> 1) & 1, 2)
+    gate = swapped(gate, head >> 2, 4)
     halo = lax.ppermute(rows[-1, :STEPS].reshape(WIDE // 128, 16, 128)[:, 8:], "z", [(source, source + 1) for source in range(ZS - 1)])
     message, act, decay, step = call(
         front_kernel,
@@ -456,7 +473,7 @@
         got = lax.all_to_all(message, "z", 0, 0)
         own, inflow = call(
             within_kernel,
-            (places, prompt_lengths, act, decay, step, rows, skip),
+            (places, prompt_lengths, act, decay, step, skip),
             (shape((ROW, WIDTH), F32), shape((ROW, WIDTH), F32)),
             (pltpu.VMEM((2, 128, 128), F32),),
             scalars=2,
@@ -492,13 +509,14 @@
     shared = lax.all_to_all(shared, "x", 0, 0)
     hidden, final, edge_inner, edge_state = call(
         last_kernel,
-        (shared, norm_gain[None]),
+        (shared, gate.reshape(BLOCK, XS * WIDTH), norm_gain[None]),
         (
             shape((BLOCK, XS * WIDTH), BF16),
             shape((XS * WIDTH, STATE), F32),
             shape((1, 3, XS * WIDTH), BF16),
             shape((1, 3, 256), BF16),
         ),
+        (pltpu.VMEM((BLOCK, XS * WIDTH), F32),),
     )
     return hidden, final.reshape(1, heads, HEAD, STATE), edge_inner, edge_state
 

time: 109 us -> 111 us (1.018)
  blocking collectives: 38.7 us -> 0 us
  waiting for transfers between devices: 25 us -> 46.8 us
  starting transfers between devices: 27.5 us -> 45 us
    all_to_all x2 -> x0, blocking collectives: 38.7 us -> none  [the longest x1 27.4 us: per_device(): back = lax.all_to_all(answer, 'z', 0, 0)]
    all_to_all x0 -> x2, waiting for transfers between devices: none -> 15.8 us  [the longest x1 15.8 us: per_device(): back = lax.all_to_all(answer, 'z', 0, 0)]
    all_to_all x0 -> x2, starting transfers between devices: none -> 10.6 us  [the longest x1 5.54 us: per_device(): back = lax.all_to_all(answer, 'z', 0, 0)]
    ppermute x0 -> x3, waiting for transfers between devices: none -> 7.74 us  [swapped(): lax.ppermute(send, 'head', [(source, source ^ mask) for source in range(H...]
    ppermute x0 -> x3, starting transfers between devices: none -> 6.92 us  [swapped(): lax.ppermute(send, 'head', [(source, source ^ mask) for source in range(H...]
    all_to_all x1, waiting for transfers between devices: 11 us -> 8.57 us  [per_device(): rows = lax.all_to_all(packed, ('x', 'head'), 0, 0)]
    pallas_call x6 -> x7, Pallas kernels: 11.5 us -> 12.2 us  [call(): pl.pallas_call(kernel, out_shape=outs, in_specs=[smem] * scalars + [vmem]...]
  transfers between devices with their start and end apart: 3 -> 8, of which waited for: 2 -> 5; matrix products, arithmetic and copies ran while one was open for 1% -> 1% of each run, Pallas kernels for 3% -> 3%
where the time goes in v4:
time: 111 us; the launch traced here: 110 us
  waiting for transfers between devices  46.8 us (42%)
  starting transfers between devices  45 us (41%)
  Pallas kernels  12.2 us (11%)
  local copies, waits for them, and re-layouts  2.84 us (3%)
  between operations  2.15 us (2%)
  other arithmetic  1.17 us (1%)
    all_to_all x1, starting transfers between devices, onward(): got = lax.all_to_all(message, 'z', 0, 0)  16 us
    all_to_all x1, waiting for transfers between devices, per_device(): back = lax.all_to_all(answer, 'z', 0, 0)  15.8 us
    all_to_all x1, waiting for transfers between devices, onward(): got = lax.all_to_all(message, 'z', 0, 0)  14.7 us
    pallas_call x7, Pallas kernels, call(): pl.pallas_call(kernel, out_shape=outs, in_specs=[smem] * scalars + [vmem]...  12.2 us
    all_to_all x1, starting transfers between devices, per_device(): rows = lax.all_to_all(packed, ('x', 'head'), 0, 0)  9.47 us
    all_to_all x1, waiting for transfers between devices, per_device(): rows = lax.all_to_all(packed, ('x', 'head'), 0, 0)  8.57 us
    ppermute x3, waiting for transfers between devices, swapped(): lax.ppermute(send, 'head', [(source, source ^ mask) for source in range(H...  7.74 us
    ppermute x3, starting transfers between devices, swapped(): lax.ppermute(send, 'head', [(source, source ^ mask) for source in range(H...  6.92 us
  transfers between devices with their start and end apart: 8, of which 5 were waited for; matrix products, arithmetic and copies ran while one was open for 1% of the time, Pallas kernels for 3%

profile of v4, /device:TPU:2, one launch (start us, length us, event | category | flops | bytes accessed | tf_op | source)
XLA Modules:
  0.0 110.2 jit_solution(14956167391805880831)
XLA Ops:
  1.3 1.9 %shard_map.147 = bf16[32,72,128]{2,1,0:T(8,128)(2,1)} custom-call(s32[1,1]{1,0:T(1,128)S(6)} %copy.30.request_ref, bf16[16,8192]{1,0:T(8,128)(2,1)} %inner_ref.1, bf16[16,2048]{1,0:T(8,128)(2,1)} %proj_ref.1, bf16[16,128]{1,0:T(8,128)(2,1)} %step_ref.1), custom_call_target="tpu_custom_call" | custom-call | tf_op jit(solution)/shard_map/pallas_call | solution.py:405
  3.2 9.5 %all-to-all-start.2 = ((bf16[32,72,128]{2,1,0:T(8,128)(2,1)}), bf16[32,72,128]{2,1,0:T(8,128)(2,1)S(1)}, u32[]{:S(2)}, u32[]{:S(2)}) async-start(bf16[32,72,128]{2,1,0:T(8,128)(2,1)} %shard_map.147), calls=%async_computation.2 | async-start | bytes 1179648 | tf_op jit(solution)/shard_map/all_to_all | solution.py:451
  12.7 0.6 copy-done.4
  13.5 0.7 copy-done.5
  14.4 8.6 %all-to-all-done.2.rows_ref = bf16[32,72,128]{2,1,0:T(8,128)(2,1)S(1)} async-done(((bf16[32,72,128]{2,1,0:T(8,128)(2,1)}), bf16[32,72,128]{2,1,0:T(8,128)(2,1)S(1)}, u32[]{:S(2)}, u32[]{:S(2)}) %all-to-all-start.2) | async-done | bytes 589856 | tf_op jit(solution)/shard_map/all_to_all | solution.py:451
  23.0 2.0 %collective-permute-start = (bf16[4,8,128]{2,1,0:T(8,128)(2,1)S(1)}, bf16[4,8,128]{2,1,0:T(8,128)(2,1)S(1)}, u32[]{:S(2)}, u32[]{:S(2)}) collective-permute-start(bf16[4,8,128]{2,1,0:T(8,128)(2,1)S(1)} %slice.9), channel_id=1, source_target_pairs={{0,32},{32,64},{64,96},{96,128},{128,160},{160,192},{192,224},{224... | collective-permute-start | bytes 24584 | tf_op jit(solution)/shard_map/ppermute | solution.py:457
  25.1 0.6 reduce_max.9
  27.2 3.7 %shard_map.148 = (bf16[16,56,128]{2,1,0:T(8,128)(2,1)}, bf16[512,512]{1,0:T(8,128)(2,1)S(1)}, f32[512,128]{1,0:T(8,128)S(1)}, f32[512,128]{1,0:T(8,128)S(1)}) custom-call(s32[3]{0:T(128)S(1)} %pad_add_fusion.place_ref, s32[7]{0:T(128)S(1)} %copy-done.4, bf16[32,72,128]{2,1,0:T(8,128)(2,1)S(1)} %all-to-all-done.2.rows_ref, ...), custom_call_target="tpu_custom_call" | custom-call | tf_op jit(solution)/shard_map/pallas_call | solution.py:405
  30.9 35.1 %conditional.1 = (bf16[16,88,128]{2,1,0:T(8,128)(2,1)}, f32[512,256]{1,0:T(8,128)S(1)}, f32[512,256]{1,0:T(8,128)S(1)}) conditional(s32[]{:T(128)} %convert_element_type.9, (bf16[16,56,128]{2,1,0:T(8,128)(2,1)}, s32[3]{0:T(128)S(1)}, s32[7]{0:T(128)S(1)}, bf16[512,512]{1,0:T(8,128)(2,1)S(1)}, f32[512,128]{1,0:T(8,128)S(1)}, ...), branch_computations={%region_3.4_spmd, %region_4.5_spmd} | conditional | bytes 1671224 | solution.py:506
  30.9 16.0 %all-to-all-start = ((bf16[16,56,128]{2,1,0:T(8,128)(2,1)}), bf16[16,56,128]{2,1,0:T(8,128)(2,1)S(1)}, u32[]{:S(2)}, u32[]{:S(2)}) async-start(bf16[16,56,128]{2,1,0:T(8,128)(2,1)} %get-tuple-element.34), calls=%async_computation | async-start | bytes 458752 | tf_op jit(solution)/shard_map/cond/branch_0_fun/all_to_all | solution.py:473
  46.9 2.5 %branch_0_fun.3 = (f32[512,256]{1,0:T(8,128)S(1)}, f32[512,256]{1,0:T(8,128)S(1)}) custom-call(s32[3]{0:T(128)S(1)} %get-tuple-element.32.place_ref, s32[7]{0:T(128)S(1)} %get-tuple-element.33.length_ref, bf16[512,512]{1,0:T(8,128)(2,1)S(1)} %get-tuple-element.35.act_ref, f32[512,128]{1,0:T(8,128)S(1)} %get-tuple-element.36.decay_ref, ...), custom_call_target="tpu_custom_call" | custom-call | tf_op jit(solution)/shard_map/cond/branch_0_fun/pallas_call | solution.py:405
  49.4 14.7 %all-to-all-done.got_ref = bf16[16,56,128]{2,1,0:T(8,128)(2,1)S(1)} async-done(((bf16[16,56,128]{2,1,0:T(8,128)(2,1)}), bf16[16,56,128]{2,1,0:T(8,128)(2,1)S(1)}, u32[]{:S(2)}, u32[]{:S(2)}) %all-to-all-start) | async-done | bytes 229408 | tf_op jit(solution)/shard_map/cond/branch_0_fun/all_to_all | solution.py:473
  64.1 1.9 %branch_0_fun.2 = bf16[16,88,128]{2,1,0:T(8,128)(2,1)} custom-call(s32[3]{0:T(128)S(1)} %get-tuple-element.32.place_ref, s32[7]{0:T(128)S(1)} %get-tuple-element.33.length_ref, bf16[16,56,128]{2,1,0:T(8,128)(2,1)S(1)} %all-to-all-done.got_ref), custom_call_target="tpu_custom_call" | custom-call | tf_op jit(solution)/shard_map/cond/branch_0_fun/pallas_call | solution.py:405
  66.0 5.5 %all-to-all-start.3 = ((bf16[16,88,128]{2,1,0:T(8,128)(2,1)}), bf16[16,88,128]{2,1,0:T(8,128)(2,1)S(1)}, u32[]{:S(2)}, u32[]{:S(2)}) async-start(bf16[16,88,128]{2,1,0:T(8,128)(2,1)} %get-tuple-element.73), calls=%async_computation.3 | async-start | bytes 720896 | tf_op jit(solution)/shard_map/all_to_all | solution.py:507
  71.6 1.9 %collective-permute-start.1 = (bf16[2,2,16,1024]{3,2,1,0:T(8,128)(2,1)S(1)}, bf16[2,2,16,1024]{3,2,1,0:T(8,128)(2,1)S(1)}, u32[]{:S(2)}, u32[]{:S(2)}) collective-permute-start(bf16[2,2,16,1024]{3,2,1,0:T(8,128)(2,1)S(1)} %get-tuple-element.83), channel_id=1, source_target_pairs={{0,1},{1,0},{2,3},{3,2},{4,5},{5,4},{6,7},{7,6},{8,9},{9,8},{10,11... | collective-permute-start | bytes 393224 | tf_op jit(solution)/shard_map/ppermute | solution.py:418
  73.5 1.3 %collective-permute-done.1 = bf16[2,2,16,1024]{3,2,1,0:T(8,128)(2,1)S(1)} collective-permute-done((bf16[2,2,16,1024]{3,2,1,0:T(8,128)(2,1)S(1)}, bf16[2,2,16,1024]{3,2,1,0:T(8,128)(2,1)S(1)}, u32[]{:S(2)}, u32[]{:S(2)}) %collective-permute-start.1) | collective-permute-done | bytes 131104 | tf_op jit(solution)/shard_map/ppermute | solution.py:418
  74.9 3.1 %collective-permute-start.2 = (bf16[2,2,16,1024]{3,2,0,1:T(8,128)(2,1)S(1)}, bf16[2,2,16,1024]{3,2,0,1:T(8,128)(2,1)S(1)}, u32[]{:S(2)}, u32[]{:S(2)}) collective-permute-start(bf16[2,2,16,1024]{3,2,0,1:T(8,128)(2,1)S(1)} %bitcast.43), channel_id=1, source_target_pairs={{0,2},{1,3},{2,0},{3,1},{4,6},{5,7},{6,4},{7,5},{8,10},{9,11},{10,... | collective-permute-start | bytes 393224 | tf_op jit(solution)/shard_map/ppermute | solution.py:418
  78.0 15.8 %all-to-all-done.3.got_ref = bf16[16,88,128]{2,1,0:T(8,128)(2,1)S(1)} async-done(((bf16[16,88,128]{2,1,0:T(8,128)(2,1)}), bf16[16,88,128]{2,1,0:T(8,128)(2,1)S(1)}, u32[]{:S(2)}, u32[]{:S(2)}) %all-to-all-start.3) | async-done | bytes 360480 | tf_op jit(solution)/shard_map/all_to_all | solution.py:507
  93.8 1.1 %shard_map.149 = bf16[4,528,128]{2,1,0:T(8,128)(2,1)} custom-call(bf16[512,512]{1,0:T(8,128)(2,1)S(1)} %get-tuple-element.67.act_ref, f32[512,256]{1,0:T(8,128)S(1)} %get-tuple-element.71.own_ref, f32[512,256]{1,0:T(8,128)S(1)} %get-tuple-element.72.in_ref, bf16[16,88,128]{2,1,0:T(8,128)(2,1)S(1)} %all-to-all-done.3.got_ref), custom_call_target="tpu_custom_call" | custom-call | tf_op jit(solution)/shard_map/pallas_call | solution.py:405
  94.9 5.1 %all-to-all-start.4 = ((bf16[4,528,128]{2,1,0:T(8,128)(2,1)}), bf16[4,528,128]{2,1,0:T(8,128)(2,1)S(1)}, u32[]{:S(2)}, u32[]{:S(2)}) async-start(bf16[4,528,128]{2,1,0:T(8,128)(2,1)} %shard_map.149), calls=%async_computation.4 | async-start | bytes 1081344 | tf_op jit(solution)/shard_map/all_to_all | solution.py:509
  100.0 1.9 %collective-permute-start.3 = (bf16[2,2,16,1024]{3,2,1,0:T(8,128)(2,1)S(1)}, bf16[2,2,16,1024]{3,2,1,0:T(8,128)(2,1)S(1)}, u32[]{:S(2)}, u32[]{:S(2)}) collective-permute-start(bf16[2,2,16,1024]{3,2,1,0:T(8,128)(2,1)S(1)} %get-tuple-element.79), channel_id=1, source_target_pairs={{0,4},{1,5},{2,6},{3,7},{4,0},{5,1},{6,2},{7,3},{8,12},{9,13},{10,... | collective-permute-start | bytes 393224 | tf_op jit(solution)/shard_map/ppermute | solution.py:418
  102.0 6.4 %collective-permute-done.3 = bf16[2,2,16,1024]{3,2,1,0:T(8,128)(2,1)S(1)} collective-permute-done((bf16[2,2,16,1024]{3,2,1,0:T(8,128)(2,1)S(1)}, bf16[2,2,16,1024]{3,2,1,0:T(8,128)(2,1)S(1)}, u32[]{:S(2)}, u32[]{:S(2)}) %collective-permute-start.3) | collective-permute-done | bytes 131104 | tf_op jit(solution)/shard_map/ppermute | solution.py:418
  108.5 0.6 copy-done.3
  109.1 1.1 shard_map.151
  (34 shorter events, 1.5 us)
Async XLA Ops:
  3.2 19.8 %all-to-all-start.2 = ((bf16[32,72,128]{2,1,0:T(8,128)(2,1)}), bf16[32,72,128]{2,1,0:T(8,128)(2,1)S(1)}, u32[]{:S(2)}, u32[]{:S(2)}) async-start(bf16[32,72,128]{2,1,0:T(8,128)(2,1)} %shard_map.147), calls=%async_computation.2 | async-start | bytes 1179648 | tf_op jit(solution)/shard_map/all_to_all | solution.py:451
  12.7 0.7 copy-start.4
  13.5 0.7 copy-start.5
  13.5 0.7 copy-start.6
  23.0 3.4 %copy-start.7 = (f32[16]{0:T(128)S(1)}, f32[16]{0:T(128)}, u32[]{:S(2)}) copy-start(f32[16]{0:T(128)} %param.20) | copy-start | bytes 196
  23.0 3.6 %collective-permute-start = (bf16[4,8,128]{2,1,0:T(8,128)(2,1)S(1)}, bf16[4,8,128]{2,1,0:T(8,128)(2,1)S(1)}, u32[]{:S(2)}, u32[]{:S(2)}) collective-permute-start(bf16[4,8,128]{2,1,0:T(8,128)(2,1)S(1)} %slice.9), channel_id=1, source_target_pairs={{0,32},{32,64},{64,96},{96,128},{128,160},{160,192},{192,224},{224... | collective-permute-start | bytes 24584 | tf_op jit(solution)/shard_map/ppermute | solution.py:457
  25.0 1.5 %copy-start.1 = (f32[4,1024]{1,0:T(4,128)S(1)}, f32[4,1024]{1,0:T(4,128)}, u32[]{:S(2)}) copy-start(f32[4,1024]{1,0:T(4,128)} %inner_taps_ref.1) | copy-start | bytes 49156
  26.5 0.7 copy-start.2
  30.9 33.2 %all-to-all-start = ((bf16[16,56,128]{2,1,0:T(8,128)(2,1)}), bf16[16,56,128]{2,1,0:T(8,128)(2,1)S(1)}, u32[]{:S(2)}, u32[]{:S(2)}) async-start(bf16[16,56,128]{2,1,0:T(8,128)(2,1)} %get-tuple-element.34), calls=%async_computation | async-start | bytes 458752 | tf_op jit(solution)/shard_map/cond/branch_0_fun/all_to_all | solution.py:473
  66.0 5.6 %copy-start = (bf16[16,8192]{1,0:T(8,128)(2,1)S(1)}, bf16[16,8192]{1,0:T(8,128)(2,1)}, u32[]{:S(2)}) copy-start(bf16[16,8192]{1,0:T(8,128)(2,1)} %gate_ref.1) | copy-start | bytes 786436
  66.0 27.8 %all-to-all-start.3 = ((bf16[16,88,128]{2,1,0:T(8,128)(2,1)}), bf16[16,88,128]{2,1,0:T(8,128)(2,1)S(1)}, u32[]{:S(2)}, u32[]{:S(2)}) async-start(bf16[16,88,128]{2,1,0:T(8,128)(2,1)} %get-tuple-element.73), calls=%async_computation.3 | async-start | bytes 720896 | tf_op jit(solution)/shard_map/all_to_all | solution.py:507
  71.6 3.2 %collective-permute-start.1 = (bf16[2,2,16,1024]{3,2,1,0:T(8,128)(2,1)S(1)}, bf16[2,2,16,1024]{3,2,1,0:T(8,128)(2,1)S(1)}, u32[]{:S(2)}, u32[]{:S(2)}) collective-permute-start(bf16[2,2,16,1024]{3,2,1,0:T(8,128)(2,1)S(1)} %get-tuple-element.83), channel_id=1, source_target_pairs={{0,1},{1,0},{2,3},{3,2},{4,5},{5,4},{6,7},{7,6},{8,9},{9,8},{10,11... | collective-permute-start | bytes 393224 | tf_op jit(solution)/shard_map/ppermute | solution.py:418
  74.9 25.1 %collective-permute-start.2 = (bf16[2,2,16,1024]{3,2,0,1:T(8,128)(2,1)S(1)}, bf16[2,2,16,1024]{3,2,0,1:T(8,128)(2,1)S(1)}, u32[]{:S(2)}, u32[]{:S(2)}) collective-permute-start(bf16[2,2,16,1024]{3,2,0,1:T(8,128)(2,1)S(1)} %bitcast.43), channel_id=1, source_target_pairs={{0,2},{1,3},{2,0},{3,1},{4,6},{5,7},{6,4},{7,5},{8,10},{9,11},{10,... | collective-permute-start | bytes 393224 | tf_op jit(solution)/shard_map/ppermute | solution.py:418
  94.9 13.5 %all-to-all-start.4 = ((bf16[4,528,128]{2,1,0:T(8,128)(2,1)}), bf16[4,528,128]{2,1,0:T(8,128)(2,1)S(1)}, u32[]{:S(2)}, u32[]{:S(2)}) async-start(bf16[4,528,128]{2,1,0:T(8,128)(2,1)} %shard_map.149), calls=%async_computation.4 | async-start | bytes 1081344 | tf_op jit(solution)/shard_map/all_to_all | solution.py:509
  100.0 8.4 %collective-permute-start.3 = (bf16[2,2,16,1024]{3,2,1,0:T(8,128)(2,1)S(1)}, bf16[2,2,16,1024]{3,2,1,0:T(8,128)(2,1)S(1)}, u32[]{:S(2)}, u32[]{:S(2)}) collective-permute-start(bf16[2,2,16,1024]{3,2,1,0:T(8,128)(2,1)S(1)} %get-tuple-element.79), channel_id=1, source_target_pairs={{0,4},{1,5},{2,6},{3,7},{4,0},{5,1},{6,2},{7,3},{8,12},{9,13},{10,... | collective-permute-start | bytes 393224 | tf_op jit(solution)/shard_map/ppermute | solution.py:418
  108.4 0.7 copy-start.3

commit v5 on v4

--- a/solution.py
+++ b/solution.py
@@ -109,39 +109,54 @@
     return jnp.concatenate([early, late], axis=1).reshape(BLOCK, 128)
 
 
-def padded_rows(rows_ref, halo_ref, padded):
+def tokens(act, b):
+    return (act[0], slice(0, BLOCK)) if b == 0 else (act[1], slice((b - 1) * BLOCK, b * BLOCK))
+
+
+def convolve(out_ref, out_at, padded, at, b, first, starts, taps_ref):
+    position = iota((BLOCK, 128), 0) + (first + b * BLOCK)
+    row_start = jnp.zeros_like(position)
+    for start in starts:
+        row_start = jnp.where(position >= start, start, row_start)
+    inside = [(position - 3 + k) >= row_start for k in range(4)]
     for tile in range(WIDE // 128):
         cols = slice(tile * 128, (tile + 1) * 128)
-        padded[0:8, cols] = halo_ref[tile].astype(F32)
-        for b in range(BLOCKS):
-            at = 8 + b * BLOCK
-            padded[at : at + BLOCK, cols] = block_of(rows_ref, b, tile * 16).astype(F32)
-
-
-def weigh(weighted, act_ref, decay_ref, step_ref, end_decay, member_of):
+        total = jnp.zeros((BLOCK, 128), F32)
+        for k in range(4):
+            total = total + jnp.where(inside[k], padded[at - 3 + k : at - 3 + k + BLOCK, cols], 0.0) * taps_ref[k : k + 1, cols]
+        out_ref[out_at : out_at + BLOCK, cols] = (total * jax.nn.sigmoid(total)).astype(BF16)
+
+
+def outer(weighted, act, blocks, decay_ref, step_ref, end_decay, member_of):
     lane = iota((BLOCK, 128), 1)
-    for b in range(BLOCKS):
+    for at, b in enumerate(blocks):
         rows = slice(b * BLOCK, (b + 1) * BLOCK)
+        ref, held = tokens(act, b)
         gap = jnp.minimum(end_decay - decay_ref[rows, :], 0.0)
         weights = jnp.where(member_of(b), jnp.exp(gap), 0.0) * step_ref[rows, :]
         for tile in range(2):
             cols = slice(tile * 128, (tile + 1) * 128)
-            weighted[rows, cols] = (spread(weights, tile, lane) * act_ref[rows, cols].astype(F32)).astype(BF16)
-
-
-def send_state(message_ref, at, weighted, act_ref):
+            value = spread(weights, tile, lane) * ref[held, cols].astype(F32)
+            weighted[at * BLOCK : (at + 1) * BLOCK, cols] = value.astype(BF16)
+    out = []
     for tile in range(2):
-        state = dot(weighted[:, tile * 128 : (tile + 1) * 128], act_ref[:, WIDTH : WIDTH + STATE], ((0,), (0,)))
-        message_ref[tile * 8 : (tile + 1) * 8, at : at + 16, :] = state.astype(BF16).reshape(8, 16, 128)
-
-
-def send_ends(slots, first, length_ref, rows_ref, act_ref, decay_ref, step_ref, message_ref, padded, weighted):
-    starts, ends = bounds(length_ref)
-    before = segment_at(first - 1, starts)
-    last = segment_at(first + ROW - 1, starts)
-    sub = iota((BLOCK, 128), 0)
-    row = iota((1, 128), 1)
-    index = iota((8, 128), 0)
+        cols = slice(tile * 128, (tile + 1) * 128)
+        total, at = None, 0
+        for ref, count in ((act[0], int(0 in blocks)), (act[1], len([b for b in blocks if b]))):
+            if count:
+                part = dot(weighted[at * BLOCK : (at + count) * BLOCK, cols], ref[:, WIDTH : WIDTH + STATE], ((0,), (0,)))
+                total = part if total is None else total + part
+                at += count
+        out.append(total)
+    return out
+
+
+def send_state(message_ref, at, state):
+    for tile in range(2):
+        message_ref[tile * 8 : (tile + 1) * 8, at : at + 16, :] = state[tile].astype(BF16).reshape(8, 16, 128)
+
+
+def ends_in(slots, first, starts, ends):
     found = [[jnp.int32(BIG), jnp.int32(-2), jnp.int32(0)] for _ in range(slots)]
     count = jnp.int32(0)
     for p in range(PROMPTS):
@@ -151,24 +166,48 @@
             for at, value in enumerate((ends[p], jnp.int32(p), starts[p])):
                 found[m][at] = jnp.where(mine, value, found[m][at])
         count = count + here.astype(jnp.int32)
+    return found
+
+
+def between(first, start, end):
+    def member_of(b):
+        position = iota((BLOCK, 128), 0) + (first + b * BLOCK)
+        return (position >= start) & (position <= end)
+
+    return member_of
+
+
+def raw_row(rows_ref, halo_ref, local, tile):
+    inside = jnp.maximum(local, 0)
+    block = rows_ref[inside // 16, tile * 16 : tile * 16 + 16, :].astype(F32)
+    here = jnp.sum(jnp.where(iota((16, 128), 0) == inside % 16, block, 0.0), axis=0, keepdims=True)
+    before = jnp.sum(jnp.where(iota((8, 128), 0) == local + 8, halo_ref[tile].astype(F32), 0.0), axis=0, keepdims=True)
+    return jnp.where(local >= 0, here, before)
+
+
+def send_ends(
+    slots, first, length_ref, rows_ref, halo_ref, act, blocks, decay_ref, step_ref, part_ref, message_ref, weighted,
+):
+    starts, ends = bounds(length_ref)
+    before = segment_at(first - 1, starts)
+    last = segment_at(first + ROW - 1, starts)
+    row = iota((1, 128), 1)
+    index = iota((8, 128), 0)
     carry = decay_ref[ROW - 1 : ROW, :]
     small = laid_out(jnp.where(last == before, jnp.exp(carry), 0.0), 0, row)
     edges = []
-    for m in range(slots):
-        end, prompt, start = found[m]
+    for m, (end, prompt, start) in enumerate(ends_in(slots, first, starts, ends)):
         some = end < BIG
         local = jnp.where(some, end - first, 0)
         end_decay = decay_ref[pl.ds(local, 1), :]
         at = 16 * (m + 1)
 
         @pl.when(some)
-        def _(end=end, start=start, end_decay=end_decay, at=at):
-            def member_of(b):
-                position = sub + (first + b * BLOCK)
-                return (position >= start) & (position <= end)
-
-            weigh(weighted, act_ref, decay_ref, step_ref, end_decay, member_of)
-            send_state(message_ref, at, weighted, act_ref)
+        def _(end=end, start=start, end_decay=end_decay, at=at, m=m):
+            state = outer(weighted, act, blocks, decay_ref, step_ref, end_decay, between(first, start, end))
+            if part_ref is not None:
+                state = [state[tile] + part_ref[m + 1, tile] for tile in range(2)]
+            send_state(message_ref, at, state)
 
         @pl.when(jnp.logical_not(some))
         def _(at=at):
@@ -179,7 +218,7 @@
         edge = []
         for k in range(3):
             valid = some & (end - 2 + k >= start)
-            edge.append(jnp.where(valid, padded[pl.ds(8 + local - 2 + k, 1), :], 0.0))
+            edge.append([jnp.where(valid, raw_row(rows_ref, halo_ref, local - 2 + k, tile), 0.0) for tile in range(4)])
         edges.append(edge)
     for k in range(XS):
         request = rows_ref[k * 8, STEPS:SENT, :].astype(F32)[0:1, :]
@@ -190,67 +229,94 @@
         value = block
         if k < 12:
             for m in range(slots):
-                piece = edges[m][k // 4][:, (k % 4) * 128 : (k % 4 + 1) * 128]
-                value = jnp.where(index == m, piece, value)
+                value = jnp.where(index == m, edges[m][k // 4][k % 4], value)
         message_ref[k, tail : tail + 8, :] = value.astype(BF16)
 
 
-def front_kernel(
-    place_ref, length_ref, rows_ref, halo_ref, inner_taps_ref, state_taps_ref, head_ref,
-    message_ref, act_ref, decay_ref, step_ref, padded, weighted,
+def taps_kernel(place_ref, inner_ref, state_ref, out_ref):
+    for tile in range(2):
+        cols = slice(tile * 128, (tile + 1) * 128)
+        out_ref[:, cols] = inner_ref[:, pl.ds(pl.multiple_of(place_ref[1] * WIDTH + tile * 128, 128), 128)]
+    out_ref[:, WIDTH:] = state_ref[...]
+
+
+def early_kernel(
+    place_ref, length_ref, rows_ref, taps_ref, head_ref,
+    rest_ref, decay_ref, step_ref, part_ref, padded, weighted,
 ):
     first = place_ref[0] * ROW
-    quarter = place_ref[1]
-    starts, _ = bounds(length_ref)
+    starts, ends = bounds(length_ref)
     sub = iota((BLOCK, 128), 0)
     last = segment_at(first + ROW - 1, starts)
     heads = pltpu.roll(head_ref[...], place_ref[2], 1)
     bias = heads[0:1, :]
     scale = -jnp.exp(heads[1:2, :])
     lower = (sub >= iota((BLOCK, 128), 1)).astype(F32)
-
-    padded_rows(rows_ref, halo_ref, padded)
+    for tile in range(WIDE // 128):
+        cols = slice(tile * 128, (tile + 1) * 128)
+        padded[0:8, cols] = rows_ref[7, tile * 16 : tile * 16 + 16, :].astype(F32)[8:16]
+        for b in range(1, BLOCKS):
+            at = 8 + (b - 1) * BLOCK
+            padded[at : at + BLOCK, cols] = block_of(rows_ref, b, tile * 16).astype(F32)
     carry = jnp.zeros((1, 128), F32)
     for b in range(BLOCKS):
         rows = slice(b * BLOCK, (b + 1) * BLOCK)
-        position = sub + (first + b * BLOCK)
-        row_start = jnp.zeros_like(position)
-        for start in starts:
-            row_start = jnp.where(position >= start, start, row_start)
-        inside = [(position - 3 + k) >= row_start for k in range(4)]
-        for tile in range(WIDE // 128):
-            cols = slice(tile * 128, (tile + 1) * 128)
-            total = jnp.zeros((BLOCK, 128), F32)
-            for k in range(4):
-                if tile < 2:
-                    at = pl.multiple_of(quarter * WIDTH + tile * 128, 128)
-                    taps = inner_taps_ref[k : k + 1, pl.ds(at, 128)]
-                else:
-                    taps = state_taps_ref[k : k + 1, (tile - 2) * 128 : (tile - 1) * 128]
-                at = b * BLOCK + 5 + k
-                total = total + jnp.where(inside[k], padded[at : at + BLOCK, cols], 0.0) * taps
-            act_ref[rows, cols] = (total * jax.nn.sigmoid(total)).astype(BF16)
         step = jax.nn.softplus(steps_of(rows_ref, b) + bias)
         decay = dot(lower, step * scale, ((1,), (0,)), lax.Precision.HIGHEST) + carry
         carry = decay[BLOCK - 1 : BLOCK, :]
         step_ref[rows, :] = step
         decay_ref[rows, :] = decay
+        if b:
+            at = (b - 1) * BLOCK
+            convolve(rest_ref, at, padded, at + 8, b, first, starts, taps_ref)
 
     def member_of(b):
         return segment_at(sub + (first + b * BLOCK), starts) == last
 
-    weigh(weighted, act_ref, decay_ref, step_ref, carry, member_of)
-    send_state(message_ref, 0, weighted, act_ref)
-    send_ends(FEW, first, length_ref, rows_ref, act_ref, decay_ref, step_ref, message_ref, padded, weighted)
+    act, blocks = (None, rest_ref), (1, 2, 3)
+    state = outer(weighted, act, blocks, decay_ref, step_ref, carry, member_of)
+    part_ref[0, 0], part_ref[0, 1] = state
+    for m, (end, _, start) in enumerate(ends_in(FEW, first, starts, ends)):
+
+        @pl.when(end < BIG)
+        def _(end=end, start=start, m=m):
+            end_decay = decay_ref[pl.ds(end - first, 1), :]
+            state = outer(weighted, act, blocks, decay_ref, step_ref, end_decay, between(first, start, end))
+            part_ref[m + 1, 0], part_ref[m + 1, 1] = state
+
+
+def front_kernel(
+    place_ref, length_ref, rows_ref, halo_ref, taps_ref, decay_ref, step_ref, part_ref,
+    message_ref, act_ref, padded, weighted,
+):
+    first = place_ref[0] * ROW
+    starts, _ = bounds(length_ref)
+    sub = iota((BLOCK, 128), 0)
+    last = segment_at(first + ROW - 1, starts)
+    for tile in range(WIDE // 128):
+        cols = slice(tile * 128, (tile + 1) * 128)
+        padded[0:8, cols] = halo_ref[tile].astype(F32)
+        padded[8:, cols] = block_of(rows_ref, 0, tile * 16).astype(F32)
+    convolve(act_ref, 0, padded, 8, 0, first, starts, taps_ref)
+
+    def member_of(b):
+        return segment_at(sub + (first + b * BLOCK), starts) == last
+
+    act, blocks = (act_ref, None), (0,)
+    state = outer(weighted, act, blocks, decay_ref, step_ref, decay_ref[ROW - 1 : ROW, :], member_of)
+    send_state(message_ref, 0, [state[tile] + part_ref[0, tile] for tile in range(2)])
+    send_ends(
+        FEW, first, length_ref, rows_ref, halo_ref, act, blocks, decay_ref, step_ref, part_ref, message_ref, weighted
+    )
 
 
 def many_kernel(
-    place_ref, length_ref, rows_ref, halo_ref, act_ref, decay_ref, step_ref, few_ref, message_ref, padded, weighted,
+    place_ref, length_ref, rows_ref, halo_ref, act_ref, rest_ref, decay_ref, step_ref, few_ref, message_ref, weighted,
 ):
-    padded_rows(rows_ref, halo_ref, padded)
     message_ref[:, 0:16, :] = few_ref[:, 0:16, :]
     send_ends(
-        PROMPTS, place_ref[0] * ROW, length_ref, rows_ref, act_ref, decay_ref, step_ref, message_ref, padded, weighted
+        PROMPTS, place_ref[0] * ROW, length_ref, rows_ref, halo_ref, (act_ref, rest_ref), (0, 1, 2, 3),
+        decay_ref, step_ref, None, message_ref, weighted,
     )
 
 
@@ -296,7 +362,7 @@
 
 
 def within_kernel(
-    place_ref, length_ref, act_ref, decay_ref, step_ref, skip_ref, own_ref, in_ref, carried,
+    place_ref, length_ref, act_ref, rest_ref, decay_ref, step_ref, skip_ref, own_ref, in_ref, carried,
 ):
     first = place_ref[0] * ROW
     quarter = place_ref[1]
@@ -312,8 +378,9 @@
         last = segment_at(at + BLOCK - 1, starts)
         segment = segment_at(sub + at, starts)
         causal = (segment == segment_at(lane + at, starts)) & (sub >= lane)
-        write = act_ref[rows, WIDTH : WIDTH + STATE]
-        read = act_ref[rows, WIDTH + STATE : WIDE]
+        ref, held = tokens((act_ref, rest_ref), b)
+        write = ref[held, WIDTH : WIDTH + STATE]
+        read = ref[held, WIDTH + STATE : WIDE]
         scores = dot(read, write, ((1,), (1,)))
         decay = decay_ref[rows, :]
         step = step_ref[rows, :]
@@ -326,7 +393,7 @@
         keep = jnp.where(last == before, jnp.exp(end - carry), 0.0)
         for tile in range(2):
             cols = slice(tile * 128, (tile + 1) * 128)
-            x = act_ref[rows, cols]
+            x = ref[held, cols]
             mixing = []
             for head in (2 * tile, 2 * tile + 1):
                 gap = decay[:, head : head + 1] - decay_t[head : head + 1, :]
@@ -352,13 +419,14 @@
         carry = end
 
 
-def across_kernel(act_ref, own_ref, in_ref, got_ref, out_ref):
+def across_kernel(act_ref, rest_ref, own_ref, in_ref, got_ref, out_ref):
     for tile in range(2):
         cols = slice(tile * 128, (tile + 1) * 128)
         state = got_ref[tile * 8 : (tile + 1) * 8, 0:16, :].reshape(128, 128)
         for b in range(BLOCKS):
             rows = slice(b * BLOCK, (b + 1) * BLOCK)
-            across = dot(act_ref[rows, WIDTH + STATE : WIDE], state, ((1,), (1,)))
+            ref, held = tokens((act_ref, rest_ref), b)
+            across = dot(ref[held, WIDTH + STATE : WIDE], state, ((1,), (1,)))
             value = own_ref[rows, cols] + in_ref[rows, cols] * across
             out_ref[b, tile * BLOCK : (tile + 1) * BLOCK, :] = value.astype(BF16)
     index = iota((16, 128), 0)
@@ -438,8 +506,6 @@
     quarter = lax.axis_index("x").astype(jnp.int32)
     heads = step_bias.shape[0]
     places = jnp.stack([place, quarter, (128 - 4 * quarter) % 128])
-    heads_in = jnp.pad(jnp.stack([step_bias, decay_log]), ((0, 6), (0, 128 - heads)))
-    skip = jnp.repeat(skip_gain, HEAD)[None]
     packed = call(
         pack_kernel,
         (request_prompt, head_inputs, state_proj, step_raw),
@@ -451,29 +517,46 @@
     rows = lax.all_to_all(packed, ("x", "head"), 0, 0)
     gate = call(gate_kernel, (gate_inputs,), shape((HS, 16, XS * WIDTH), BF16))
     gate = gate.reshape(2, 2, 2, 16, XS * WIDTH)
+    taps = call(taps_kernel, (places, filter_inner, filter_state), shape((4, WIDE), F32), scalars=1)
+    heads_in = jnp.pad(jnp.stack([step_bias, decay_log]), ((0, 6), (0, 128 - heads)))
+    skip = jnp.repeat(skip_gain, HEAD)[None]
+    z = (jnp.cumsum(prompt_lengths) - 1) // ROW
+    most = jnp.max(jnp.sum((z[None, :] == z[:, None]).astype(jnp.int32), axis=1))
+    crowded = most > FEW
     gate = swapped(gate, head & 1, 1)
     gate = swapped(gate, (head >> 1) & 1, 2)
     gate = swapped(gate, head >> 2, 4)
-    halo = lax.ppermute(rows[-1, :STEPS].reshape(WIDE // 128, 16, 128)[:, 8:], "z", [(source, source + 1) for source in range(ZS - 1)])
-    message, act, decay, step = call(
-        front_kernel,
-        (places, prompt_lengths, rows, halo, filter_inner, filter_state, heads_in),
+    halo = lax.ppermute(
+        rows[-1, :STEPS].reshape(WIDE // 128, 16, 128)[:, 8:],
+        "z",
+        [(source, source + 1) for source in range(ZS - 1)],
+    )
+    weighted = pltpu.VMEM((ROW, WIDTH), BF16)
+    rest, decay, step, part = call(
+        early_kernel,
+        (places, prompt_lengths, rows, taps, heads_in),
         (
-            shape((ZS, 16 * (FEW + 1) + 8, 128), BF16),
-            shape((ROW, WIDE), BF16),
+            shape((ROW - BLOCK, WIDE), BF16),
             shape((ROW, 128), F32),
             shape((ROW, 128), F32),
+            shape((FEW + 1, 2, 128, 128), F32),
         ),
-        (pltpu.VMEM((ROW + 8, WIDE), F32), pltpu.VMEM((ROW, WIDTH), BF16)),
+        (pltpu.VMEM((ROW - BLOCK + 8, WIDE), F32), weighted),
         scalars=2,
     )
-    scratch = (pltpu.VMEM((ROW + 8, WIDE), F32), pltpu.VMEM((ROW, WIDTH), BF16))
+    message, act = call(
+        front_kernel,
+        (places, prompt_lengths, rows, halo, taps, decay, step, part),
+        (shape((ZS, 16 * (FEW + 1) + 8, 128), BF16), shape((BLOCK, WIDE), BF16)),
+        (pltpu.VMEM((BLOCK + 8, WIDE), F32), weighted),
+        scalars=2,
+    )
 
     def onward(slots, message):
         got = lax.all_to_all(message, "z", 0, 0)
         own, inflow = call(
             within_kernel,
-            (places, prompt_lengths, act, decay, step, skip),
+            (places, prompt_lengths, act, rest, decay, step, skip),
             (shape((ROW, WIDTH), F32), shape((ROW, WIDTH), F32)),
             (pltpu.VMEM((2, 128, 128), F32),),
             scalars=2,
@@ -494,18 +577,16 @@
     def many():
         full = call(
             many_kernel,
-            (places, prompt_lengths, rows, halo, act, decay, step, message),
+            (places, prompt_lengths, rows, halo, act, rest, decay, step, message),
             shape((ZS, 16 * (PROMPTS + 1) + 8, 128), BF16),
-            scratch,
+            (weighted,),
             scalars=2,
         )
         return onward(PROMPTS, full)
 
-    z = (jnp.cumsum(prompt_lengths) - 1) // ROW
-    most = jnp.max(jnp.sum((z[None, :] == z[:, None]).astype(jnp.int32), axis=1))
-    answer, own, inflow = lax.cond(most > FEW, many, lambda: onward(FEW, message))
+    answer, own, inflow = lax.cond(crowded, many, lambda: onward(FEW, message))
     back = lax.all_to_all(answer, "z", 0, 0)
-    shared = call(across_kernel, (act, own, inflow, back), shape((XS, 528, 128), BF16))
+    shared = call(across_kernel, (act, rest, own, inflow, back), shape((XS, 528, 128), BF16))
     shared = lax.all_to_all(shared, "x", 0, 0)
     hidden, final, edge_inner, edge_state = call(
         last_kernel,

time: 111 us -> 112 us (level)
  Pallas kernels: 12.2 us -> 13.6 us
  starting transfers between devices: 45 us -> 43.6 us
    all_to_all x1, starting transfers between devices: 16 us -> 14.3 us  [onward(): got = lax.all_to_all(message, 'z', 0, 0)]
    pallas_call x7 -> x9, Pallas kernels: 12.2 us -> 13.6 us  [call(): pl.pallas_call(kernel, out_shape=outs, in_specs=[smem] * scalars + [vmem]...]
  transfers between devices with their start and end apart: 8 -> 8, of which waited for: 5 -> 5; matrix products, arithmetic and copies ran while one was open for 1% -> 1% of each run, Pallas kernels for 3% -> 6%
where the time goes in v5:
time: 112 us; the launch traced here: 111 us
  waiting for transfers between devices  47.7 us (43%)
  starting transfers between devices  43.6 us (39%)
  Pallas kernels  13.6 us (12%)
  local copies, waits for them, and re-layouts  2.85 us (3%)
  between operations  2.17 us (2%)
  other arithmetic  1.17 us (1%)
    all_to_all x1, waiting for transfers between devices, per_device(): back = lax.all_to_all(answer, 'z', 0, 0)  16.6 us
    all_to_all x1, waiting for transfers between devices, onward(): got = lax.all_to_all(message, 'z', 0, 0)  14.8 us
    all_to_all x1, starting transfers between devices, onward(): got = lax.all_to_all(message, 'z', 0, 0)  14.3 us
    pallas_call x9, Pallas kernels, call(): pl.pallas_call(kernel, out_shape=outs, in_specs=[smem] * scalars + [vmem]...  13.6 us
    all_to_all x1, starting transfers between devices, per_device(): rows = lax.all_to_all(packed, ('x', 'head'), 0, 0)  9.47 us
    all_to_all x1, waiting for transfers between devices, per_device(): rows = lax.all_to_all(packed, ('x', 'head'), 0, 0)  8.57 us
    ppermute x3, waiting for transfers between devices, swapped(): lax.ppermute(send, 'head', [(source, source ^ mask) for source in range(H...  7.74 us
    ppermute x3, starting transfers between devices, swapped(): lax.ppermute(send, 'head', [(source, source ^ mask) for source in range(H...  6.55 us
  transfers between devices with their start and end apart: 8, of which 5 were waited for; matrix products, arithmetic and copies ran while one was open for 1% of the time, Pallas kernels for 6%

profile of v5, /device:TPU:2, one launch (start us, length us, event | category | flops | bytes accessed | tf_op | source)
XLA Modules:
  0.0 111.0 jit_solution(8633732046255798344)
XLA Ops:
  1.3 1.9 %shard_map.147 = bf16[32,72,128]{2,1,0:T(8,128)(2,1)} custom-call(s32[1,1]{1,0:T(1,128)S(6)} %copy.30.request_ref, bf16[16,8192]{1,0:T(8,128)(2,1)} %inner_ref.2, bf16[16,2048]{1,0:T(8,128)(2,1)} %proj_ref.1, bf16[16,128]{1,0:T(8,128)(2,1)} %step_ref.1), custom_call_target="tpu_custom_call" | custom-call | tf_op jit(solution)/shard_map/pallas_call | solution.py:473
  3.2 9.5 %all-to-all-start.2 = ((bf16[32,72,128]{2,1,0:T(8,128)(2,1)}), bf16[32,72,128]{2,1,0:T(8,128)(2,1)S(1)}, u32[]{:S(2)}, u32[]{:S(2)}) async-start(bf16[32,72,128]{2,1,0:T(8,128)(2,1)} %shard_map.147), calls=%async_computation.2 | async-start | bytes 1179648 | tf_op jit(solution)/shard_map/all_to_all | solution.py:517
  12.7 0.6 copy-done.4
  13.5 0.7 copy-done.5
  14.4 8.6 %all-to-all-done.2.rows_ref = bf16[32,72,128]{2,1,0:T(8,128)(2,1)S(1)} async-done(((bf16[32,72,128]{2,1,0:T(8,128)(2,1)}), bf16[32,72,128]{2,1,0:T(8,128)(2,1)S(1)}, u32[]{:S(2)}, u32[]{:S(2)}) %all-to-all-start.2) | async-done | bytes 589856 | tf_op jit(solution)/shard_map/all_to_all | solution.py:517
  23.0 2.0 %collective-permute-start = (bf16[4,8,128]{2,1,0:T(8,128)(2,1)S(1)}, bf16[4,8,128]{2,1,0:T(8,128)(2,1)S(1)}, u32[]{:S(2)}, u32[]{:S(2)}) collective-permute-start(bf16[4,8,128]{2,1,0:T(8,128)(2,1)S(1)} %slice.9), channel_id=1, source_target_pairs={{0,32},{32,64},{64,96},{96,128},{128,160},{160,192},{192,224},{224... | collective-permute-start | bytes 24584 | tf_op jit(solution)/shard_map/ppermute | solution.py:529
  27.7 2.4 %shard_map.149 = (bf16[384,512]{1,0:T(8,128)(2,1)S(1)}, f32[512,128]{1,0:T(8,128)S(1)}, f32[512,128]{1,0:T(8,128)S(1)}, f32[3,2,128,128]{3,2,1,0:T(8,128)S(1)}) custom-call(s32[3]{0:T(128)S(1)} %pad_add_fusion.place_ref, s32[7]{0:T(128)S(1)} %copy-done.4, bf16[32,72,128]{2,1,0:T(8,128)(2,1)S(1)} %all-to-all-done.2.rows_ref, ...), custom_call_target="tpu_custom_call" | custom-call | tf_op jit(solution)/shard_map/pallas_call | solution.py:473
  30.2 2.0 %shard_map.150 = (bf16[16,56,128]{2,1,0:T(8,128)(2,1)}, bf16[128,512]{1,0:T(8,128)(2,1)S(1)}) custom-call(s32[3]{0:T(128)S(1)} %pad_add_fusion.place_ref, s32[7]{0:T(128)S(1)} %copy-done.4, bf16[32,72,128]{2,1,0:T(8,128)(2,1)S(1)} %all-to-all-done.2.rows_ref, bf16[4,8,128]{2,1,0:T(8,128)(2,1)S(1)} %collective-permute-done.halo_ref, ...), custom_call_target="tpu_custom_call" | custom-call | tf_op jit(solution)/shard_map/pallas_call | solution.py:473
  32.2 33.5 %conditional.1 = (bf16[16,88,128]{2,1,0:T(8,128)(2,1)}, f32[512,256]{1,0:T(8,128)S(1)}, f32[512,256]{1,0:T(8,128)S(1)}) conditional(s32[]{:T(128)} %convert_element_type.9, (bf16[16,56,128]{2,1,0:T(8,128)(2,1)}, s32[3]{0:T(128)S(1)}, s32[7]{0:T(128)S(1)}, bf16[128,512]{1,0:T(8,128)(2,1)S(1)}, bf16[384,512]{1,0:T(8,128)(2,1)S(1)}, ...), branch_computations={%region_3.4_spmd, %region_4.5_spmd} | conditional | bytes 1671224 | solution.py:587
  32.2 14.3 %all-to-all-start = ((bf16[16,56,128]{2,1,0:T(8,128)(2,1)}), bf16[16,56,128]{2,1,0:T(8,128)(2,1)S(1)}, u32[]{:S(2)}, u32[]{:S(2)}) async-start(bf16[16,56,128]{2,1,0:T(8,128)(2,1)} %get-tuple-element.38), calls=%async_computation | async-start | bytes 458752 | tf_op jit(solution)/shard_map/cond/branch_0_fun/all_to_all | solution.py:556
  46.5 2.5 %branch_0_fun.3 = (f32[512,256]{1,0:T(8,128)S(1)}, f32[512,256]{1,0:T(8,128)S(1)}) custom-call(s32[3]{0:T(128)S(1)} %get-tuple-element.36.place_ref, s32[7]{0:T(128)S(1)} %get-tuple-element.37.length_ref, bf16[128,512]{1,0:T(8,128)(2,1)S(1)} %get-tuple-element.39.act_ref, bf16[384,512]{1,0:T(8,128)(2,1)S(1)} %get-tuple-element.40.rest_ref, ...), custom_call_target="tpu_custom_call" | custom-call | tf_op jit(solution)/shard_map/cond/branch_0_fun/pallas_call | solution.py:473
  49.1 14.8 %all-to-all-done.got_ref = bf16[16,56,128]{2,1,0:T(8,128)(2,1)S(1)} async-done(((bf16[16,56,128]{2,1,0:T(8,128)(2,1)}), bf16[16,56,128]{2,1,0:T(8,128)(2,1)S(1)}, u32[]{:S(2)}, u32[]{:S(2)}) %all-to-all-start) | async-done | bytes 229408 | tf_op jit(solution)/shard_map/cond/branch_0_fun/all_to_all | solution.py:556
  63.9 1.9 %branch_0_fun.2 = bf16[16,88,128]{2,1,0:T(8,128)(2,1)} custom-call(s32[3]{0:T(128)S(1)} %get-tuple-element.36.place_ref, s32[7]{0:T(128)S(1)} %get-tuple-element.37.length_ref, bf16[16,56,128]{2,1,0:T(8,128)(2,1)S(1)} %all-to-all-done.got_ref), custom_call_target="tpu_custom_call" | custom-call | tf_op jit(solution)/shard_map/cond/branch_0_fun/pallas_call | solution.py:473
  65.7 6.3 %all-to-all-start.3 = ((bf16[16,88,128]{2,1,0:T(8,128)(2,1)}), bf16[16,88,128]{2,1,0:T(8,128)(2,1)S(1)}, u32[]{:S(2)}, u32[]{:S(2)}) async-start(bf16[16,88,128]{2,1,0:T(8,128)(2,1)} %get-tuple-element.83), calls=%async_computation.3 | async-start | bytes 720896 | tf_op jit(solution)/shard_map/all_to_all | solution.py:588
  72.1 1.9 %collective-permute-start.1 = (bf16[2,2,16,1024]{3,2,1,0:T(8,128)(2,1)S(1)}, bf16[2,2,16,1024]{3,2,1,0:T(8,128)(2,1)S(1)}, u32[]{:S(2)}, u32[]{:S(2)}) collective-permute-start(bf16[2,2,16,1024]{3,2,1,0:T(8,128)(2,1)S(1)} %get-tuple-element.93), channel_id=1, source_target_pairs={{0,1},{1,0},{2,3},{3,2},{4,5},{5,4},{6,7},{7,6},{8,9},{9,8},{10,11... | collective-permute-start | bytes 393224 | tf_op jit(solution)/shard_map/ppermute | solution.py:486
  74.1 1.3 %collective-permute-done.1 = bf16[2,2,16,1024]{3,2,1,0:T(8,128)(2,1)S(1)} collective-permute-done((bf16[2,2,16,1024]{3,2,1,0:T(8,128)(2,1)S(1)}, bf16[2,2,16,1024]{3,2,1,0:T(8,128)(2,1)S(1)}, u32[]{:S(2)}, u32[]{:S(2)}) %collective-permute-start.1) | collective-permute-done | bytes 131104 | tf_op jit(solution)/shard_map/ppermute | solution.py:486
  75.4 2.7 %collective-permute-start.2 = (bf16[2,2,16,1024]{3,2,0,1:T(8,128)(2,1)S(1)}, bf16[2,2,16,1024]{3,2,0,1:T(8,128)(2,1)S(1)}, u32[]{:S(2)}, u32[]{:S(2)}) collective-permute-start(bf16[2,2,16,1024]{3,2,0,1:T(8,128)(2,1)S(1)} %bitcast.43), channel_id=1, source_target_pairs={{0,2},{1,3},{2,0},{3,1},{4,6},{5,7},{6,4},{7,5},{8,10},{9,11},{10,... | collective-permute-start | bytes 393224 | tf_op jit(solution)/shard_map/ppermute | solution.py:486
  78.2 16.6 %all-to-all-done.3.got_ref = bf16[16,88,128]{2,1,0:T(8,128)(2,1)S(1)} async-done(((bf16[16,88,128]{2,1,0:T(8,128)(2,1)}), bf16[16,88,128]{2,1,0:T(8,128)(2,1)S(1)}, u32[]{:S(2)}, u32[]{:S(2)}) %all-to-all-start.3) | async-done | bytes 360480 | tf_op jit(solution)/shard_map/all_to_all | solution.py:588
  94.8 1.1 shard_map.151
  95.9 5.0 %all-to-all-start.4 = ((bf16[4,528,128]{2,1,0:T(8,128)(2,1)}), bf16[4,528,128]{2,1,0:T(8,128)(2,1)S(1)}, u32[]{:S(2)}, u32[]{:S(2)}) async-start(bf16[4,528,128]{2,1,0:T(8,128)(2,1)} %shard_map.151), calls=%async_computation.4 | async-start | bytes 1081344 | tf_op jit(solution)/shard_map/all_to_all | solution.py:590
  100.9 1.9 %collective-permute-start.3 = (bf16[2,2,16,1024]{3,2,1,0:T(8,128)(2,1)S(1)}, bf16[2,2,16,1024]{3,2,1,0:T(8,128)(2,1)S(1)}, u32[]{:S(2)}, u32[]{:S(2)}) collective-permute-start(bf16[2,2,16,1024]{3,2,1,0:T(8,128)(2,1)S(1)} %get-tuple-element.89), channel_id=1, source_target_pairs={{0,4},{1,5},{2,6},{3,7},{4,0},{5,1},{6,2},{7,3},{8,12},{9,13},{10,... | collective-permute-start | bytes 393224 | tf_op jit(solution)/shard_map/ppermute | solution.py:486
  102.8 6.4 %collective-permute-done.3 = bf16[2,2,16,1024]{3,2,1,0:T(8,128)(2,1)S(1)} collective-permute-done((bf16[2,2,16,1024]{3,2,1,0:T(8,128)(2,1)S(1)}, bf16[2,2,16,1024]{3,2,1,0:T(8,128)(2,1)S(1)}, u32[]{:S(2)}, u32[]{:S(2)}) %collective-permute-start.3) | collective-permute-done | bytes 131104 | tf_op jit(solution)/shard_map/ppermute | solution.py:486
  109.3 0.6 copy-done.2
  110.0 1.1 shard_map.153
  (36 shorter events, 2.6 us)
Async XLA Ops:
  3.2 19.8 %all-to-all-start.2 = ((bf16[32,72,128]{2,1,0:T(8,128)(2,1)}), bf16[32,72,128]{2,1,0:T(8,128)(2,1)S(1)}, u32[]{:S(2)}, u32[]{:S(2)}) async-start(bf16[32,72,128]{2,1,0:T(8,128)(2,1)} %shard_map.147), calls=%async_computation.2 | async-start | bytes 1179648 | tf_op jit(solution)/shard_map/all_to_all | solution.py:517
  12.7 0.7 copy-start.4
  13.5 0.7 copy-start.5
  13.5 0.7 copy-start.6
  23.0 3.4 %copy-start.7 = (f32[16]{0:T(128)S(1)}, f32[16]{0:T(128)}, u32[]{:S(2)}) copy-start(f32[16]{0:T(128)} %param.20) | copy-start | bytes 196
  23.0 7.1 %collective-permute-start = (bf16[4,8,128]{2,1,0:T(8,128)(2,1)S(1)}, bf16[4,8,128]{2,1,0:T(8,128)(2,1)S(1)}, u32[]{:S(2)}, u32[]{:S(2)}) collective-permute-start(bf16[4,8,128]{2,1,0:T(8,128)(2,1)S(1)} %slice.9), channel_id=1, source_target_pairs={{0,32},{32,64},{64,96},{96,128},{128,160},{160,192},{192,224},{224... | collective-permute-start | bytes 24584 | tf_op jit(solution)/shard_map/ppermute | solution.py:529
  25.0 1.5 %copy-start.1 = (f32[4,1024]{1,0:T(4,128)S(1)}, f32[4,1024]{1,0:T(4,128)}, u32[]{:S(2)}) copy-start(f32[4,1024]{1,0:T(4,128)} %inner_ref.3) | copy-start | bytes 49156
  26.5 0.7 copy-start.3
  32.2 31.7 %all-to-all-start = ((bf16[16,56,128]{2,1,0:T(8,128)(2,1)}), bf16[16,56,128]{2,1,0:T(8,128)(2,1)S(1)}, u32[]{:S(2)}, u32[]{:S(2)}) async-start(bf16[16,56,128]{2,1,0:T(8,128)(2,1)} %get-tuple-element.38), calls=%async_computation | async-start | bytes 458752 | tf_op jit(solution)/shard_map/cond/branch_0_fun/all_to_all | solution.py:556
  65.7 6.3 %copy-start = (bf16[16,8192]{1,0:T(8,128)(2,1)S(1)}, bf16[16,8192]{1,0:T(8,128)(2,1)}, u32[]{:S(2)}) copy-start(bf16[16,8192]{1,0:T(8,128)(2,1)} %gate_ref.1) | copy-start | bytes 786436
  65.7 29.0 %all-to-all-start.3 = ((bf16[16,88,128]{2,1,0:T(8,128)(2,1)}), bf16[16,88,128]{2,1,0:T(8,128)(2,1)S(1)}, u32[]{:S(2)}, u32[]{:S(2)}) async-start(bf16[16,88,128]{2,1,0:T(8,128)(2,1)} %get-tuple-element.83), calls=%async_computation.3 | async-start | bytes 720896 | tf_op jit(solution)/shard_map/all_to_all | solution.py:588
  72.1 3.2 %collective-permute-start.1 = (bf16[2,2,16,1024]{3,2,1,0:T(8,128)(2,1)S(1)}, bf16[2,2,16,1024]{3,2,1,0:T(8,128)(2,1)S(1)}, u32[]{:S(2)}, u32[]{:S(2)}) collective-permute-start(bf16[2,2,16,1024]{3,2,1,0:T(8,128)(2,1)S(1)} %get-tuple-element.93), channel_id=1, source_target_pairs={{0,1},{1,0},{2,3},{3,2},{4,5},{5,4},{6,7},{7,6},{8,9},{9,8},{10,11... | collective-permute-start | bytes 393224 | tf_op jit(solution)/shard_map/ppermute | solution.py:486
  75.4 25.4 %collective-permute-start.2 = (bf16[2,2,16,1024]{3,2,0,1:T(8,128)(2,1)S(1)}, bf16[2,2,16,1024]{3,2,0,1:T(8,128)(2,1)S(1)}, u32[]{:S(2)}, u32[]{:S(2)}) collective-permute-start(bf16[2,2,16,1024]{3,2,0,1:T(8,128)(2,1)S(1)} %bitcast.43), channel_id=1, source_target_pairs={{0,2},{1,3},{2,0},{3,1},{4,6},{5,7},{6,4},{7,5},{8,10},{9,11},{10,... | collective-permute-start | bytes 393224 | tf_op jit(solution)/shard_map/ppermute | solution.py:486
  95.9 13.4 %all-to-all-start.4 = ((bf16[4,528,128]{2,1,0:T(8,128)(2,1)}), bf16[4,528,128]{2,1,0:T(8,128)(2,1)S(1)}, u32[]{:S(2)}, u32[]{:S(2)}) async-start(bf16[4,528,128]{2,1,0:T(8,128)(2,1)} %shard_map.151), calls=%async_computation.4 | async-start | bytes 1081344 | tf_op jit(solution)/shard_map/all_to_all | solution.py:590
  100.9 8.4 %collective-permute-start.3 = (bf16[2,2,16,1024]{3,2,1,0:T(8,128)(2,1)S(1)}, bf16[2,2,16,1024]{3,2,1,0:T(8,128)(2,1)S(1)}, u32[]{:S(2)}, u32[]{:S(2)}) collective-permute-start(bf16[2,2,16,1024]{3,2,1,0:T(8,128)(2,1)S(1)} %get-tuple-element.89), channel_id=1, source_target_pairs={{0,4},{1,5},{2,6},{3,7},{4,0},{5,1},{6,2},{7,3},{8,12},{9,13},{10,... | collective-permute-start | bytes 393224 | tf_op jit(solution)/shard_map/ppermute | solution.py:486
  109.3 0.7 copy-start.2

commit v6 on v5

--- a/solution.py
+++ b/solution.py
@@ -320,7 +320,7 @@
     )
 
 
-def scan_kernel(slots, place_ref, length_ref, got_ref, out_ref, small, states, finals):
+def scan_kernel(slots, place_ref, length_ref, got_ref, sent_ref, small, states, finals, out_ref, sems):
     _, ends = bounds(length_ref)
     head = place_ref[0] // 4
     tail_at = 16 * (slots + 1)
@@ -348,6 +348,7 @@
             value = jnp.where(rank == m, jnp.concatenate([own, edge], axis=0), value)
         finals[p] = value
     index = iota((8, 128), 0)
+    copies = []
     for z in range(ZS):
         edges = jnp.zeros((8, 128), F32)
         for k in range(XS):
@@ -359,6 +360,10 @@
             out_ref[z, 16 * k + 16 : 16 * k + 32, :] = value[0:16].astype(BF16)
             edges = jnp.where(index == k, value[16:24], edges)
         out_ref[z, 80:88, :] = edges.astype(BF16)
+        copies.append(pltpu.make_async_copy(out_ref.at[z], sent_ref.at[z], sems.at[z]))
+        copies[-1].start()
+    for copy in copies:
+        copy.wait()
 
 
 def within_kernel(
@@ -467,14 +472,14 @@
                     proj_ref[0, k : k + 1, c * 128 : (c + 1) * 128] = edges[4 * k + 2 + c : 4 * k + 3 + c, :].astype(BF16)
 
 
-def call(kernel, ins, outs, scratch=(), scalars=0, limit=24 << 20):
+def call(kernel, ins, outs, scratch=(), scalars=0, limit=24 << 20, kept=False):
     smem = pl.BlockSpec(memory_space=pltpu.SMEM)
     vmem = pl.BlockSpec(memory_space=pltpu.VMEM)
     return pl.pallas_call(
         kernel,
         out_shape=outs,
         in_specs=[smem] * scalars + [vmem] * (len(ins) - scalars),
-        out_specs=jax.tree.map(lambda _: vmem, outs),
+        out_specs=jax.tree.map(lambda _: pl.BlockSpec(memory_space=pl.ANY) if kept else vmem, outs),
         scratch_shapes=list(scratch),
         compiler_params=pltpu.CompilerParams(vmem_limit_bytes=limit),
     )(*ins)
@@ -569,8 +574,11 @@
                 pltpu.VMEM((ZS * 8, 128 * (slots + 1 + XS)), F32),
                 pltpu.VMEM((ZS, 16, 128), F32),
                 pltpu.VMEM((PROMPTS, 24, 128), F32),
+                pltpu.VMEM((ZS, 88, 128), BF16),
+                pltpu.SemaphoreType.DMA((ZS,)),
             ),
             scalars=2,
+            kept=True,
         )
         return answer, own, inflow
 

time: 112 us -> 112 us (level)
  no operation moved by 1% of the time
where the time goes in v6:
time: 112 us; the launch traced here: 111 us
  waiting for transfers between devices  47.7 us (43%)
  starting transfers between devices  43.6 us (39%)
  Pallas kernels  13.7 us (12%)
  local copies, waits for them, and re-layouts  2.85 us (3%)
  between operations  2.18 us (2%)
  other arithmetic  1.17 us (1%)
    all_to_all x1, waiting for transfers between devices, per_device(): back = lax.all_to_all(answer, 'z', 0, 0)  16.6 us
    all_to_all x1, waiting for transfers between devices, onward(): got = lax.all_to_all(message, 'z', 0, 0)  14.8 us
    all_to_all x1, starting transfers between devices, onward(): got = lax.all_to_all(message, 'z', 0, 0)  14.3 us
    pallas_call x9, Pallas kernels, call(): pl.pallas_call(kernel, out_shape=outs, in_specs=[smem] * scalars + [vmem]...  13.7 us
    all_to_all x1, starting transfers between devices, per_device(): rows = lax.all_to_all(packed, ('x', 'head'), 0, 0)  9.47 us
    all_to_all x1, waiting for transfers between devices, per_device(): rows = lax.all_to_all(packed, ('x', 'head'), 0, 0)  8.57 us
    ppermute x3, waiting for transfers between devices, swapped(): lax.ppermute(send, 'head', [(source, source ^ mask) for source in range(H...  7.74 us
    ppermute x3, starting transfers between devices, swapped(): lax.ppermute(send, 'head', [(source, source ^ mask) for source in range(H...  6.55 us
  transfers between devices with their start and end apart: 8, of which 5 were waited for; matrix products, arithmetic and copies ran while one was open for 1% of the time, Pallas kernels for 6%

profile of v6, /device:TPU:2, one launch (start us, length us, event | category | flops | bytes accessed | tf_op | source)
XLA Modules:
  0.0 111.4 jit_solution(14716563098443746213)
XLA Ops:
  1.3 1.9 %shard_map.147 = bf16[32,72,128]{2,1,0:T(8,128)(2,1)} custom-call(s32[1,1]{1,0:T(1,128)S(6)} %copy.30.request_ref, bf16[16,8192]{1,0:T(8,128)(2,1)} %inner_ref.2, bf16[16,2048]{1,0:T(8,128)(2,1)} %proj_ref.1, bf16[16,128]{1,0:T(8,128)(2,1)} %step_ref.1), custom_call_target="tpu_custom_call" | custom-call | tf_op jit(solution)/shard_map/pallas_call | solution.py:478
  3.2 9.5 %all-to-all-start.2 = ((bf16[32,72,128]{2,1,0:T(8,128)(2,1)}), bf16[32,72,128]{2,1,0:T(8,128)(2,1)S(1)}, u32[]{:S(2)}, u32[]{:S(2)}) async-start(bf16[32,72,128]{2,1,0:T(8,128)(2,1)} %shard_map.147), calls=%async_computation.2 | async-start | bytes 1179648 | tf_op jit(solution)/shard_map/all_to_all | solution.py:522
  12.7 0.6 copy-done.4
  13.5 0.7 copy-done.5
  14.4 8.6 %all-to-all-done.2.rows_ref = bf16[32,72,128]{2,1,0:T(8,128)(2,1)S(1)} async-done(((bf16[32,72,128]{2,1,0:T(8,128)(2,1)}), bf16[32,72,128]{2,1,0:T(8,128)(2,1)S(1)}, u32[]{:S(2)}, u32[]{:S(2)}) %all-to-all-start.2) | async-done | bytes 589856 | tf_op jit(solution)/shard_map/all_to_all | solution.py:522
  23.0 2.0 %collective-permute-start = (bf16[4,8,128]{2,1,0:T(8,128)(2,1)S(1)}, bf16[4,8,128]{2,1,0:T(8,128)(2,1)S(1)}, u32[]{:S(2)}, u32[]{:S(2)}) collective-permute-start(bf16[4,8,128]{2,1,0:T(8,128)(2,1)S(1)} %slice.9), channel_id=1, source_target_pairs={{0,32},{32,64},{64,96},{96,128},{128,160},{160,192},{192,224},{224... | collective-permute-start | bytes 24584 | tf_op jit(solution)/shard_map/ppermute | solution.py:534
  27.7 2.4 %shard_map.149 = (bf16[384,512]{1,0:T(8,128)(2,1)S(1)}, f32[512,128]{1,0:T(8,128)S(1)}, f32[512,128]{1,0:T(8,128)S(1)}, f32[3,2,128,128]{3,2,1,0:T(8,128)S(1)}) custom-call(s32[3]{0:T(128)S(1)} %pad_add_fusion.place_ref, s32[7]{0:T(128)S(1)} %copy-done.4, bf16[32,72,128]{2,1,0:T(8,128)(2,1)S(1)} %all-to-all-done.2.rows_ref, ...), custom_call_target="tpu_custom_call" | custom-call | tf_op jit(solution)/shard_map/pallas_call | solution.py:478
  30.2 2.0 %shard_map.150 = (bf16[16,56,128]{2,1,0:T(8,128)(2,1)}, bf16[128,512]{1,0:T(8,128)(2,1)S(1)}) custom-call(s32[3]{0:T(128)S(1)} %pad_add_fusion.place_ref, s32[7]{0:T(128)S(1)} %copy-done.4, bf16[32,72,128]{2,1,0:T(8,128)(2,1)S(1)} %all-to-all-done.2.rows_ref, bf16[4,8,128]{2,1,0:T(8,128)(2,1)S(1)} %collective-permute-done.halo_ref, ...), custom_call_target="tpu_custom_call" | custom-call | tf_op jit(solution)/shard_map/pallas_call | solution.py:478
  32.2 33.9 %conditional.1 = (bf16[16,88,128]{2,1,0:T(8,128)(2,1)}, f32[512,256]{1,0:T(8,128)S(1)}, f32[512,256]{1,0:T(8,128)S(1)}) conditional(s32[]{:T(128)} %convert_element_type.9, (bf16[16,56,128]{2,1,0:T(8,128)(2,1)}, s32[3]{0:T(128)S(1)}, s32[7]{0:T(128)S(1)}, bf16[128,512]{1,0:T(8,128)(2,1)S(1)}, bf16[384,512]{1,0:T(8,128)(2,1)S(1)}, ...), branch_computations={%region_3.4_spmd, %region_4.5_spmd} | conditional | bytes 1671224 | solution.py:595
  32.2 14.3 %all-to-all-start = ((bf16[16,56,128]{2,1,0:T(8,128)(2,1)}), bf16[16,56,128]{2,1,0:T(8,128)(2,1)S(1)}, u32[]{:S(2)}, u32[]{:S(2)}) async-start(bf16[16,56,128]{2,1,0:T(8,128)(2,1)} %get-tuple-element.38), calls=%async_computation | async-start | bytes 458752 | tf_op jit(solution)/shard_map/cond/branch_0_fun/all_to_all | solution.py:561
  46.5 2.5 %branch_0_fun.3 = (f32[512,256]{1,0:T(8,128)S(1)}, f32[512,256]{1,0:T(8,128)S(1)}) custom-call(s32[3]{0:T(128)S(1)} %get-tuple-element.36.place_ref, s32[7]{0:T(128)S(1)} %get-tuple-element.37.length_ref, bf16[128,512]{1,0:T(8,128)(2,1)S(1)} %get-tuple-element.39.act_ref, bf16[384,512]{1,0:T(8,128)(2,1)S(1)} %get-tuple-element.40.rest_ref, ...), custom_call_target="tpu_custom_call" | custom-call | tf_op jit(solution)/shard_map/cond/branch_0_fun/pallas_call | solution.py:478
  49.1 14.8 %all-to-all-done.got_ref = bf16[16,56,128]{2,1,0:T(8,128)(2,1)S(1)} async-done(((bf16[16,56,128]{2,1,0:T(8,128)(2,1)}), bf16[16,56,128]{2,1,0:T(8,128)(2,1)S(1)}, u32[]{:S(2)}, u32[]{:S(2)}) %all-to-all-start) | async-done | bytes 229408 | tf_op jit(solution)/shard_map/cond/branch_0_fun/all_to_all | solution.py:561
  63.9 2.0 %branch_0_fun.2 = bf16[16,88,128]{2,1,0:T(8,128)(2,1)} custom-call(s32[3]{0:T(128)S(1)} %get-tuple-element.36.place_ref, s32[7]{0:T(128)S(1)} %get-tuple-element.37.length_ref, bf16[16,56,128]{2,1,0:T(8,128)(2,1)S(1)} %all-to-all-done.got_ref), custom_call_target="tpu_custom_call" | custom-call | tf_op jit(solution)/shard_map/cond/branch_0_fun/pallas_call | solution.py:478
  66.1 6.3 %all-to-all-start.3 = ((bf16[16,88,128]{2,1,0:T(8,128)(2,1)}), bf16[16,88,128]{2,1,0:T(8,128)(2,1)S(1)}, u32[]{:S(2)}, u32[]{:S(2)}) async-start(bf16[16,88,128]{2,1,0:T(8,128)(2,1)} %get-tuple-element.83), calls=%async_computation.3 | async-start | bytes 720896 | tf_op jit(solution)/shard_map/all_to_all | solution.py:596
  72.5 1.9 %collective-permute-start.1 = (bf16[2,2,16,1024]{3,2,1,0:T(8,128)(2,1)S(1)}, bf16[2,2,16,1024]{3,2,1,0:T(8,128)(2,1)S(1)}, u32[]{:S(2)}, u32[]{:S(2)}) collective-permute-start(bf16[2,2,16,1024]{3,2,1,0:T(8,128)(2,1)S(1)} %get-tuple-element.93), channel_id=1, source_target_pairs={{0,1},{1,0},{2,3},{3,2},{4,5},{5,4},{6,7},{7,6},{8,9},{9,8},{10,11... | collective-permute-start | bytes 393224 | tf_op jit(solution)/shard_map/ppermute | solution.py:491
  74.4 1.3 %collective-permute-done.1 = bf16[2,2,16,1024]{3,2,1,0:T(8,128)(2,1)S(1)} collective-permute-done((bf16[2,2,16,1024]{3,2,1,0:T(8,128)(2,1)S(1)}, bf16[2,2,16,1024]{3,2,1,0:T(8,128)(2,1)S(1)}, u32[]{:S(2)}, u32[]{:S(2)}) %collective-permute-start.1) | collective-permute-done | bytes 131104 | tf_op jit(solution)/shard_map/ppermute | solution.py:491
  75.8 2.7 %collective-permute-start.2 = (bf16[2,2,16,1024]{3,2,0,1:T(8,128)(2,1)S(1)}, bf16[2,2,16,1024]{3,2,0,1:T(8,128)(2,1)S(1)}, u32[]{:S(2)}, u32[]{:S(2)}) collective-permute-start(bf16[2,2,16,1024]{3,2,0,1:T(8,128)(2,1)S(1)} %bitcast.43), channel_id=1, source_target_pairs={{0,2},{1,3},{2,0},{3,1},{4,6},{5,7},{6,4},{7,5},{8,10},{9,11},{10,... | collective-permute-start | bytes 393224 | tf_op jit(solution)/shard_map/ppermute | solution.py:491
  78.6 16.6 %all-to-all-done.3.got_ref = bf16[16,88,128]{2,1,0:T(8,128)(2,1)S(1)} async-done(((bf16[16,88,128]{2,1,0:T(8,128)(2,1)}), bf16[16,88,128]{2,1,0:T(8,128)(2,1)S(1)}, u32[]{:S(2)}, u32[]{:S(2)}) %all-to-all-start.3) | async-done | bytes 360480 | tf_op jit(solution)/shard_map/all_to_all | solution.py:596
  95.1 1.1 shard_map.151
  96.2 5.0 %all-to-all-start.4 = ((bf16[4,528,128]{2,1,0:T(8,128)(2,1)}), bf16[4,528,128]{2,1,0:T(8,128)(2,1)S(1)}, u32[]{:S(2)}, u32[]{:S(2)}) async-start(bf16[4,528,128]{2,1,0:T(8,128)(2,1)} %shard_map.151), calls=%async_computation.4 | async-start | bytes 1081344 | tf_op jit(solution)/shard_map/all_to_all | solution.py:598
  101.3 1.9 %collective-permute-start.3 = (bf16[2,2,16,1024]{3,2,1,0:T(8,128)(2,1)S(1)}, bf16[2,2,16,1024]{3,2,1,0:T(8,128)(2,1)S(1)}, u32[]{:S(2)}, u32[]{:S(2)}) collective-permute-start(bf16[2,2,16,1024]{3,2,1,0:T(8,128)(2,1)S(1)} %get-tuple-element.89), channel_id=1, source_target_pairs={{0,4},{1,5},{2,6},{3,7},{4,0},{5,1},{6,2},{7,3},{8,12},{9,13},{10,... | collective-permute-start | bytes 393224 | tf_op jit(solution)/shard_map/ppermute | solution.py:491
  103.2 6.4 %collective-permute-done.3 = bf16[2,2,16,1024]{3,2,1,0:T(8,128)(2,1)S(1)} collective-permute-done((bf16[2,2,16,1024]{3,2,1,0:T(8,128)(2,1)S(1)}, bf16[2,2,16,1024]{3,2,1,0:T(8,128)(2,1)S(1)}, u32[]{:S(2)}, u32[]{:S(2)}) %collective-permute-start.3) | collective-permute-done | bytes 131104 | tf_op jit(solution)/shard_map/ppermute | solution.py:491
  109.7 0.6 copy-done.2
  110.3 1.1 shard_map.153
  (36 shorter events, 2.7 us)
Async XLA Ops:
  3.2 19.8 %all-to-all-start.2 = ((bf16[32,72,128]{2,1,0:T(8,128)(2,1)}), bf16[32,72,128]{2,1,0:T(8,128)(2,1)S(1)}, u32[]{:S(2)}, u32[]{:S(2)}) async-start(bf16[32,72,128]{2,1,0:T(8,128)(2,1)} %shard_map.147), calls=%async_computation.2 | async-start | bytes 1179648 | tf_op jit(solution)/shard_map/all_to_all | solution.py:522
  12.7 0.7 copy-start.4
  13.5 0.7 copy-start.5
  13.5 0.7 copy-start.6
  23.0 3.4 %copy-start.7 = (f32[16]{0:T(128)S(1)}, f32[16]{0:T(128)}, u32[]{:S(2)}) copy-start(f32[16]{0:T(128)} %param.20) | copy-start | bytes 196
  23.0 7.1 %collective-permute-start = (bf16[4,8,128]{2,1,0:T(8,128)(2,1)S(1)}, bf16[4,8,128]{2,1,0:T(8,128)(2,1)S(1)}, u32[]{:S(2)}, u32[]{:S(2)}) collective-permute-start(bf16[4,8,128]{2,1,0:T(8,128)(2,1)S(1)} %slice.9), channel_id=1, source_target_pairs={{0,32},{32,64},{64,96},{96,128},{128,160},{160,192},{192,224},{224... | collective-permute-start | bytes 24584 | tf_op jit(solution)/shard_map/ppermute | solution.py:534
  25.0 1.5 %copy-start.1 = (f32[4,1024]{1,0:T(4,128)S(1)}, f32[4,1024]{1,0:T(4,128)}, u32[]{:S(2)}) copy-start(f32[4,1024]{1,0:T(4,128)} %inner_ref.3) | copy-start | bytes 49156
  26.5 0.7 copy-start.3
  32.2 31.7 %all-to-all-start = ((bf16[16,56,128]{2,1,0:T(8,128)(2,1)}), bf16[16,56,128]{2,1,0:T(8,128)(2,1)S(1)}, u32[]{:S(2)}, u32[]{:S(2)}) async-start(bf16[16,56,128]{2,1,0:T(8,128)(2,1)} %get-tuple-element.38), calls=%async_computation | async-start | bytes 458752 | tf_op jit(solution)/shard_map/cond/branch_0_fun/all_to_all | solution.py:561
  66.1 6.3 %copy-start = (bf16[16,8192]{1,0:T(8,128)(2,1)S(1)}, bf16[16,8192]{1,0:T(8,128)(2,1)}, u32[]{:S(2)}) copy-start(bf16[16,8192]{1,0:T(8,128)(2,1)} %gate_ref.1) | copy-start | bytes 786436
  66.1 29.1 %all-to-all-start.3 = ((bf16[16,88,128]{2,1,0:T(8,128)(2,1)}), bf16[16,88,128]{2,1,0:T(8,128)(2,1)S(1)}, u32[]{:S(2)}, u32[]{:S(2)}) async-start(bf16[16,88,128]{2,1,0:T(8,128)(2,1)} %get-tuple-element.83), calls=%async_computation.3 | async-start | bytes 720896 | tf_op jit(solution)/shard_map/all_to_all | solution.py:596
  72.5 3.2 %collective-permute-start.1 = (bf16[2,2,16,1024]{3,2,1,0:T(8,128)(2,1)S(1)}, bf16[2,2,16,1024]{3,2,1,0:T(8,128)(2,1)S(1)}, u32[]{:S(2)}, u32[]{:S(2)}) collective-permute-start(bf16[2,2,16,1024]{3,2,1,0:T(8,128)(2,1)S(1)} %get-tuple-element.93), channel_id=1, source_target_pairs={{0,1},{1,0},{2,3},{3,2},{4,5},{5,4},{6,7},{7,6},{8,9},{9,8},{10,11... | collective-permute-start | bytes 393224 | tf_op jit(solution)/shard_map/ppermute | solution.py:491
  75.8 25.4 %collective-permute-start.2 = (bf16[2,2,16,1024]{3,2,0,1:T(8,128)(2,1)S(1)}, bf16[2,2,16,1024]{3,2,0,1:T(8,128)(2,1)S(1)}, u32[]{:S(2)}, u32[]{:S(2)}) collective-permute-start(bf16[2,2,16,1024]{3,2,0,1:T(8,128)(2,1)S(1)} %bitcast.43), channel_id=1, source_target_pairs={{0,2},{1,3},{2,0},{3,1},{4,6},{5,7},{6,4},{7,5},{8,10},{9,11},{10,... | collective-permute-start | bytes 393224 | tf_op jit(solution)/shard_map/ppermute | solution.py:491
  96.2 13.4 %all-to-all-start.4 = ((bf16[4,528,128]{2,1,0:T(8,128)(2,1)}), bf16[4,528,128]{2,1,0:T(8,128)(2,1)S(1)}, u32[]{:S(2)}, u32[]{:S(2)}) async-start(bf16[4,528,128]{2,1,0:T(8,128)(2,1)} %shard_map.151), calls=%async_computation.4 | async-start | bytes 1081344 | tf_op jit(solution)/shard_map/all_to_all | solution.py:598
  101.3 8.4 %collective-permute-start.3 = (bf16[2,2,16,1024]{3,2,1,0:T(8,128)(2,1)S(1)}, bf16[2,2,16,1024]{3,2,1,0:T(8,128)(2,1)S(1)}, u32[]{:S(2)}, u32[]{:S(2)}) collective-permute-start(bf16[2,2,16,1024]{3,2,1,0:T(8,128)(2,1)S(1)} %get-tuple-element.89), channel_id=1, source_target_pairs={{0,4},{1,5},{2,6},{3,7},{4,0},{5,1},{6,2},{7,3},{8,12},{9,13},{10,... | collective-permute-start | bytes 393224 | tf_op jit(solution)/shard_map/ppermute | solution.py:491
  109.6 0.7 copy-start.2
